TPU v7x, 128 devices: a whole 4x4x4 slice. The times are simulated.
128 devices in a mesh: grp: 4 (over y_hi, core), row: 4 (over z), col: 8 (over x, y_lo).
Axes of the slice: x: 4, y: 4 (y_hi: 2, y_lo: 2; y = y_hi * 2 + y_lo), z: 4, core: 2. Of those that a mesh axis runs over, the one named last changes fastest.
Arguments:
- pair_rep: bfloat16 [4, 512, 512, 128], P('grp', 'row', 'col'), may hold values from -6 to 6
- cotangent: bfloat16 [4, 512, 512, 128], P('grp', 'row', 'col'), may hold values from -6 to 6
- lengths: int32 [4], replicated, may hold values from 128 to 512, as said below
- weight_in: bfloat16 [128, 640], replicated, may hold values from -0.5 to 0.5
- weight_out: bfloat16 [128, 128], replicated, may hold values from -0.5 to 0.5
- gain_in: float32 [128], replicated, may hold values from 0.1 to 1.9
- gain_out: float32 [128], replicated, may hold values from 0.1 to 1.9
Outputs:
- mixed: bfloat16 [4, 512, 512, 128], P('grp', 'row', 'col')
- grad_pair: bfloat16 [4, 512, 512, 128], P('grp', 'row', 'col')
- grad_weight_in: float32 [128, 640], replicated
- grad_weight_out: float32 [128, 128], replicated
- grad_gain_in: float32 [128], replicated
- grad_gain_out: float32 [128], replicated
Inputs may be any that keep to these rules, and one draw needn't show every extreme that they name: `lengths`: in every draw one complex has exactly 512 real residues and another exactly 128.
All inputs are finite; a program needn't handle non-finite values.
Results may differ from a plain program's by a relative error of at most 0.0089.
Values may be sent and summed in bfloat16 or wider, within the bound.
No kernel may reach another device: no remote copies, remote signals or barrier semaphores. Data moves between devices by JAX's collectives and lax.ppermute only.
A program may use at most 128 MiB of HBM per device.

v0:
```python
import jax
import jax.numpy as jnp
from jax import lax
from jax.sharding import PartitionSpec as P

N = 512
KBLOCK = 128


epsilon = 1e-05


def normalize(values, along):
    centred = values - jnp.mean(values, axis=along, keepdims=True)
    inverse = lax.rsqrt(jnp.mean(centred * centred, axis=along, keepdims=True) + epsilon)
    return (centred * inverse, inverse)


def normalize_back(grad_hat, normed, inverse, along):
    first_mean = jnp.mean(grad_hat, axis=along, keepdims=True)
    second_mean = jnp.mean(grad_hat * normed, axis=along, keepdims=True)
    return inverse * (grad_hat - first_mean - normed * second_mean)


def to_channels(tile_set):
    rows_n = lax.axis_size("row")
    cols_n = lax.axis_size("col")
    hidden_width, stack_size, col_len, row_len = tile_set.shape
    arrived = lax.all_to_all(
        tile_set[:, None], ("row", "col"), split_axis=0, concat_axis=1, tiled=True
    )
    share_size = hidden_width // (rows_n * cols_n)
    arrived = arrived.reshape(share_size, rows_n, cols_n, stack_size, col_len, row_len)
    arrived = arrived.transpose(0, 3, 2, 4, 1, 5)
    return arrived.reshape(share_size, stack_size, cols_n * col_len, rows_n * row_len)


def from_channels(pieces):
    rows_n = lax.axis_size("row")
    cols_n = lax.axis_size("col")
    share_size, stack_size, full_cols, full_rows = pieces.shape
    col_len = full_cols // cols_n
    row_len = full_rows // rows_n
    spread = pieces.reshape(share_size, stack_size, cols_n, col_len, rows_n, row_len)
    spread = spread.transpose(4, 2, 0, 1, 3, 5).reshape(
        rows_n * cols_n, share_size, stack_size, col_len, row_len
    )
    return lax.all_to_all(spread, ("row", "col"), split_axis=0, concat_axis=1, tiled=True)[0]


def triangle(pair_block, length):
    left_vals = pair_block[:, 0]
    right_vals = pair_block[:, 1]
    block_count = (length + KBLOCK - 1) // KBLOCK

    def advance(block_index, running):
        offset_rows = block_index * KBLOCK
        left_part = lax.dynamic_slice_in_dim(left_vals, offset_rows, KBLOCK, 1)
        right_part = lax.dynamic_slice_in_dim(right_vals, offset_rows, KBLOCK, 1)
        return running + jnp.einsum(
            "hkj,hki->hji", right_part, left_part, preferred_element_type=jnp.float32
        )

    empty = jnp.zeros((left_vals.shape[0], right_vals.shape[2], left_vals.shape[2]), jnp.float32)
    return lax.fori_loop(0, block_count, advance, empty)


def triangle_back(pair_block, grad_block, length):
    left_vals = pair_block[:, 0]
    right_vals = pair_block[:, 1]
    grad_vals = grad_block[:, 0]
    block_count = (length + KBLOCK - 1) // KBLOCK

    def advance(block_index, running):
        offset_rows = block_index * KBLOCK
        left_part = lax.dynamic_slice_in_dim(left_vals, offset_rows, KBLOCK, 1)
        right_part = lax.dynamic_slice_in_dim(right_vals, offset_rows, KBLOCK, 1)
        left_grad = jnp.einsum(
            "hkj,hji->hki", right_part, grad_vals, preferred_element_type=jnp.float32
        )
        right_grad = jnp.einsum(
            "hki,hji->hkj", left_part, grad_vals, preferred_element_type=jnp.float32
        )
        both_grads = jnp.stack([left_grad, right_grad], 1).astype(jnp.bfloat16)
        return lax.dynamic_update_slice_in_dim(running, both_grads, offset_rows, 2)

    empty = jnp.zeros(pair_block.shape, jnp.bfloat16)
    return lax.fori_loop(0, block_count, advance, empty)


def on_device(pair_rep, cotangent, lengths, weight_in, weight_out, gain_in, gain_out):
    groups = lax.axis_size("grp")
    row_len = pair_rep.shape[1]
    col_len = pair_rep.shape[2]
    hidden_width = weight_out.shape[0]
    lookup = jnp.arange(groups) == lax.axis_index("grp")
    own_length = jnp.sum(jnp.where(lookup, lengths, 0))
    row_pos = lax.axis_index("row") * row_len + jnp.arange(row_len)
    col_pos = lax.axis_index("col") * col_len + jnp.arange(col_len)
    inside = ((row_pos[:, None] < own_length) & (col_pos[None, :] < own_length)).astype(jnp.float32)
    flipped = inside.T
    inside_c = inside[:, :, None]
    z_hat, z_inverse = normalize(pair_rep[0].astype(jnp.float32), -1)
    z_norm = (z_hat * gain_in).astype(jnp.bfloat16)
    w_tri = weight_in[:, : 4 * hidden_width]
    w_gate = weight_in[:, 4 * hidden_width :]
    projected = jnp.einsum("ijc,cq->qji", z_norm, w_tri, preferred_element_type=jnp.float32)
    gate_pre = jnp.einsum("ijc,cd->ijd", z_norm, w_gate, preferred_element_type=jnp.float32)
    left_lin = projected[0:hidden_width]
    left_pre = projected[hidden_width : 2 * hidden_width]
    right_lin = projected[2 * hidden_width : 3 * hidden_width]
    right_pre = projected[3 * hidden_width :]
    left_sig = jax.nn.sigmoid(left_pre)
    right_sig = jax.nn.sigmoid(right_pre)
    pair_tiles = jnp.stack(
        [left_sig * left_lin * flipped, right_sig * right_lin * flipped], 1
    ).astype(jnp.bfloat16)
    pair_ch = to_channels(pair_tiles)
    outer_ch = triangle(pair_ch, own_length).astype(jnp.bfloat16)[:, None]
    outer_tile = from_channels(outer_ch)[:, 0].astype(jnp.float32)
    o_hat, o_inverse = normalize(outer_tile, 0)
    o_norm = (o_hat * gain_out[:, None, None]).astype(jnp.bfloat16)
    proj_out = jnp.einsum("hji,hc->ijc", o_norm, weight_out, preferred_element_type=jnp.float32)
    gate = jax.nn.sigmoid(gate_pre)
    mixed = (gate * proj_out * inside_c).astype(jnp.bfloat16)
    grad_out = cotangent[0].astype(jnp.float32)
    grad_proj = (grad_out * gate * inside_c).astype(jnp.bfloat16)
    grad_gate = (grad_out * proj_out * inside_c * gate * (1.0 - gate)).astype(jnp.bfloat16)
    grad_w_out = jnp.einsum("hji,ijc->hc", o_norm, grad_proj, preferred_element_type=jnp.float32)
    grad_o_norm = jnp.einsum(
        "ijc,hc->hji", grad_proj, weight_out, preferred_element_type=jnp.float32
    )
    grad_g_out = jnp.sum(grad_o_norm * o_hat, axis=(1, 2))
    grad_outer = normalize_back(grad_o_norm * gain_out[:, None, None], o_hat, o_inverse, 0).astype(
        jnp.bfloat16
    )[:, None]
    grad_ch = to_channels(grad_outer)
    grad_parts = triangle_back(pair_ch, grad_ch, own_length)
    grad_tiles = from_channels(grad_parts).astype(jnp.float32)
    grad_left = grad_tiles[:, 0]
    grad_right = grad_tiles[:, 1]
    d_left_lin = grad_left * left_sig * flipped
    d_left_pre = grad_left * left_lin * flipped * left_sig * (1.0 - left_sig)
    d_right_lin = grad_right * right_sig * flipped
    d_right_pre = grad_right * right_lin * flipped * right_sig * (1.0 - right_sig)
    grad_proj_in = jnp.concatenate([d_left_lin, d_left_pre, d_right_lin, d_right_pre], 0).astype(
        jnp.bfloat16
    )
    grad_z_norm = jnp.einsum("qji,cq->ijc", grad_proj_in, w_tri, preferred_element_type=jnp.float32)
    grad_z_norm = grad_z_norm + jnp.einsum(
        "ijd,cd->ijc", grad_gate, w_gate, preferred_element_type=jnp.float32
    )
    grad_w_tri = jnp.einsum("ijc,qji->cq", z_norm, grad_proj_in, preferred_element_type=jnp.float32)
    grad_w_gate = jnp.einsum("ijc,ijd->cd", z_norm, grad_gate, preferred_element_type=jnp.float32)
    grad_g_in = jnp.sum(grad_z_norm * z_hat, axis=(0, 1))
    grad_pair = normalize_back(grad_z_norm * gain_in, z_hat, z_inverse, -1).astype(jnp.bfloat16)
    totals = lax.psum(
        (jnp.concatenate([grad_w_tri, grad_w_gate], 1), grad_w_out, grad_g_in, grad_g_out),
        ("grp", "row", "col"),
    )
    return (
        mixed[None],
        grad_pair[None],
        totals[0] / N,
        totals[1] / N,
        totals[2] / N,
        totals[3] / N,
    )


def solution(mesh):
    return jax.shard_map(
        on_device,
        mesh=mesh,
        in_specs=(
            P("grp", "row", "col", None),
            P("grp", "row", "col", None),
            P(),
            P(),
            P(),
            P(),
            P(),
        ),
        out_specs=(P("grp", "row", "col", None), P("grp", "row", "col", None), P(), P(), P(), P()),
        check_vma=False,
    )
```

profile of v0, /device:TPU:1, one launch (start us, length us, event | category | flops | bytes accessed | tf_op | source)
XLA Modules:
  0.0 611.2 jit_solution(5704843328865412465)
XLA Ops:
  23.2 4.7 copy.53
  27.9 10.4 %all-to-all-start = ((bf16[128,1,2,64,128]{4,3,2,1,0:T(8,128)(2,1)}), bf16[128,1,2,64,128]{4,3,2,1,0:T(8,128)(2,1)}, u32[]{:S(2)}, u32[]{:S(2)}) async-start(bf16[128,1,2,64,128]{4,3,2,1,0:T(8,128)(2,1)} %copy.53), calls=%async_computation | async-start | bytes 8388608 | tf_op jit(solution)/shard_map/all_to_all | solution.py:29
  39.0 52.5 %all-to-all-done = bf16[128,1,2,64,128]{4,3,2,1,0:T(8,128)(2,1)} async-done(((bf16[128,1,2,64,128]{4,3,2,1,0:T(8,128)(2,1)}), bf16[128,1,2,64,128]{4,3,2,1,0:T(8,128)(2,1)}, u32[]{:S(2)}, u32[]{:S(2)}) %all-to-all-start) | async-done | bytes 4194336 | tf_op jit(solution)/shard_map/all_to_all | solution.py:29
  91.5 12.5 %copy.96 = bf16[4,4,8,2,64,128]{5,1,4,2,0,3:T(4,128)(2,1)} copy(bf16[4,4,8,2,64,128]{5,4,3,0,2,1:T(8,128)(2,1)} %bitcast.10) | data formatting | bytes 8388608 | tf_op jit(solution)/shard_map/reshape | solution.py:33
  104.0 7.2 %reshape.196 = bf16[4,2,512,512]{3,2,0,1:T(8,128)(2,1)} reshape(bf16[4,2,8,64,4,128]{5,4,3,2,0,1:T(4,128)(2,1)} %bitcast.180) | data formatting | bytes 8388608 | tf_op jit(solution)/shard_map/reshape | solution.py:35
  111.2 4.5 slice_bitcast_fusion
  118.3 5.4 while.20
  118.3 5.3 convolution_add_fusion.2
  131.5 4.7 copy.56
  136.2 8.7 %all-to-all-start.1 = ((bf16[32,4,1,64,128]{4,1,3,2,0:T(4,128)(2,1)}), bf16[32,4,1,64,128]{4,1,3,2,0:T(4,128)(2,1)}, u32[]{:S(2)}, u32[]{:S(2)}) async-start(bf16[32,4,1,64,128]{4,1,3,2,0:T(4,128)(2,1)} %bitcast.182), calls=%async_computation.1 | async-start | bytes 4194304 | tf_op jit(solution)/shard_map/all_to_all | solution.py:48
  144.9 18.4 %all-to-all-done.1 = bf16[32,4,1,64,128]{4,1,3,2,0:T(4,128)(2,1)} async-done(((bf16[32,4,1,64,128]{4,1,3,2,0:T(4,128)(2,1)}), bf16[32,4,1,64,128]{4,1,3,2,0:T(4,128)(2,1)}, u32[]{:S(2)}, u32[]{:S(2)}) %all-to-all-start.1) | async-done | bytes 2097184 | tf_op jit(solution)/shard_map/all_to_all | solution.py:48
  174.6 6.8 %fusion.28 = (bf16[128,64,128]{2,0,1:T(8,128)(2,1)}, bf16[1,128,64,128]{3,1,2,0:T(8,128)(2,1)}, bf16[128,64,128]{2,0,1:T(8,128)(2,1)S(1)}) fusion(f32[64,128,128]{2,1,0:T(8,128)S(1)} %fusion.52, f32[128,64]{0,1:T(8,128)S(1)} %and_convert_fusion, bf16[1,128,64,128]{3,2,1,0:T(8,128)(2,1)S(1)} %copy-done.18, bf16[128,640]{1,0:T(8,128)(2,1)S(1)} %copy-done.15, ...), kind=kOutput, calls=%fused_computation.38 | convolution fusion | flops 290455552 | bytes 14811648 | tf_op jit(solution)/shard_map/ijc,cd->ijd/dot_general | solution.py:108
  191.8 18.5 %all-to-all-done.2 = bf16[128,1,1,64,128]{4,3,2,1,0:T(8,128)(2,1)S(1)} async-done(((bf16[128,1,1,64,128]{4,3,2,1,0:T(8,128)(2,1)}), bf16[128,1,1,64,128]{4,3,2,1,0:T(8,128)(2,1)S(1)}, u32[]{:S(2)}, u32[]{:S(2)}) %all-to-all-start.2) | async-done | bytes 2097184 | tf_op jit(solution)/shard_map/all_to_all | solution.py:29
  223.0 6.9 %reshape.199 = bf16[4,2,8,64,4,128]{5,4,3,2,0,1:T(4,128)(2,1)} reshape(bf16[4,2,512,512]{3,2,0,1:T(8,128)(2,1)} %get-tuple-element.68) | data formatting | bytes 8388608 | tf_op jit(solution)/shard_map/reshape | solution.py:44
  230.0 8.1 %copy.62 = bf16[4,2,8,64,4,128]{5,0,3,1,2,4:T(4,128)(2,1)} copy(bf16[4,2,8,64,4,128]{5,4,3,2,0,1:T(4,128)(2,1)} %reshape.199) | data formatting | bytes 8388608 | tf_op jit(solution)/shard_map/reshape | solution.py:44
  238.0 4.9 all-to-all-start.3
  254.5 20.0 %all-to-all-done.3 = bf16[32,4,2,64,128]{4,1,3,2,0:T(4,128)(2,1)} async-done(((bf16[32,4,2,64,128]{4,1,3,2,0:T(4,128)(2,1)}), bf16[32,4,2,64,128]{4,1,3,2,0:T(4,128)(2,1)}, u32[]{:S(2)}, u32[]{:S(2)}) %all-to-all-start.3) | async-done | bytes 4194336 | tf_op jit(solution)/shard_map/all_to_all | solution.py:48
  278.0 5.4 bitcast_convert_fusion
  283.5 8.5 %fusion.66 = (f32[128,1,64,128]{3,2,1,0:T(8,128)}, f32[128,1,64,128]{3,2,1,0:T(8,128)}) fusion(f32[128,2,64,128]{3,2,1,0:T(8,128)} %bitcast_convert_fusion), kind=kLoop, calls=%fused_computation.120 | loop fusion | bytes 16777216 | tf_op jit(solution)/shard_map/slice | solution.py:140
  292.0 12.8 %multiply_convert_fusion.3 = (bf16[128,64,128]{2,0,1:T(8,128)(2,1)}, bf16[128,64,128]{2,0,1:T(8,128)(2,1)}, bf16[128,64,128]{2,0,1:T(8,128)(2,1)}, bf16[128,64,128]{2,0,1:T(8,128)(2,1)}) fusion(f32[128,1,64,128]{3,2,1,0:T(8,128)} %get-tuple-element.144, f32[64,128]{1,0:T(8,128)S(1)} %and_convert_fusion.1, f32[512,64,128]{2,0,1:T(8,128)S(1)} %bitcast.174, ...), kind=kLoop, calls=%fused_computation.62 | loop fusion | flops 25165824 | bytes 33587200 | tf_op jit(solution)/shard_map/convert.7
  304.8 6.7 %fusion.45 = f32[128,512]{1,0:T(8,128)S(1)} fusion(bf16[128,64,128]{2,0,1:T(8,128)(2,1)} %get-tuple-element.138, bf16[128,64,128]{2,0,1:T(8,128)(2,1)} %get-tuple-element.139, bf16[128,64,128]{2,0,1:T(8,128)(2,1)} %get-tuple-element.135, bf16[128,64,128]{2,0,1:T(8,128)(2,1)} %get-tuple-element.134, bf16[1,128,64,128]{1,3,2,0:T(8,128)(2,1)S(1)} %copy-done.6, ...), kind=kOutput, calls=%fused_computation.83 | convolution fusion | flops 1112539136 | bytes 10813952 | tf_op jit(solution)/shard_map/ijc,qji->cq/dot_general | solution.py:153
  316.1 132.1 %all-reduce = (f32[128]{0:T(128)S(1)}, f32[128]{0:T(128)S(1)}) all-reduce(f32[128]{0:T(128)S(1)} %get-tuple-element.104, f32[128]{0:T(128)S(1)} %get-tuple-element.102), channel_id=1, replica_groups=mesh['grp'=4,'row'=4,'col'=8] {'grp','row','col'}, use_global_device_ids=true, to_apply=%region_16.17 | all-reduce | flops 256 | bytes 2048 | tf_op jit(solution)/shard_map/psum | solution.py:157
  448.7 4.8 fusion.43
  458.9 141.8 %all-reduce.4.cloned.1.call-done = (f32[128,640]{1,0:T(8,128)}, f32[128,128]{1,0:T(8,128)}) async-done(((f32[128,640]{1,0:T(8,128)}, f32[128,128]{1,0:T(8,128)}), (f32[128,640]{1,0:T(8,128)}, f32[128,128]{1,0:T(8,128)})) %all-reduce.4.cloned.1.call-update) | async-done | bytes 393232 | tf_op jit(solution)/shard_map/psum | solution.py:157
  (97 shorter events, 93.8 us)
Async XLA Ops:
  7.2 164.3 %copy-start = (bf16[128,128]{1,0:T(8,128)(2,1)S(1)}, bf16[128,128]{1,0:T(8,128)(2,1)}, u32[]{:S(2)}) copy-start(bf16[128,128]{1,0:T(8,128)(2,1)} %param.15) | copy-start | bytes 98308
  9.8 4.8 copy-start.15
  9.8 4.8 copy-start.17
  13.2 159.2 %copy-start.5 = (bf16[1,128,64,128]{1,3,2,0:T(8,128)(2,1)}, bf16[1,128,64,128]{1,3,2,0:T(8,128)(2,1)S(1)}, u32[]{:S(2)}) copy-start(bf16[1,128,64,128]{1,3,2,0:T(8,128)(2,1)S(1)} %copy.49) | copy-start | bytes 6291460
  17.1 5.7 copy-start.2
  27.9 63.6 %all-to-all-start = ((bf16[128,1,2,64,128]{4,3,2,1,0:T(8,128)(2,1)}), bf16[128,1,2,64,128]{4,3,2,1,0:T(8,128)(2,1)}, u32[]{:S(2)}, u32[]{:S(2)}) async-start(bf16[128,1,2,64,128]{4,3,2,1,0:T(8,128)(2,1)} %copy.53), calls=%async_computation | async-start | bytes 8388608 | tf_op jit(solution)/shard_map/all_to_all | solution.py:29
  136.2 27.1 %all-to-all-start.1 = ((bf16[32,4,1,64,128]{4,1,3,2,0:T(4,128)(2,1)}), bf16[32,4,1,64,128]{4,1,3,2,0:T(4,128)(2,1)}, u32[]{:S(2)}, u32[]{:S(2)}) async-start(bf16[32,4,1,64,128]{4,1,3,2,0:T(4,128)(2,1)} %bitcast.182), calls=%async_computation.1 | async-start | bytes 4194304 | tf_op jit(solution)/shard_map/all_to_all | solution.py:48
  165.8 5.7 copy-start.16
  171.5 11.7 %copy-start.3 = (f32[32,4,1,64,128]{4,1,0,3,2:T(4,128)}, f32[32,4,1,64,128]{4,1,0,3,2:T(4,128)S(1)}, u32[]{:S(2)}) copy-start(f32[32,4,1,64,128]{4,1,0,3,2:T(4,128)S(1)} %copy.57) | copy-start | bytes 12582916
  187.6 22.7 %all-to-all-start.2 = ((bf16[128,1,1,64,128]{4,3,2,1,0:T(8,128)(2,1)}), bf16[128,1,1,64,128]{4,3,2,1,0:T(8,128)(2,1)S(1)}, u32[]{:S(2)}, u32[]{:S(2)}) async-start(bf16[128,1,1,64,128]{4,3,2,1,0:T(8,128)(2,1)} %copy.60), calls=%async_computation.2 | async-start | bytes 4194304 | tf_op jit(solution)/shard_map/all_to_all | solution.py:29
  238.0 36.5 %all-to-all-start.3 = ((bf16[32,4,2,64,128]{4,1,3,2,0:T(4,128)(2,1)}), bf16[32,4,2,64,128]{4,1,3,2,0:T(4,128)(2,1)}, u32[]{:S(2)}, u32[]{:S(2)}) async-start(bf16[32,4,2,64,128]{4,1,3,2,0:T(4,128)(2,1)} %bitcast.179), calls=%async_computation.3 | async-start | bytes 8388608 | tf_op jit(solution)/shard_map/all_to_all | solution.py:48
  242.9 4.7 copy-start.6
  242.9 357.7 %all-reduce.4.cloned.1.call-start = ((), (), s32[]{:S(2)}) async-start(), calls=%async_computation.4 | async-start | bytes 786432 | tf_op jit(solution)/shard_map/psum | solution.py:157
  243.2 4.4 copy-start.10
  274.5 17.5 %slice-start = ((s8[16777216]{0:T(1024)(128)(4,1)}), s8[4194304]{0:T(1024)(128)(4,1)S(1)}, s32[]{:S(2)}) async-start(s8[16777216]{0:T(1024)(128)(4,1)} %bitcast.173), calls=%async_computation.5 | async-start | bytes 8388608
  278.0 13.9 %slice-start.1 = ((s8[16777216]{0:T(1024)(128)(4,1)}), s8[4194304]{0:T(1024)(128)(4,1)S(1)}, s32[]{:S(2)}) async-start(s8[16777216]{0:T(1024)(128)(4,1)} %bitcast.173), calls=%async_computation.6 | async-start | bytes 8388608
  278.0 13.9 %slice-start.2 = ((s8[16777216]{0:T(1024)(128)(4,1)}), s8[4194304]{0:T(1024)(128)(4,1)S(1)}, s32[]{:S(2)}) async-start(s8[16777216]{0:T(1024)(128)(4,1)} %bitcast.173), calls=%async_computation.7 | async-start | bytes 8388608
  283.5 8.5 %slice-start.3 = ((s8[16777216]{0:T(1024)(128)(4,1)}), s8[4194304]{0:T(1024)(128)(4,1)S(1)}, s32[]{:S(2)}) async-start(s8[16777216]{0:T(1024)(128)(4,1)} %bitcast.173), calls=%async_computation.8 | async-start | bytes 8388608
  304.8 6.8 %copy-start.9 = (f32[128,64,128]{0,2,1:T(8,128)S(1)}, f32[128,64,128]{0,2,1:T(8,128)}, u32[]{:S(2)}) copy-start(f32[128,64,128]{0,2,1:T(8,128)} %fusion.54) | copy-start | bytes 12582916
  304.8 6.8 %copy-start.11 = (bf16[128,64,128]{2,0,1:T(8,128)(2,1)S(1)}, bf16[128,64,128]{2,0,1:T(8,128)(2,1)}, u32[]{:S(2)}) copy-start(bf16[128,64,128]{2,0,1:T(8,128)(2,1)} %get-tuple-element.134) | copy-start | bytes 6291460
  304.8 6.8 %copy-start.12 = (bf16[128,64,128]{2,0,1:T(8,128)(2,1)S(1)}, bf16[128,64,128]{2,0,1:T(8,128)(2,1)}, u32[]{:S(2)}) copy-start(bf16[128,64,128]{2,0,1:T(8,128)(2,1)} %get-tuple-element.135) | copy-start | bytes 6291460
  304.8 6.8 %copy-start.13 = (bf16[128,64,128]{2,0,1:T(8,128)(2,1)S(1)}, bf16[128,64,128]{2,0,1:T(8,128)(2,1)}, u32[]{:S(2)}) copy-start(bf16[128,64,128]{2,0,1:T(8,128)(2,1)} %get-tuple-element.138) | copy-start | bytes 6291460
  304.8 7.2 %copy-start.14 = (bf16[128,64,128]{2,0,1:T(8,128)(2,1)S(1)}, bf16[128,64,128]{2,0,1:T(8,128)(2,1)}, u32[]{:S(2)}) copy-start(bf16[128,64,128]{2,0,1:T(8,128)(2,1)} %get-tuple-element.139) | copy-start | bytes 6291460
  448.6 155.2 %copy-start.1 = (bf16[128,128]{1,0:T(8,128)(2,1)S(1)}, bf16[128,128]{1,0:T(8,128)(2,1)}, u32[]{:S(2)}) copy-start(bf16[128,128]{1,0:T(8,128)(2,1)} %param.15) | copy-start | bytes 98308
  (4 other events, 12.7 us)
Sparse Core Ops, SparseCore 0:
  458.5 142.1 all-reduce.3
where the time goes:
time: 619 us; the launch traced here: 611 us
  waiting for transfers between devices  251 us (41%)
  blocking collectives  132 us (21%)
  local copies, waits for them, and re-layouts  100 us (16%)
  other arithmetic  47.1 us (8%)
  matrix products  36.6 us (6%)
  starting transfers between devices  28.4 us (5%)
  between operations  15.7 us (3%)
    psum x1, waiting for transfers between devices, on_device(): lax.psum((jnp.concatenate([grad_w_tri, grad_w_gate], 1), grad_w_out, grad...  142 us
    psum x1, blocking collectives, on_device(): lax.psum((jnp.concatenate([grad_w_tri, grad_w_gate], 1), grad_w_out, grad...  132 us
    all_to_all x2, waiting for transfers between devices, to_channels(): lax.all_to_all(tile_set[:, None], ('row', 'col'), split_axis=0, concat_ax...  71 us
    all_to_all x2, waiting for transfers between devices, from_channels(): lax.all_to_all(spread, ('row', 'col'), split_axis=0, concat_axis=1, tiled...  38.3 us
    unnamed x49, local copies, waits for them, and re-layouts  19.4 us
    reshape x2, local copies, waits for them, and re-layouts, to_channels(): arrived.reshape(share_size, rows_n, cols_n, stack_size, col_len, row_len)  15.8 us
    reshape x2, local copies, waits for them, and re-layouts, from_channels(): pieces.reshape(share_size, stack_size, cols_n, col_len, rows_n, row_len)  15 us
    all_to_all x2, starting transfers between devices, to_channels(): lax.all_to_all(tile_set[:, None], ('row', 'col'), split_axis=0, concat_ax...  14.6 us
  transfers between devices with their start and end apart: 5, of which 5 were waited for; matrix products, arithmetic and copies ran while one was open for 2% of the time, Pallas kernels for 0%

commit v1 on v0

v1 whole, which is shorter than its diff:
```python
import functools

import jax
import jax.numpy as jnp
from jax import lax
from jax.experimental import pallas as pl
from jax.experimental.pallas import tpu as pltpu
from jax.sharding import PartitionSpec as P

N = 512
ALL = ("grp", "row", "col")
TILE = ("row", "col")


epsilon = 1e-05


def normalize(values, along):
    centred = values - jnp.mean(values, axis=along, keepdims=True)
    inverse = lax.rsqrt(jnp.mean(centred * centred, axis=along, keepdims=True) + epsilon)
    return (centred * inverse, inverse)


def normalize_back(grad_hat, normed, inverse, along):
    first_mean = jnp.mean(grad_hat, axis=along, keepdims=True)
    second_mean = jnp.mean(grad_hat * normed, axis=along, keepdims=True)
    return inverse * (grad_hat - first_mean - normed * second_mean)


def exchange(tiles):
    return lax.all_to_all(tiles, TILE, split_axis=0, concat_axis=0, tiled=True)


def forward_kernel(rows_n, cols_n, pair_ref, out_ref, left_ref, right_ref):
    col_len, row_len = pair_ref.shape[3], pair_ref.shape[4]
    for r in range(rows_n):
        for c in range(cols_n):
            at = (pl.ds(c * col_len, col_len), pl.ds(r * row_len, row_len))
            left_ref[at] = pair_ref[r * cols_n + c, 0, 0]
            right_ref[at] = pair_ref[r * cols_n + c, 0, 1]
    outer = lax.dot_general(
        right_ref[...], left_ref[...], (((0,), (0,)), ((), ())), preferred_element_type=jnp.float32
    ).astype(jnp.bfloat16)
    for r in range(rows_n):
        for c in range(cols_n):
            out_ref[r * cols_n + c, 0] = outer[
                c * col_len : (c + 1) * col_len, r * row_len : (r + 1) * row_len
            ]


def backward_kernel(rows_n, cols_n, pair_ref, grad_ref, out_ref, left_ref, right_ref, outer_ref):
    col_len, row_len = pair_ref.shape[3], pair_ref.shape[4]
    for r in range(rows_n):
        for c in range(cols_n):
            at = (pl.ds(c * col_len, col_len), pl.ds(r * row_len, row_len))
            left_ref[at] = pair_ref[r * cols_n + c, 0, 0]
            right_ref[at] = pair_ref[r * cols_n + c, 0, 1]
            outer_ref[at] = grad_ref[r * cols_n + c, 0]
    grad_left = lax.dot_general(
        right_ref[...], outer_ref[...], (((1,), (0,)), ((), ())), preferred_element_type=jnp.float32
    ).astype(jnp.bfloat16)
    grad_right = lax.dot_general(
        left_ref[...], outer_ref[...], (((1,), (1,)), ((), ())), preferred_element_type=jnp.float32
    ).astype(jnp.bfloat16)
    for r in range(rows_n):
        for c in range(cols_n):
            at = (slice(c * col_len, (c + 1) * col_len), slice(r * row_len, (r + 1) * row_len))
            out_ref[r * cols_n + c, 0, 0] = grad_left[at]
            out_ref[r * cols_n + c, 0, 1] = grad_right[at]


def triangle(pair_ch, rows_n, cols_n):
    devices, share, _, col_len, row_len = pair_ch.shape
    side = cols_n * col_len
    return pl.pallas_call(
        functools.partial(forward_kernel, rows_n, cols_n),
        grid=(share,),
        in_specs=[pl.BlockSpec((devices, 1, 2, col_len, row_len), lambda h: (0, h, 0, 0, 0))],
        out_specs=pl.BlockSpec((devices, 1, col_len, row_len), lambda h: (0, h, 0, 0)),
        out_shape=jax.ShapeDtypeStruct((devices, share, col_len, row_len), jnp.bfloat16),
        scratch_shapes=[pltpu.VMEM((side, side), jnp.bfloat16)] * 2,
        name="triangle_forward",
    )(pair_ch)


def triangle_back(pair_ch, grad_ch, rows_n, cols_n):
    devices, share, _, col_len, row_len = pair_ch.shape
    side = cols_n * col_len
    return pl.pallas_call(
        functools.partial(backward_kernel, rows_n, cols_n),
        grid=(share,),
        in_specs=[
            pl.BlockSpec((devices, 1, 2, col_len, row_len), lambda h: (0, h, 0, 0, 0)),
            pl.BlockSpec((devices, 1, col_len, row_len), lambda h: (0, h, 0, 0)),
        ],
        out_specs=pl.BlockSpec((devices, 1, 2, col_len, row_len), lambda h: (0, h, 0, 0, 0)),
        out_shape=jax.ShapeDtypeStruct(pair_ch.shape, jnp.bfloat16),
        scratch_shapes=[pltpu.VMEM((side, side), jnp.bfloat16)] * 3,
        name="triangle_backward",
    )(pair_ch, grad_ch)


def total_over_all(values):
    devices = lax.axis_size(ALL)
    width = values.shape[1]
    pieces = values.reshape(devices, -1)
    arrived = lax.all_to_all(pieces, ALL, split_axis=0, concat_axis=0, tiled=True)
    own = jnp.sum(arrived, axis=0, keepdims=True)
    spread = jnp.broadcast_to(own, pieces.shape)
    return lax.all_to_all(spread, ALL, split_axis=0, concat_axis=0, tiled=True).reshape(-1, width)


def on_device(pair_rep, cotangent, lengths, weight_in, weight_out, gain_in, gain_out):
    groups = lax.axis_size("grp")
    rows_n = lax.axis_size("row")
    cols_n = lax.axis_size("col")
    devices = rows_n * cols_n
    row_len = pair_rep.shape[1]
    col_len = pair_rep.shape[2]
    hidden_width = weight_out.shape[0]
    share = hidden_width // devices
    lookup = jnp.arange(groups) == lax.axis_index("grp")
    own_length = jnp.sum(jnp.where(lookup, lengths, 0))
    row_pos = lax.axis_index("row") * row_len + jnp.arange(row_len)
    col_pos = lax.axis_index("col") * col_len + jnp.arange(col_len)
    inside = ((row_pos[:, None] < own_length) & (col_pos[None, :] < own_length)).astype(jnp.float32)
    flipped = inside.T
    inside_c = inside[:, :, None]
    z_hat, z_inverse = normalize(pair_rep[0].astype(jnp.float32), -1)
    z_norm = (z_hat * gain_in).astype(jnp.bfloat16)
    w_tri = weight_in[:, : 4 * hidden_width]
    w_gate = weight_in[:, 4 * hidden_width :]
    projected = jnp.einsum("ijc,cq->qji", z_norm, w_tri, preferred_element_type=jnp.float32)
    gate_pre = jnp.einsum("ijc,cd->ijd", z_norm, w_gate, preferred_element_type=jnp.float32)
    left_lin = projected[0:hidden_width]
    left_pre = projected[hidden_width : 2 * hidden_width]
    right_lin = projected[2 * hidden_width : 3 * hidden_width]
    right_pre = projected[3 * hidden_width :]
    left_sig = jax.nn.sigmoid(left_pre)
    right_sig = jax.nn.sigmoid(right_pre)
    pair_tiles = jnp.stack(
        [left_sig * left_lin * flipped, right_sig * right_lin * flipped], 1
    ).astype(jnp.bfloat16)
    pair_ch = exchange(pair_tiles).reshape(devices, share, 2, col_len, row_len)
    outer_ch = triangle(pair_ch, rows_n, cols_n)
    outer_tile = exchange(outer_ch.reshape(hidden_width, col_len, row_len)).astype(jnp.float32)
    o_hat, o_inverse = normalize(outer_tile, 0)
    o_norm = (o_hat * gain_out[:, None, None]).astype(jnp.bfloat16)
    proj_out = jnp.einsum("hji,hc->ijc", o_norm, weight_out, preferred_element_type=jnp.float32)
    gate = jax.nn.sigmoid(gate_pre)
    mixed = (gate * proj_out * inside_c).astype(jnp.bfloat16)
    grad_out = cotangent[0].astype(jnp.float32)
    grad_proj = (grad_out * gate * inside_c).astype(jnp.bfloat16)
    grad_gate = (grad_out * proj_out * inside_c * gate * (1.0 - gate)).astype(jnp.bfloat16)
    grad_w_out = jnp.einsum("hji,ijc->hc", o_norm, grad_proj, preferred_element_type=jnp.float32)
    grad_o_norm = jnp.einsum(
        "ijc,hc->hji", grad_proj, weight_out, preferred_element_type=jnp.float32
    )
    grad_outer = normalize_back(grad_o_norm * gain_out[:, None, None], o_hat, o_inverse, 0).astype(
        jnp.bfloat16
    )
    grad_ch = exchange(grad_outer).reshape(devices, share, col_len, row_len)
    grad_parts = triangle_back(pair_ch, grad_ch, rows_n, cols_n)
    grad_tiles = exchange(grad_parts.reshape(hidden_width, 2, col_len, row_len)).astype(jnp.float32)
    grad_left = grad_tiles[:, 0]
    grad_right = grad_tiles[:, 1]
    d_left_lin = grad_left * left_sig * flipped
    d_left_pre = grad_left * left_lin * flipped * left_sig * (1.0 - left_sig)
    d_right_lin = grad_right * right_sig * flipped
    d_right_pre = grad_right * right_lin * flipped * right_sig * (1.0 - right_sig)
    grad_proj_in = jnp.concatenate([d_left_lin, d_left_pre, d_right_lin, d_right_pre], 0).astype(
        jnp.bfloat16
    )
    grad_z_norm = jnp.einsum("qji,cq->ijc", grad_proj_in, w_tri, preferred_element_type=jnp.float32)
    grad_z_norm = grad_z_norm + jnp.einsum(
        "ijd,cd->ijc", grad_gate, w_gate, preferred_element_type=jnp.float32
    )
    grad_w_tri = jnp.einsum("ijc,qji->cq", z_norm, grad_proj_in, preferred_element_type=jnp.float32)
    grad_w_gate = jnp.einsum("ijc,ijd->cd", z_norm, grad_gate, preferred_element_type=jnp.float32)
    grad_pair = normalize_back(grad_z_norm * gain_in, z_hat, z_inverse, -1).astype(jnp.bfloat16)
    totals = total_over_all(jnp.concatenate([grad_w_tri, grad_w_gate, grad_w_out], 1)) / N
    grad_w_in = totals[:, : weight_in.shape[1]]
    grad_w_out = totals[:, weight_in.shape[1] :]
    grad_g_in = jnp.sum(grad_w_in * weight_in.astype(jnp.float32), axis=1) / gain_in
    grad_g_out = jnp.sum(grad_w_out * weight_out.astype(jnp.float32), axis=1) / gain_out
    return (mixed[None], grad_pair[None], grad_w_in, grad_w_out, grad_g_in, grad_g_out)


def solution(mesh):
    return jax.shard_map(
        on_device,
        mesh=mesh,
        in_specs=(
            P("grp", "row", "col", None),
            P("grp", "row", "col", None),
            P(),
            P(),
            P(),
            P(),
            P(),
        ),
        out_specs=(P("grp", "row", "col", None), P("grp", "row", "col", None), P(), P(), P(), P()),
        check_vma=False,
    )
```

time: 619 us -> 312 us (0.50)
  waiting for transfers between devices: 251 us -> 88.6 us
  local copies, waits for them, and re-layouts: 100 us -> 21.5 us
  blocking collectives: 132 us -> 92.6 us
  between operations: 15.7 us -> 1.25 us
  other arithmetic: 47.1 us -> 32.8 us
  Pallas kernels: 0 us -> 11.9 us
  matrix products: 36.6 us -> 26 us
    psum x1 -> x0, waiting for transfers between devices: 142 us -> none  [on_device(): lax.psum((jnp.concatenate([grad_w_tri, grad_w_gate], 1), grad_w_out, grad...]
    psum x1 -> x0, blocking collectives: 132 us -> none  [on_device(): lax.psum((jnp.concatenate([grad_w_tri, grad_w_gate], 1), grad_w_out, grad...]
    all_to_all x0 -> x2, blocking collectives: none -> 92.6 us  [exchange(): return lax.all_to_all(tiles, TILE, split_axis=0, concat_axis=0, tiled=True)]
    reshape x5 -> x0, local copies, waits for them, and re-layouts: 38 us -> none  [the longest x2 15.8 us: to_channels(): arrived.reshape(share_size, rows_n, cols_n, stack_size, col_len, row_len)]
    all_to_all x4, waiting for transfers between devices: 109 us -> 88.6 us  [the longest x2 72.6 us: exchange(): return lax.all_to_all(tiles, TILE, split_axis=0, concat_axis=0, tiled=True)]
    another operation x4 -> x0, local copies, waits for them, and re-layouts: 14.1 us -> none  [the longest x2 8.66 us: from_channels(): pieces.reshape(share_size, stack_size, cols_n, col_len, rows_n, row_len)]
    pallas_call x0 -> x2, Pallas kernels: none -> 11.9 us  [the longest x1 6.64 us: triangle_back(): pl.pallas_call(functools.partial(backward_kernel, rows_n, cols_n), grid=(...]
    dot_general x3 -> x0, matrix products: 8.64 us -> none  [the longest x1 5.29 us: advance(): jnp.einsum('hkj,hki->hji', right_part, left_part, preferred_element_type=...]
  transfers between devices with their start and end apart: 5 -> 4, of which waited for: 5 -> 4; matrix products, arithmetic and copies ran while one was open for 2% -> 6% of each run, Pallas kernels for 0% -> 0%
where the time goes in v1:
time: 312 us; the launch traced here: 308 us
  blocking collectives  92.6 us (30%)
  waiting for transfers between devices  88.6 us (28%)
  starting transfers between devices  33 us (11%)
  other arithmetic  32.8 us (11%)
  matrix products  26 us (8%)
  local copies, waits for them, and re-layouts  21.5 us (7%)
  Pallas kernels  11.9 us (4%)
    all_to_all x2, blocking collectives, exchange(): return lax.all_to_all(tiles, TILE, split_axis=0, concat_axis=0, tiled=True)  92.6 us
    all_to_all x2, waiting for transfers between devices, exchange(): return lax.all_to_all(tiles, TILE, split_axis=0, concat_axis=0, tiled=True)  72.6 us
    all_to_all x2, starting transfers between devices, exchange(): return lax.all_to_all(tiles, TILE, split_axis=0, concat_axis=0, tiled=True)  19 us
    unnamed x32, local copies, waits for them, and re-layouts  15.4 us
    all_to_all x1, waiting for transfers between devices, total_over_all(): lax.all_to_all(pieces, ALL, split_axis=0, concat_axis=0, tiled=True)  12.4 us
    all_to_all x1, starting transfers between devices, total_over_all(): lax.all_to_all(pieces, ALL, split_axis=0, concat_axis=0, tiled=True)  9.61 us
    another operation x1, other arithmetic  8.23 us
    dot_general x1, matrix products, on_device(): jnp.einsum('ijc,cd->ijd', z_norm, w_gate, preferred_element_type=jnp.floa...  6.87 us
  transfers between devices with their start and end apart: 4, of which 4 were waited for; matrix products, arithmetic and copies ran while one was open for 6% of the time, Pallas kernels for 0%

profile of v1, /device:TPU:1, one launch (start us, length us, event | category | flops | bytes accessed | tf_op | source)
XLA Modules:
  0.0 307.6 jit_solution(3780995744246136160)
XLA Ops:
  3.3 3.4 %copy.30 = bf16[1,128,64,128]{1,3,2,0:T(8,128)(2,1)S(1)} copy(bf16[1,128,64,128]{3,2,1,0:T(8,128)(2,1)} %param.7) | data formatting | bytes 4194304 | tf_op args[0]
  13.0 3.4 %copy-done = f32[512,64,128]{2,0,1:T(8,128)} copy-done((f32[512,64,128]{2,0,1:T(8,128)}, f32[512,64,128]{2,0,1:T(8,128)S(1)}, u32[]{:S(2)}) %copy-start) | copy-done | bytes 16777240
  16.8 2.7 copy.34
  19.5 60.0 %all_to_all.35 = bf16[128,2,64,128]{3,2,1,0:T(8,128)(2,1)} all-to-all(bf16[128,2,64,128]{3,2,1,0:T(8,128)(2,1)S(1)} %copy.34), channel_id=1, replica_groups=mesh['grp'=4,'row'=4,'col'=8] {'row','col'}, dimensions={0} | all-to-all | bytes 8388608 | tf_op jit(solution)/shard_map/all_to_all | solution.py:31
  79.5 5.2 %triangle_forward.1 = bf16[32,4,64,128]{3,2,1,0:T(8,128)(2,1)} custom-call(bf16[32,4,2,64,128]{4,3,2,1,0:T(8,128)(2,1)} %bitcast.119), custom_call_target="tpu_custom_call" | custom-call | tf_op jit(solution)/shard_map/triangle_forward/pallas_call | solution.py:75
  84.7 5.4 %all-to-all-start.1 = ((bf16[128,64,128]{2,1,0:T(8,128)(2,1)}), bf16[128,64,128]{2,1,0:T(8,128)(2,1)S(1)}, u32[]{:S(2)}, u32[]{:S(2)}) async-start(bf16[128,64,128]{2,1,0:T(8,128)(2,1)} %bitcast.122), calls=%async_computation.1 | async-start | bytes 4194304 | tf_op jit(solution)/shard_map/all_to_all | solution.py:31
  90.2 28.7 %all-to-all-done.1 = bf16[128,64,128]{2,1,0:T(8,128)(2,1)S(1)} async-done(((bf16[128,64,128]{2,1,0:T(8,128)(2,1)}), bf16[128,64,128]{2,1,0:T(8,128)(2,1)S(1)}, u32[]{:S(2)}, u32[]{:S(2)}) %all-to-all-start.1) | async-done | bytes 2097184 | tf_op jit(solution)/shard_map/all_to_all | solution.py:31
  124.4 6.9 %fusion.28 = (bf16[128,64,128]{2,0,1:T(8,128)(2,1)}, bf16[1,128,64,128]{3,1,2,0:T(8,128)(2,1)}, bf16[128,64,128]{2,0,1:T(8,128)(2,1)S(1)}) fusion(f32[64,128,128]{2,1,0:T(8,128)S(1)} %fusion.49, f32[128,64]{0,1:T(8,128)S(1)} %and_convert_fusion, bf16[1,128,64,128]{3,2,1,0:T(8,128)(2,1)S(1)} %copy-done.11, bf16[128,640]{1,0:T(8,128)(2,1)S(1)} %copy-done.7, ...), kind=kOutput, calls=%fused_computation.36 | convolution fusion | flops 290455552 | bytes 14811648 | tf_op jit(solution)/shard_map/ijc,cd->ijd/dot_general | solution.py:134
  137.3 32.6 %all_to_all.36 = bf16[128,64,128]{2,1,0:T(8,128)(2,1)} all-to-all(bf16[128,64,128]{2,1,0:T(8,128)(2,1)S(1)} %copy.38), channel_id=1, replica_groups=mesh['grp'=4,'row'=4,'col'=8] {'row','col'}, dimensions={0} | all-to-all | bytes 4194304 | tf_op jit(solution)/shard_map/all_to_all | solution.py:31
  169.8 6.6 %triangle_backward.1 = bf16[32,4,2,64,128]{4,3,2,1,0:T(8,128)(2,1)} custom-call(bf16[32,4,2,64,128]{4,3,2,1,0:T(8,128)(2,1)} %bitcast.120, bf16[32,4,64,128]{3,2,1,0:T(8,128)(2,1)} %bitcast.123), custom_call_target="tpu_custom_call" | custom-call | tf_op jit(solution)/shard_map/triangle_backward/pallas_call | solution.py:89
  176.5 13.6 %all-to-all-start.3 = ((bf16[128,2,64,128]{3,2,1,0:T(8,128)(2,1)}), bf16[128,2,64,128]{3,2,1,0:T(8,128)(2,1)}, u32[]{:S(2)}, u32[]{:S(2)}) async-start(bf16[128,2,64,128]{3,2,1,0:T(8,128)(2,1)} %bitcast.121), calls=%async_computation.3 | async-start | bytes 8388608 | tf_op jit(solution)/shard_map/all_to_all | solution.py:31
  190.1 4.4 %copy.46 = bf16[1,128,64,128]{3,2,1,0:T(8,128)(2,1)} copy(bf16[1,128,64,128]{3,1,2,0:T(8,128)(2,1)} %get-tuple-element.33) | data formatting | bytes 4194304
  195.5 2.7 fusion.54
  199.9 43.9 %all-to-all-done.3 = bf16[128,2,64,128]{3,2,1,0:T(8,128)(2,1)} async-done(((bf16[128,2,64,128]{3,2,1,0:T(8,128)(2,1)}), bf16[128,2,64,128]{3,2,1,0:T(8,128)(2,1)}, u32[]{:S(2)}, u32[]{:S(2)}) %all-to-all-start.3) | async-done | bytes 4194336 | tf_op jit(solution)/shard_map/all_to_all | solution.py:31
  243.8 4.6 %copy_convert_fusion = f32[128,2,64,128]{3,0,2,1:T(8,128)S(1)} fusion(bf16[128,2,64,128]{3,2,1,0:T(8,128)(2,1)} %all-to-all-done.3), kind=kLoop, calls=%fused_computation.55 | loop fusion | flops 2097152 | bytes 12582912 | tf_op jit(solution)/shard_map/convert_element_type | solution.py:164
  248.4 8.2 %multiply_convert_fusion.3 = (bf16[128,64,128]{2,0,1:T(8,128)(2,1)S(1)}, bf16[128,64,128]{2,0,1:T(8,128)(2,1)S(1)}, bf16[128,64,128]{2,0,1:T(8,128)(2,1)S(1)}, bf16[128,64,128]{2,0,1:T(8,128)(2,1)S(1)}) fusion(f32[128,2,64,128]{3,0,2,1:T(8,128)S(1)} %copy_convert_fusion, f32[64,128]{1,0:T(8,128)S(1)} %and_convert_fusion.1, f32[512,64,128]{2,0,1:T(8,128)} %copy-done), kind=kLoop, calls=%fused_computation.59 | loop fusion | flops 25165824 | bytes 33587200 | tf_op jit(solution)/shard_map/convert.1
  256.6 2.9 fusion.43
  259.5 3.7 %fusion.66 = (f32[128,64]{0,1:T(8,128)S(1)}, f32[128,64]{0,1:T(8,128)S(1)}, f32[128,64,128]{0,2,1:T(8,128)}) fusion(f32[128,64]{0,1:T(8,128)S(1)} %add_rsqrt_fusion.1, f32[128,64]{0,1:T(8,128)S(1)} %broadcast_multiply_fusion.6, bf16[1,128,64,128]{1,3,2,0:T(8,128)(2,1)S(1)} %copy-done.4, f32[128]{0:T(128)S(1)} %copy-done.10, ...), kind=kOutput, calls=%fused_computation.105 | convolution fusion | flops 1115668480 | bytes 19137024 | tf_op jit(solution)/shard_map/qji,cq->ijc/dot_general | solution.py:174
  264.5 9.6 %all-to-all-start.4 = ((f32[128,1,768]{2,1,0:T(1,128)}), f32[128,1,768]{2,1,0:T(1,128)S(1)}, u32[]{:S(2)}, u32[]{:S(2)}) async-start(f32[128,1,768]{2,1,0:T(1,128)} %copy.45), calls=%async_computation.4 | async-start | bytes 786432 | tf_op jit(solution)/shard_map/all_to_all | solution.py:107
  274.1 12.4 %all-to-all-done.4 = f32[128,1,768]{2,1,0:T(1,128)S(1)} async-done(((f32[128,1,768]{2,1,0:T(1,128)}), f32[128,1,768]{2,1,0:T(1,128)S(1)}, u32[]{:S(2)}, u32[]{:S(2)}) %all-to-all-start.4) | async-done | bytes 393248 | tf_op jit(solution)/shard_map/all_to_all | solution.py:107
  287.7 4.3 %all-to-all-start.5 = ((f32[128,1,768]{2,1,0:T(1,128)}), f32[128,1,768]{2,1,0:T(1,128)S(1)}, u32[]{:S(2)}, u32[]{:S(2)}) async-start(f32[128,1,768]{2,1,0:T(1,128)} %broadcast_in_dim.13), calls=%async_computation.5 | async-start | bytes 786432 | tf_op jit(solution)/shard_map/all_to_all | solution.py:110
  292.1 4.8 %fusion.41 = bf16[1,128,64,128]{1,3,2,0:T(8,128)(2,1)} fusion(bf16[1,128,64,128]{1,3,2,0:T(8,128)(2,1)S(1)} %copy-done.4, f32[128,64,128]{0,2,1:T(8,128)} %get-tuple-element.36, f32[128,64]{0,1:T(8,128)S(1)} %broadcast_multiply_fusion.4, f32[128,64]{0,1:T(8,128)S(1)} %broadcast_multiply_fusion.5, f32[128,64]{0,1:T(8,128)S(1)} %add_rsqrt_fusion.1, ...), kind=kLoop, calls=%fused_computation.66 | loop fusion | flops 8388608 | bytes 8519680 | tf_op jit(solution)/shard_map/broadcast_in_dim | solution.py:186
  296.9 4.1 %copy.47 = bf16[1,128,64,128]{3,2,1,0:T(8,128)(2,1)} copy(bf16[1,128,64,128]{1,3,2,0:T(8,128)(2,1)} %fusion.41) | data formatting | bytes 4194304
  301.0 3.6 %all-to-all-done.5 = f32[128,1,768]{2,1,0:T(1,128)S(1)} async-done(((f32[128,1,768]{2,1,0:T(1,128)}), f32[128,1,768]{2,1,0:T(1,128)S(1)}, u32[]{:S(2)}, u32[]{:S(2)}) %all-to-all-start.5) | async-done | bytes 393248 | tf_op jit(solution)/shard_map/all_to_all | solution.py:110
  (62 shorter events, 28.6 us)
Async XLA Ops:
  3.2 4.8 %copy-start.7 = (bf16[128,640]{1,0:T(8,128)(2,1)S(1)}, bf16[128,640]{1,0:T(8,128)(2,1)}, u32[]{:S(2)}) copy-start(bf16[128,640]{1,0:T(8,128)(2,1)} %param.10) | copy-start | bytes 491524
  3.3 4.8 %copy-start.10 = (f32[128]{0:T(128)S(1)}, f32[128]{0:T(128)}, u32[]{:S(2)}) copy-start(f32[128]{0:T(128)} %param.12) | copy-start | bytes 1540
  6.7 3.9 %copy-start.1 = (bf16[1,128,64,128]{1,3,2,0:T(8,128)(2,1)}, bf16[1,128,64,128]{1,3,2,0:T(8,128)(2,1)S(1)}, u32[]{:S(2)}) copy-start(bf16[1,128,64,128]{1,3,2,0:T(8,128)(2,1)S(1)} %copy.30) | copy-start | bytes 6291460
  10.5 5.8 %copy-start = (f32[512,64,128]{2,0,1:T(8,128)}, f32[512,64,128]{2,0,1:T(8,128)S(1)}, u32[]{:S(2)}) copy-start(f32[512,64,128]{2,0,1:T(8,128)S(1)} %convolution_bitcast_fusion) | copy-start | bytes 50331652
  84.7 37.1 %copy-start.8 = (bf16[128,128]{1,0:T(8,128)(2,1)S(1)}, bf16[128,128]{1,0:T(8,128)(2,1)}, u32[]{:S(2)}) copy-start(bf16[128,128]{1,0:T(8,128)(2,1)} %param.11) | copy-start | bytes 98308
  84.7 37.1 %copy-start.9 = (f32[128]{0:T(128)S(1)}, f32[128]{0:T(128)}, u32[]{:S(2)}) copy-start(f32[128]{0:T(128)} %param.13) | copy-start | bytes 1540
  84.7 34.2 %all-to-all-start.1 = ((bf16[128,64,128]{2,1,0:T(8,128)(2,1)}), bf16[128,64,128]{2,1,0:T(8,128)(2,1)S(1)}, u32[]{:S(2)}, u32[]{:S(2)}) async-start(bf16[128,64,128]{2,1,0:T(8,128)(2,1)} %bitcast.122), calls=%async_computation.1 | async-start | bytes 4194304 | tf_op jit(solution)/shard_map/all_to_all | solution.py:31
  120.2 4.1 %copy-start.2 = (bf16[1,128,64,128]{1,3,2,0:T(8,128)(2,1)S(1)}, bf16[1,128,64,128]{1,3,2,0:T(8,128)(2,1)}, u32[]{:S(2)}) copy-start(bf16[1,128,64,128]{1,3,2,0:T(8,128)(2,1)} %copy-done.1) | copy-start | bytes 6291460
  120.2 4.1 %copy-start.11 = (bf16[1,128,64,128]{3,2,1,0:T(8,128)(2,1)S(1)}, bf16[1,128,64,128]{3,2,1,0:T(8,128)(2,1)}, u32[]{:S(2)}) copy-start(bf16[1,128,64,128]{3,2,1,0:T(8,128)(2,1)} %param.8) | copy-start | bytes 6291460
  131.2 2.2 copy-start.12
  176.5 67.3 %all-to-all-start.3 = ((bf16[128,2,64,128]{3,2,1,0:T(8,128)(2,1)}), bf16[128,2,64,128]{3,2,1,0:T(8,128)(2,1)}, u32[]{:S(2)}, u32[]{:S(2)}) async-start(bf16[128,2,64,128]{3,2,1,0:T(8,128)(2,1)} %bitcast.121), calls=%async_computation.3 | async-start | bytes 8388608 | tf_op jit(solution)/shard_map/all_to_all | solution.py:31
  190.1 4.4 %copy-start.3 = (bf16[1,128,64,128]{1,3,2,0:T(8,128)(2,1)S(1)}, bf16[1,128,64,128]{1,3,2,0:T(8,128)(2,1)}, u32[]{:S(2)}) copy-start(bf16[1,128,64,128]{1,3,2,0:T(8,128)(2,1)} %copy-done.1) | copy-start | bytes 6291460
  190.1 4.4 %copy-start.6 = (bf16[128,64,128]{2,0,1:T(8,128)(2,1)S(1)}, bf16[128,64,128]{2,0,1:T(8,128)(2,1)}, u32[]{:S(2)}) copy-start(bf16[128,64,128]{2,0,1:T(8,128)(2,1)} %get-tuple-element.32) | copy-start | bytes 6291460
  195.5 2.7 copy-start.13
  248.4 8.2 %copy-start.4 = (bf16[1,128,64,128]{1,3,2,0:T(8,128)(2,1)S(1)}, bf16[1,128,64,128]{1,3,2,0:T(8,128)(2,1)}, u32[]{:S(2)}) copy-start(bf16[1,128,64,128]{1,3,2,0:T(8,128)(2,1)} %copy-done.1) | copy-start | bytes 6291460
  256.6 2.9 copy-start.5
  264.5 22.1 %all-to-all-start.4 = ((f32[128,1,768]{2,1,0:T(1,128)}), f32[128,1,768]{2,1,0:T(1,128)S(1)}, u32[]{:S(2)}, u32[]{:S(2)}) async-start(f32[128,1,768]{2,1,0:T(1,128)} %copy.45), calls=%async_computation.4 | async-start | bytes 786432 | tf_op jit(solution)/shard_map/all_to_all | solution.py:107
  287.7 16.8 %all-to-all-start.5 = ((f32[128,1,768]{2,1,0:T(1,128)}), f32[128,1,768]{2,1,0:T(1,128)S(1)}, u32[]{:S(2)}, u32[]{:S(2)}) async-start(f32[128,1,768]{2,1,0:T(1,128)} %broadcast_in_dim.13), calls=%async_computation.5 | async-start | bytes 786432 | tf_op jit(solution)/shard_map/all_to_all | solution.py:110

commit v2 on v1

--- a/solution.py
+++ b/solution.py
@@ -110,6 +110,73 @@
     return lax.all_to_all(spread, ALL, split_axis=0, concat_axis=0, tiled=True).reshape(-1, width)
 
 
+def project_kernel(scalar_ref, pair_ref, weight_ref, gain_ref, tile_ref, norm_ref):
+    block = pl.program_id(0)
+    row_len, block_len, _ = pair_ref.shape
+    channels = weight_ref.shape[0] // 2
+    values = jnp.swapaxes(pair_ref[...].astype(jnp.float32), 0, 1)
+    normed, _ = normalize(values, -1)
+    normed = (normed * gain_ref[...]).astype(jnp.bfloat16)
+    norm_ref[...] = normed
+    length, row_start, col_start = scalar_ref[0], scalar_ref[1], scalar_ref[2]
+    row_in = row_start + lax.broadcasted_iota(jnp.int32, (1, row_len), 1) < length
+    gated = []
+    for j in range(block_len):
+        projected = lax.dot_general(
+            weight_ref[...], normed[j], (((1,), (1,)), ((), ())), preferred_element_type=jnp.float32
+        )
+        col_in = col_start + block * block_len + j < length
+        inside = jnp.where(row_in & col_in, 1.0, 0.0)
+        gated.append(projected[:channels] * jax.nn.sigmoid(projected[channels:]) * inside)
+    gated = jnp.swapaxes(jnp.stack(gated, 0), 0, 1).astype(jnp.bfloat16)
+    tile_ref[...] = gated.reshape(tile_ref.shape)
+
+
+def project(scalars, pair_rep, weight_rows, gain, block_len=16):
+    row_len, col_len, width = pair_rep.shape
+    hidden_width = weight_rows.shape[0] // 4
+    return pl.pallas_call(
+        project_kernel,
+        grid=(col_len // block_len,),
+        in_specs=[
+            pl.BlockSpec(memory_space=pltpu.SMEM),
+            pl.BlockSpec((row_len, block_len, width), lambda j: (0, j, 0)),
+            pl.BlockSpec(weight_rows.shape, lambda j: (0, 0)),
+            pl.BlockSpec((1, width), lambda j: (0, 0)),
+        ],
+        out_specs=[
+            pl.BlockSpec((hidden_width, 2, block_len, row_len), lambda j: (0, 0, j, 0)),
+            pl.BlockSpec((block_len, row_len, width), lambda j: (j, 0, 0)),
+        ],
+        out_shape=[
+            jax.ShapeDtypeStruct((hidden_width, 2, col_len, row_len), jnp.bfloat16),
+            jax.ShapeDtypeStruct((col_len, row_len, width), jnp.bfloat16),
+        ],
+        name="project",
+    )(scalars, pair_rep, weight_rows, gain[None])
+
+
+def outer_grad_kernel(outer_ref, back_ref, mean_ref, grad_ref):
+    o_hat, o_inverse = normalize(outer_ref[...].astype(jnp.float32), 0)
+    back = back_ref[...]
+    second_mean = jnp.mean(back * o_hat, axis=0, keepdims=True)
+    grad = o_inverse * (back - mean_ref[...][None] - o_hat * second_mean)
+    grad_ref[...] = grad.astype(jnp.bfloat16)
+
+
+def outer_grad(outer_tile, back, back_mean, block_len=16):
+    hidden_width, col_len, row_len = outer_tile.shape
+    whole = pl.BlockSpec((hidden_width, block_len, row_len), lambda j: (0, j, 0))
+    return pl.pallas_call(
+        outer_grad_kernel,
+        grid=(col_len // block_len,),
+        in_specs=[whole, whole, pl.BlockSpec((block_len, row_len), lambda j: (j, 0))],
+        out_specs=whole,
+        out_shape=jax.ShapeDtypeStruct(outer_tile.shape, jnp.bfloat16),
+        name="outer_grad",
+    )(outer_tile, back, back_mean)
+
+
 def on_device(pair_rep, cotangent, lengths, weight_in, weight_out, gain_in, gain_out):
     groups = lax.axis_size("grp")
     rows_n = lax.axis_size("row")
@@ -117,72 +184,81 @@
     devices = rows_n * cols_n
     row_len = pair_rep.shape[1]
     col_len = pair_rep.shape[2]
+    width = pair_rep.shape[3]
     hidden_width = weight_out.shape[0]
     share = hidden_width // devices
     lookup = jnp.arange(groups) == lax.axis_index("grp")
     own_length = jnp.sum(jnp.where(lookup, lengths, 0))
-    row_pos = lax.axis_index("row") * row_len + jnp.arange(row_len)
-    col_pos = lax.axis_index("col") * col_len + jnp.arange(col_len)
-    inside = ((row_pos[:, None] < own_length) & (col_pos[None, :] < own_length)).astype(jnp.float32)
-    flipped = inside.T
-    inside_c = inside[:, :, None]
-    z_hat, z_inverse = normalize(pair_rep[0].astype(jnp.float32), -1)
-    z_norm = (z_hat * gain_in).astype(jnp.bfloat16)
-    w_tri = weight_in[:, : 4 * hidden_width]
+    row_start = lax.axis_index("row") * row_len
+    col_start = lax.axis_index("col") * col_len
+    scalars = jnp.stack([own_length, row_start, col_start]).astype(jnp.int32)
+    row_in = row_start + jnp.arange(row_len) < own_length
+    col_in = col_start + jnp.arange(col_len) < own_length
+    flipped = (col_in[:, None] & row_in[None, :]).astype(jnp.float32)
+    flipped_c = flipped[:, :, None]
     w_gate = weight_in[:, 4 * hidden_width :]
-    projected = jnp.einsum("ijc,cq->qji", z_norm, w_tri, preferred_element_type=jnp.float32)
-    gate_pre = jnp.einsum("ijc,cd->ijd", z_norm, w_gate, preferred_element_type=jnp.float32)
-    left_lin = projected[0:hidden_width]
-    left_pre = projected[hidden_width : 2 * hidden_width]
-    right_lin = projected[2 * hidden_width : 3 * hidden_width]
-    right_pre = projected[3 * hidden_width :]
-    left_sig = jax.nn.sigmoid(left_pre)
-    right_sig = jax.nn.sigmoid(right_pre)
-    pair_tiles = jnp.stack(
-        [left_sig * left_lin * flipped, right_sig * right_lin * flipped], 1
-    ).astype(jnp.bfloat16)
+    w_tri = weight_in[:, : 4 * hidden_width].reshape(width, 2, 2, hidden_width)
+    w_tri = w_tri.transpose(0, 2, 3, 1).reshape(width, 4 * hidden_width)
+
+    pair_tiles, z_norm = project(scalars, pair_rep[0], w_tri.T, gain_in)
     pair_ch = exchange(pair_tiles).reshape(devices, share, 2, col_len, row_len)
+
+    projected = jnp.einsum("jic,cq->qji", z_norm, w_tri, preferred_element_type=jnp.float32)
+    projected = projected.reshape(2, hidden_width, 2, col_len, row_len)
+    sig = jax.nn.sigmoid(projected[1])
+    factors = jnp.stack([sig * flipped, projected[0] * flipped * sig * (1.0 - sig)], 0)
+    factors = factors.astype(jnp.bfloat16)
+    gate_pre = jnp.einsum("jic,cd->jid", z_norm, w_gate, preferred_element_type=jnp.float32)
+    gate = jax.nn.sigmoid(gate_pre) * flipped_c
+    grad_out = jnp.swapaxes(cotangent[0], 0, 1).astype(jnp.float32)
+    grad_proj = (grad_out * gate).astype(jnp.bfloat16)
+    grad_o_norm = jnp.einsum(
+        "jic,hc->hji", grad_proj, weight_out, preferred_element_type=jnp.float32
+    )
+    back = grad_o_norm * gain_out[:, None, None]
+    back_mean = jnp.mean(back, axis=0)
+    pair_ch, factors, gate, grad_proj, back, back_mean = lax.optimization_barrier(
+        (pair_ch, factors, gate, grad_proj, back, back_mean)
+    )
+
     outer_ch = triangle(pair_ch, rows_n, cols_n)
-    outer_tile = exchange(outer_ch.reshape(hidden_width, col_len, row_len)).astype(jnp.float32)
-    o_hat, o_inverse = normalize(outer_tile, 0)
+    outer_tile = exchange(outer_ch.reshape(hidden_width, col_len, row_len))
+    grad_outer = outer_grad(outer_tile, back, back_mean)
+    grad_ch = exchange(grad_outer).reshape(devices, share, col_len, row_len)
+
+    o_hat, _ = normalize(outer_tile.astype(jnp.float32), 0)
     o_norm = (o_hat * gain_out[:, None, None]).astype(jnp.bfloat16)
-    proj_out = jnp.einsum("hji,hc->ijc", o_norm, weight_out, preferred_element_type=jnp.float32)
-    gate = jax.nn.sigmoid(gate_pre)
-    mixed = (gate * proj_out * inside_c).astype(jnp.bfloat16)
-    grad_out = cotangent[0].astype(jnp.float32)
-    grad_proj = (grad_out * gate * inside_c).astype(jnp.bfloat16)
-    grad_gate = (grad_out * proj_out * inside_c * gate * (1.0 - gate)).astype(jnp.bfloat16)
-    grad_w_out = jnp.einsum("hji,ijc->hc", o_norm, grad_proj, preferred_element_type=jnp.float32)
-    grad_o_norm = jnp.einsum(
-        "ijc,hc->hji", grad_proj, weight_out, preferred_element_type=jnp.float32
-    )
-    grad_outer = normalize_back(grad_o_norm * gain_out[:, None, None], o_hat, o_inverse, 0).astype(
-        jnp.bfloat16
-    )
-    grad_ch = exchange(grad_outer).reshape(devices, share, col_len, row_len)
+    proj_out = jnp.einsum("hji,hc->jic", o_norm, weight_out, preferred_element_type=jnp.float32)
+    mixed = jnp.swapaxes((gate * proj_out).astype(jnp.bfloat16), 0, 1)
+    grad_gate = (grad_out * proj_out * gate * (1.0 - gate)).astype(jnp.bfloat16)
+    grad_w_out = jnp.einsum("hji,jic->hc", o_norm, grad_proj, preferred_element_type=jnp.float32)
+    grad_w_gate = jnp.einsum("jic,jid->cd", z_norm, grad_gate, preferred_element_type=jnp.float32)
+    grad_z_gate = jnp.einsum("jid,cd->jic", grad_gate, w_gate, preferred_element_type=jnp.float32)
+
+    grad_ch, mixed, grad_z_gate, grad_w_gate, grad_w_out = lax.optimization_barrier(
+        (grad_ch, mixed, grad_z_gate, grad_w_gate, grad_w_out)
+    )
     grad_parts = triangle_back(pair_ch, grad_ch, rows_n, cols_n)
-    grad_tiles = exchange(grad_parts.reshape(hidden_width, 2, col_len, row_len)).astype(jnp.float32)
-    grad_left = grad_tiles[:, 0]
-    grad_right = grad_tiles[:, 1]
-    d_left_lin = grad_left * left_sig * flipped
-    d_left_pre = grad_left * left_lin * flipped * left_sig * (1.0 - left_sig)
-    d_right_lin = grad_right * right_sig * flipped
-    d_right_pre = grad_right * right_lin * flipped * right_sig * (1.0 - right_sig)
-    grad_proj_in = jnp.concatenate([d_left_lin, d_left_pre, d_right_lin, d_right_pre], 0).astype(
-        jnp.bfloat16
-    )
-    grad_z_norm = jnp.einsum("qji,cq->ijc", grad_proj_in, w_tri, preferred_element_type=jnp.float32)
-    grad_z_norm = grad_z_norm + jnp.einsum(
-        "ijd,cd->ijc", grad_gate, w_gate, preferred_element_type=jnp.float32
-    )
-    grad_w_tri = jnp.einsum("ijc,qji->cq", z_norm, grad_proj_in, preferred_element_type=jnp.float32)
-    grad_w_gate = jnp.einsum("ijc,ijd->cd", z_norm, grad_gate, preferred_element_type=jnp.float32)
-    grad_pair = normalize_back(grad_z_norm * gain_in, z_hat, z_inverse, -1).astype(jnp.bfloat16)
+    grad_tiles = exchange(grad_parts.reshape(hidden_width, 2, col_len, row_len))
+    grad_proj_in = (grad_tiles.astype(jnp.float32) * factors.astype(jnp.float32)).astype(jnp.bfloat16)
+    grad_proj_in = grad_proj_in.reshape(4 * hidden_width, col_len, row_len)
+    grad_w_tri = jnp.einsum("jic,qji->cq", z_norm, grad_proj_in, preferred_element_type=jnp.float32)
     totals = total_over_all(jnp.concatenate([grad_w_tri, grad_w_gate, grad_w_out], 1)) / N
-    grad_w_in = totals[:, : weight_in.shape[1]]
+    grad_w_tri = totals[:, : 4 * hidden_width].reshape(width, 2, hidden_width, 2)
+    grad_w_tri = grad_w_tri.transpose(0, 3, 1, 2).reshape(width, 4 * hidden_width)
+    grad_w_in = jnp.concatenate(
+        [grad_w_tri, totals[:, 4 * hidden_width : weight_in.shape[1]]], 1
+    )
     grad_w_out = totals[:, weight_in.shape[1] :]
     grad_g_in = jnp.sum(grad_w_in * weight_in.astype(jnp.float32), axis=1) / gain_in
     grad_g_out = jnp.sum(grad_w_out * weight_out.astype(jnp.float32), axis=1) / gain_out
+
+    z_hat, z_inverse = normalize(jnp.swapaxes(pair_rep[0], 0, 1).astype(jnp.float32), -1)
+    grad_z_norm = grad_z_gate + jnp.einsum(
+        "qji,cq->jic", grad_proj_in, w_tri, preferred_element_type=jnp.float32
+    )
+    grad_pair = normalize_back(grad_z_norm * gain_in, z_hat, z_inverse, -1)
+    grad_pair = jnp.swapaxes(grad_pair.astype(jnp.bfloat16), 0, 1)
     return (mixed[None], grad_pair[None], grad_w_in, grad_w_out, grad_g_in, grad_g_out)
 
 

time: 312 us -> 325 us (1.042)
  blocking collectives: 92.6 us -> 36.9 us
  local copies, waits for them, and re-layouts: 21.5 us -> 45.5 us
  matrix products: 26 us -> 48.8 us
  other arithmetic: 32.8 us -> 53.5 us
  waiting for transfers between devices: 88.6 us -> 69.1 us
  Pallas kernels: 11.9 us -> 27.7 us
  starting transfers between devices: 33 us -> 37.9 us
    all_to_all x2 -> x1, blocking collectives: 92.6 us -> 36.9 us  [exchange(): return lax.all_to_all(tiles, TILE, split_axis=0, concat_axis=0, tiled=True)]
    dot_general x9, matrix products: 26 us -> 48.8 us  [the longest x1 12.9 us: on_device(): jnp.einsum('jic,qji->cq', z_norm, grad_proj_in, preferred_element_type=jn...]
    all_to_all x2 -> x3, waiting for transfers between devices: 72.6 us -> 52.9 us  [exchange(): return lax.all_to_all(tiles, TILE, split_axis=0, concat_axis=0, tiled=True)]
    pallas_call x0 -> x2, Pallas kernels: none -> 15.8 us  [the longest x1 9.86 us: project(): pl.pallas_call(project_kernel, grid=(col_len // block_len,), in_specs=[pl...]
    convert_element_type x1, local copies, waits for them, and re-layouts: 1.35 us -> 13.5 us  [on_device(): (grad_tiles.astype(jnp.float32) * factors.astype(jnp.float32)).astype(jnp...]
    div x0 -> x4, local copies, waits for them, and re-layouts: none -> 9 us  [the longest x1 8.72 us: on_device(): sig = jax.nn.sigmoid(projected[1])]
    slice x0 -> x3, local copies, waits for them, and re-layouts: none -> 8.74 us  [the longest x1 8.7 us: on_device(): projected[0] * flipped * sig * (1.0 - sig)]
    slice x0 -> x1, other arithmetic: none -> 6.92 us  [on_device(): projected[0] * flipped * sig * (1.0 - sig)]
  transfers between devices with their start and end apart: 4 -> 5, of which waited for: 4 -> 5; matrix products, arithmetic and copies ran while one was open for 6% -> 27% of each run, Pallas kernels for 0% -> 0%
where the time goes in v2:
time: 325 us; the launch traced here: 321 us
  waiting for transfers between devices  69.1 us (21%)
  other arithmetic  53.5 us (16%)
  matrix products  48.8 us (15%)
  local copies, waits for them, and re-layouts  45.5 us (14%)
  starting transfers between devices  37.9 us (12%)
  blocking collectives  36.9 us (11%)
  Pallas kernels  27.7 us (9%)
    all_to_all x3, waiting for transfers between devices, exchange(): return lax.all_to_all(tiles, TILE, split_axis=0, concat_axis=0, tiled=True)  52.9 us
    all_to_all x1, blocking collectives, exchange(): return lax.all_to_all(tiles, TILE, split_axis=0, concat_axis=0, tiled=True)  36.9 us
    all_to_all x3, starting transfers between devices, exchange(): return lax.all_to_all(tiles, TILE, split_axis=0, concat_axis=0, tiled=True)  22.7 us
    convert_element_type x1, local copies, waits for them, and re-layouts, on_device(): (grad_tiles.astype(jnp.float32) * factors.astype(jnp.float32)).astype(jnp...  13.5 us
    dot_general x1, matrix products, on_device(): jnp.einsum('jic,qji->cq', z_norm, grad_proj_in, preferred_element_type=jn...  12.9 us
    all_to_all x1, waiting for transfers between devices, total_over_all(): lax.all_to_all(pieces, ALL, split_axis=0, concat_axis=0, tiled=True)  12.1 us
    all_to_all x1, starting transfers between devices, total_over_all(): lax.all_to_all(pieces, ALL, split_axis=0, concat_axis=0, tiled=True)  10.9 us
    unnamed x37, local copies, waits for them, and re-layouts  10.5 us
  transfers between devices with their start and end apart: 5, of which 5 were waited for; matrix products, arithmetic and copies ran while one was open for 27% of the time, Pallas kernels for 0%

profile of v2, /device:TPU:1, one launch (start us, length us, event | category | flops | bytes accessed | tf_op | source)
XLA Modules:
  0.0 320.7 jit_solution(5334572993434570754)
XLA Ops:
  5.0 9.9 %project.1 = (bf16[128,2,64,128]{3,2,1,0:T(8,128)(2,1)}, bf16[64,128,128]{2,1,0:T(8,128)(2,1)}) custom-call(s32[3]{0:T(128)} %pad_add_fusion.scalar_ref, bf16[128,64,128]{2,1,0:T(8,128)(2,1)} %bitcast.126, bf16[512,128]{1,0:T(8,128)(2,1)} %bitcast.137, f32[1,128]{1,0:T(1,128)} %bitcast.143), custom_call_target="tpu_custom_call" | custom-call | tf_op jit(solution)/shard_map/project/pallas_call | solution.py:138
  14.9 10.2 %all-to-all-start = ((bf16[128,2,64,128]{3,2,1,0:T(8,128)(2,1)}), bf16[128,2,64,128]{3,2,1,0:T(8,128)(2,1)}, u32[]{:S(2)}, u32[]{:S(2)}) async-start(bf16[128,2,64,128]{3,2,1,0:T(8,128)(2,1)} %get-tuple-element.19), calls=%async_computation | async-start | bytes 8388608 | tf_op jit(solution)/shard_map/all_to_all | solution.py:31
  27.4 6.9 %fusion.52 = (f32[256,64,128]{0,2,1:T(8,128)}, f32[256,64,128]{0,2,1:T(8,128)}) fusion(f32[512,64,128]{0,2,1:T(8,128)S(1)} %convolution_bitcast_fusion), kind=kLoop, calls=%fused_computation.80 | loop fusion | flops 6291456 | bytes 33554432 | tf_op jit(solution)/shard_map/slice | solution.py:209
  34.4 8.7 %copy.89 = f32[256,64,128]{2,1,0:T(8,128)} copy(f32[256,64,128]{0,2,1:T(8,128)} %get-tuple-element.61) | data formatting | bytes 16777216 | tf_op jit(solution)/shard_map/div | solution.py:208
  43.1 8.7 %copy.90 = f32[256,64,128]{2,1,0:T(8,128)} copy(f32[256,64,128]{0,2,1:T(8,128)} %get-tuple-element.60) | data formatting | bytes 16777216 | tf_op jit(solution)/shard_map/slice | solution.py:209
  53.2 6.8 %fusion.22 = (bf16[64,128,128]{2,1,0:T(8,128)(2,1)S(1)}, f32[64,128,128]{2,1,0:T(8,128)}) fusion(bf16[1,128,64,128]{3,2,1,0:T(8,128)(2,1)} %param.8, f32[64,128]{1,0:T(8,128)S(1)} %and_convert_fusion, bf16[64,128,128]{2,1,0:T(8,128)(2,1)S(1)} %copy-done.2, bf16[128,640]{1,0:T(8,128)(2,1)} %param.10), kind=kOutput, calls=%fused_computation.34 | convolution fusion | flops 275775488 | bytes 10551296 | tf_op jit(solution)/shard_map/jic,cd->jid/dot_general | solution.py:211
  62.1 4.6 %fusion.50 = (f32[64,128]{1,0:T(8,128)S(1)}, f32[128,64,128]{2,1,0:T(8,128)}) fusion(f32[128]{0:T(128)S(1)} %copy-done.10, f32[64,128,128]{1,2,0:T(8,128)S(1)} %fusion.41), kind=kLoop, calls=%fused_computation.79 | loop fusion | flops 2088960 | bytes 8421888 | tf_op jit(solution)/shard_map/reduce_sum | solution.py:219
  71.3 6.2 %pad_maximum_fusion = bf16[2,128,2,64,128]{4,3,2,1,0:T(8,128)(2,1)} fusion(bf16[1,128,2,64,128]{4,3,2,1,0:T(8,128)(2,1)} %get-tuple-element.63, bf16[1,128,2,64,128]{4,3,2,1,0:T(8,128)(2,1)S(1)} %get-tuple-element.62), kind=kLoop, calls=%fused_computation.6 | loop fusion | flops 4194304 | bytes 16777216 | tf_op jit(solution)/shard_map/stack | solution.py:209
  78.2 5.2 %triangle_forward.1 = bf16[32,4,64,128]{3,2,1,0:T(8,128)(2,1)} custom-call(bf16[32,4,2,64,128]{4,3,2,1,0:T(8,128)(2,1)} %bitcast.10.pair_ref), custom_call_target="tpu_custom_call" | custom-call | tf_op jit(solution)/shard_map/triangle_forward/pallas_call | solution.py:75
  83.5 36.9 %all_to_all.35.outer_ref = bf16[128,64,128]{2,1,0:T(8,128)(2,1)} all-to-all(bf16[128,64,128]{2,1,0:T(8,128)(2,1)} %bitcast.135), channel_id=1, replica_groups=mesh['grp'=4,'row'=4,'col'=8] {'row','col'}, dimensions={0} | all-to-all | bytes 4194304 | tf_op jit(solution)/shard_map/all_to_all | solution.py:31
  120.4 5.9 %outer_grad.1 = bf16[128,64,128]{2,1,0:T(8,128)(2,1)} custom-call(bf16[128,64,128]{2,1,0:T(8,128)(2,1)} %all_to_all.35.outer_ref, f32[128,64,128]{2,1,0:T(8,128)} %get-tuple-element.22.back_ref, f32[64,128]{1,0:T(8,128)} %broadcast_multiply_fusion.4.mean_ref), custom_call_target="tpu_custom_call" | custom-call | tf_op jit(solution)/shard_map/outer_grad/pallas_call | solution.py:170
  126.3 4.9 %all-to-all-start.2 = ((bf16[128,64,128]{2,1,0:T(8,128)(2,1)}), bf16[128,64,128]{2,1,0:T(8,128)(2,1)}, u32[]{:S(2)}, u32[]{:S(2)}) async-start(bf16[128,64,128]{2,1,0:T(8,128)(2,1)} %outer_grad.1), calls=%async_computation.2 | async-start | bytes 4194304 | tf_op jit(solution)/shard_map/all_to_all | solution.py:31
  134.1 10.2 %fusion.25 = (bf16[64,128,128]{2,1,0:T(8,128)(2,1)S(1)}, bf16[128,64,128]{2,0,1:T(8,128)(2,1)}) fusion(f32[64,128,128]{2,1,0:T(8,128)S(1)} %copy-done.4, bf16[1,128,64,128]{3,2,1,0:T(8,128)(2,1)S(1)} %copy-done.7, bf16[128,128]{1,0:T(8,128)(2,1)S(1)} %copy-done.9, bf16[128,64,128]{2,1,0:T(8,128)(2,1)S(1)} %fusion.9), kind=kOutput, calls=%fused_computation.37 | convolution fusion | flops 276824064 | bytes 12615680 | tf_op jit(solution)/shard_map/hji,hc->jic/dot_general | solution.py:231
  150.7 8.1 %all-to-all-done.2 = bf16[128,64,128]{2,1,0:T(8,128)(2,1)} async-done(((bf16[128,64,128]{2,1,0:T(8,128)(2,1)}), bf16[128,64,128]{2,1,0:T(8,128)(2,1)}, u32[]{:S(2)}, u32[]{:S(2)}) %all-to-all-start.2) | async-done | bytes 2097184 | tf_op jit(solution)/shard_map/all_to_all | solution.py:31
  158.8 6.7 %triangle_backward.1 = bf16[32,4,2,64,128]{4,3,2,1,0:T(8,128)(2,1)} custom-call(bf16[32,4,2,64,128]{4,3,2,1,0:T(8,128)(2,1)} %bitcast.10.pair_ref, bf16[32,4,64,128]{3,2,1,0:T(8,128)(2,1)} %bitcast.22.grad_ref), custom_call_target="tpu_custom_call" | custom-call | tf_op jit(solution)/shard_map/triangle_backward/pallas_call | solution.py:89
  165.5 7.6 %all-to-all-start.3 = ((bf16[128,2,64,128]{3,2,1,0:T(8,128)(2,1)}), bf16[128,2,64,128]{3,2,1,0:T(8,128)(2,1)}, u32[]{:S(2)}, u32[]{:S(2)}) async-start(bf16[128,2,64,128]{3,2,1,0:T(8,128)(2,1)} %bitcast.134), calls=%async_computation.3 | async-start | bytes 8388608 | tf_op jit(solution)/shard_map/all_to_all | solution.py:31
  181.9 44.0 %all-to-all-done.3 = bf16[128,2,64,128]{3,2,1,0:T(8,128)(2,1)} async-done(((bf16[128,2,64,128]{3,2,1,0:T(8,128)(2,1)}), bf16[128,2,64,128]{3,2,1,0:T(8,128)(2,1)}, u32[]{:S(2)}, u32[]{:S(2)}) %all-to-all-start.3) | async-done | bytes 4194336 | tf_op jit(solution)/shard_map/all_to_all | solution.py:31
  229.2 8.7 %multiply_convert_fusion = bf16[2,128,2,64,128]{4,3,2,1,0:T(8,128)(2,1)} fusion(bf16[2,128,2,64,128]{4,3,2,1,0:T(8,128)(2,1)} %pad_maximum_fusion, f32[128,2,64,128]{3,2,1,0:T(8,128)S(1)} %convert_element_type.71), kind=kLoop, calls=%fused_computation | loop fusion | flops 12582912 | bytes 25165824 | tf_op jit(solution)/shard_map/convert_element_type | solution.py:243
  237.9 13.5 %copy.119 = bf16[2,128,2,64,128]{1,3,2,0,4:T(8,128)(2,1)} copy(bf16[2,128,2,64,128]{4,3,2,1,0:T(8,128)(2,1)} %multiply_convert_fusion) | data formatting | bytes 16777216 | tf_op jit(solution)/shard_map/convert_element_type | solution.py:243
  251.4 10.2 %fusion.49 = (f32[64,128]{0,1:T(8,128)S(1)}, f32[64,128]{0,1:T(8,128)S(1)}, f32[64,128,128]{2,0,1:T(8,128)}) fusion(f32[64,128]{0,1:T(8,128)S(1)} %copy.99, f32[64,128]{0,1:T(8,128)S(1)} %copy.97, bf16[1,128,64,128]{3,2,1,0:T(8,128)(2,1)S(1)} %copy-done.1, f32[128]{0:T(128)S(1)} %copy-done.11, bf16[2,128,2,64,128]{1,3,2,0,4:T(8,128)(2,1)} %copy.119, ...), kind=kOutput, calls=%fused_computation.78 | convolution fusion | flops 1082114048 | bytes 19137024 | tf_op jit(solution)/shard_map/qji,cq->jic/dot_general | solution.py:257
  261.7 12.9 %fusion.33 = f32[128,512]{1,0:T(8,128)S(1)} fusion(bf16[64,128,128]{2,1,0:T(8,128)(2,1)} %get-tuple-element.20, bf16[512,64,128]{2,1,0:T(8,128)(2,1)} %bitcast.127), kind=kOutput, calls=%fused_computation.48 | convolution fusion | flops 1073741824 | bytes 10747904 | tf_op jit(solution)/shard_map/jic,qji->cq/dot_general | solution.py:245
  275.8 10.9 %all-to-all-start.4 = ((f32[128,1,768]{2,1,0:T(1,128)}), f32[128,1,768]{2,1,0:T(1,128)S(1)}, u32[]{:S(2)}, u32[]{:S(2)}) async-start(f32[128,1,768]{2,1,0:T(1,128)} %copy.109), calls=%async_computation.4 | async-start | bytes 786432 | tf_op jit(solution)/shard_map/all_to_all | solution.py:107
  287.0 12.1 %all-to-all-done.4 = f32[128,1,768]{2,1,0:T(1,128)S(1)} async-done(((f32[128,1,768]{2,1,0:T(1,128)}), f32[128,1,768]{2,1,0:T(1,128)S(1)}, u32[]{:S(2)}, u32[]{:S(2)}) %all-to-all-start.4) | async-done | bytes 393248 | tf_op jit(solution)/shard_map/all_to_all | solution.py:107
  304.8 8.4 %fusion.28 = bf16[1,128,64,128]{3,2,1,0:T(8,128)(2,1)} fusion(f32[64,128,128]{2,0,1:T(8,128)} %get-tuple-element.73, f32[64,128]{0,1:T(8,128)S(1)} %copy.106, f32[64,128]{0,1:T(8,128)S(1)} %copy.104, f32[64,128]{0,1:T(8,128)S(1)} %copy.99, f32[64,128]{0,1:T(8,128)S(1)} %copy.97, bf16[1,128,64,128]{3,2,1,0:T(8,128)(2,1)S(1)} %copy-done.1), kind=kLoop, calls=%fused_computation.43 | loop fusion | flops 8388608 | bytes 8519680 | tf_op jit(solution)/shard_map/broadcast_in_dim | solution.py:262
  (89 shorter events, 51.2 us)
Async XLA Ops:
  14.9 10.2 %copy-start.2 = (bf16[64,128,128]{2,1,0:T(8,128)(2,1)S(1)}, bf16[64,128,128]{2,1,0:T(8,128)(2,1)}, u32[]{:S(2)}) copy-start(bf16[64,128,128]{2,1,0:T(8,128)(2,1)} %get-tuple-element.20) | copy-start | bytes 6291460
  14.9 10.2 %copy-start.8 = (bf16[128,2,128,2]{0,3,2,1:T(2,128)(2,1)S(1)}, bf16[128,2,128,2]{0,3,2,1:T(2,128)(2,1)}, u32[]{:S(2)}) copy-start(bf16[128,2,128,2]{0,3,2,1:T(2,128)(2,1)} %copy.87) | copy-start | bytes 393220
  14.9 63.3 %all-to-all-start = ((bf16[128,2,64,128]{3,2,1,0:T(8,128)(2,1)}), bf16[128,2,64,128]{3,2,1,0:T(8,128)(2,1)}, u32[]{:S(2)}, u32[]{:S(2)}) async-start(bf16[128,2,64,128]{3,2,1,0:T(8,128)(2,1)} %get-tuple-element.19), calls=%async_computation | async-start | bytes 8388608 | tf_op jit(solution)/shard_map/all_to_all | solution.py:31
  53.1 14.2 %slice-start = ((s8[8388608]{0:T(1024)(128)(4,1)}), s8[4194304]{0:T(1024)(128)(4,1)S(1)}, s32[]{:S(2)}) async-start(s8[8388608]{0:T(1024)(128)(4,1)} %bitcast.128), calls=%async_computation.6 | async-start | bytes 8388608
  53.1 14.2 %slice-start.2 = ((s8[8388608]{0:T(1024)(128)(4,1)}), s8[4194304]{0:T(1024)(128)(4,1)S(1)}, s32[]{:S(2)}) async-start(s8[8388608]{0:T(1024)(128)(4,1)} %bitcast.131), calls=%async_computation.8 | async-start | bytes 8388608
  53.2 8.2 %copy-start.9 = (bf16[128,128]{1,0:T(8,128)(2,1)S(1)}, bf16[128,128]{1,0:T(8,128)(2,1)}, u32[]{:S(2)}) copy-start(bf16[128,128]{1,0:T(8,128)(2,1)} %param.11) | copy-start | bytes 98308
  53.2 14.1 %slice-start.1 = ((s8[8388608]{0:T(1024)(128)(4,1)}), s8[4194304]{0:T(1024)(128)(4,1)S(1)}, s32[]{:S(2)}) async-start(s8[8388608]{0:T(1024)(128)(4,1)} %bitcast.128), calls=%async_computation.7 | async-start | bytes 8388608
  53.2 14.1 %slice-start.3 = ((s8[8388608]{0:T(1024)(128)(4,1)}), s8[4194304]{0:T(1024)(128)(4,1)S(1)}, s32[]{:S(2)}) async-start(s8[8388608]{0:T(1024)(128)(4,1)} %bitcast.131), calls=%async_computation.9 | async-start | bytes 8388608
  60.1 1.3 copy-start.5
  60.1 2.1 copy-start.10
  126.3 4.9 %copy-start = (bf16[128,64,128]{2,1,0:T(8,128)(2,1)S(1)}, bf16[128,64,128]{2,1,0:T(8,128)(2,1)}, u32[]{:S(2)}) copy-start(bf16[128,64,128]{2,1,0:T(8,128)(2,1)} %all_to_all.35.outer_ref) | copy-start | bytes 6291460
  126.3 32.5 %all-to-all-start.2 = ((bf16[128,64,128]{2,1,0:T(8,128)(2,1)}), bf16[128,64,128]{2,1,0:T(8,128)(2,1)}, u32[]{:S(2)}, u32[]{:S(2)}) async-start(bf16[128,64,128]{2,1,0:T(8,128)(2,1)} %outer_grad.1), calls=%async_computation.2 | async-start | bytes 4194304 | tf_op jit(solution)/shard_map/all_to_all | solution.py:31
  131.2 2.2 copy-start.4
  131.2 2.9 copy-start.7
  134.1 10.2 %copy-start.3 = (bf16[64,128,128]{2,1,0:T(8,128)(2,1)S(1)}, bf16[64,128,128]{2,1,0:T(8,128)(2,1)}, u32[]{:S(2)}) copy-start(bf16[64,128,128]{2,1,0:T(8,128)(2,1)} %get-tuple-element.20) | copy-start | bytes 6291460
  144.2 1.6 copy-start.6
  165.5 7.8 %copy-start.1 = (bf16[1,128,64,128]{3,2,1,0:T(8,128)(2,1)S(1)}, bf16[1,128,64,128]{3,2,1,0:T(8,128)(2,1)}, u32[]{:S(2)}) copy-start(bf16[1,128,64,128]{3,2,1,0:T(8,128)(2,1)} %param.7) | copy-start | bytes 6291460
  165.5 60.5 %all-to-all-start.3 = ((bf16[128,2,64,128]{3,2,1,0:T(8,128)(2,1)}), bf16[128,2,64,128]{3,2,1,0:T(8,128)(2,1)}, u32[]{:S(2)}, u32[]{:S(2)}) async-start(bf16[128,2,64,128]{3,2,1,0:T(8,128)(2,1)} %bitcast.134), calls=%async_computation.3 | async-start | bytes 8388608 | tf_op jit(solution)/shard_map/all_to_all | solution.py:31
  237.9 13.5 %copy-start.11 = (f32[128]{0:T(128)S(1)}, f32[128]{0:T(128)}, u32[]{:S(2)}) copy-start(f32[128]{0:T(128)} %param.12) | copy-start | bytes 1540
  275.8 23.3 %all-to-all-start.4 = ((f32[128,1,768]{2,1,0:T(1,128)}), f32[128,1,768]{2,1,0:T(1,128)S(1)}, u32[]{:S(2)}, u32[]{:S(2)}) async-start(f32[128,1,768]{2,1,0:T(1,128)} %copy.109), calls=%async_computation.4 | async-start | bytes 786432 | tf_op jit(solution)/shard_map/all_to_all | solution.py:107
  300.4 16.8 %all-to-all-start.5 = ((f32[128,1,768]{2,1,0:T(1,128)}), f32[128,1,768]{2,1,0:T(1,128)S(1)}, u32[]{:S(2)}, u32[]{:S(2)}) async-start(f32[128,1,768]{2,1,0:T(1,128)} %broadcast_in_dim.16), calls=%async_computation.5 | async-start | bytes 786432 | tf_op jit(solution)/shard_map/all_to_all | solution.py:110

commit v3 on v2

--- a/solution.py
+++ b/solution.py
@@ -102,46 +102,67 @@
 
 def total_over_all(values):
     devices = lax.axis_size(ALL)
-    width = values.shape[1]
-    pieces = values.reshape(devices, -1)
+    pieces = values.reshape(devices, -1, values.shape[1])
     arrived = lax.all_to_all(pieces, ALL, split_axis=0, concat_axis=0, tiled=True)
-    own = jnp.sum(arrived, axis=0, keepdims=True)
-    spread = jnp.broadcast_to(own, pieces.shape)
-    return lax.all_to_all(spread, ALL, split_axis=0, concat_axis=0, tiled=True).reshape(-1, width)
-
-
-def project_kernel(scalar_ref, pair_ref, weight_ref, gain_ref, tile_ref, norm_ref):
-    block = pl.program_id(0)
+    spread = jnp.broadcast_to(jnp.sum(arrived, axis=0, keepdims=True), pieces.shape)
+    return lax.all_to_all(spread, ALL, split_axis=0, concat_axis=0, tiled=True).reshape(values.shape)
+
+
+def layer_norm(values):
+    centred = values - jnp.mean(values, axis=-1, keepdims=True)
+    inverse = lax.rsqrt(jnp.mean(centred * centred, axis=-1, keepdims=True) + epsilon)
+    return centred * inverse, inverse
+
+
+def tile_inside(lengths_ref, row_len, block_len):
+    length = lengths_ref[lax.axis_index("grp")]
+    row_start = lax.axis_index("row") * row_len
+    col_start = (lax.axis_index("col") * pl.num_programs(0) + pl.program_id(0)) * block_len
+    row_in = row_start + lax.broadcasted_iota(jnp.int32, (1, row_len), 1) < length
+    return [
+        jnp.where(row_in & (col_start + j < length), 1.0, 0.0).astype(jnp.float32)
+        for j in range(block_len)
+    ]
+
+
+def project_kernel(lengths_ref, pair_ref, weight_ref, gain_ref, tile_ref, norm_ref, rows_ref):
     row_len, block_len, _ = pair_ref.shape
-    channels = weight_ref.shape[0] // 2
-    values = jnp.swapaxes(pair_ref[...].astype(jnp.float32), 0, 1)
-    normed, _ = normalize(values, -1)
+    hidden_width = tile_ref.shape[0]
+
+    @pl.when(pl.program_id(0) == 0)
+    def _():
+        for at, source in enumerate((0, 2, 1, 3)):
+            part = weight_ref[:, source * hidden_width : (source + 1) * hidden_width]
+            rows_ref[at * hidden_width : (at + 1) * hidden_width] = part.astype(jnp.float32).T.astype(
+                jnp.bfloat16
+            )
+
+    normed, _ = layer_norm(jnp.swapaxes(pair_ref[...].astype(jnp.float32), 0, 1))
     normed = (normed * gain_ref[...]).astype(jnp.bfloat16)
     norm_ref[...] = normed
-    length, row_start, col_start = scalar_ref[0], scalar_ref[1], scalar_ref[2]
-    row_in = row_start + lax.broadcasted_iota(jnp.int32, (1, row_len), 1) < length
+    inside = tile_inside(lengths_ref, row_len, block_len)
     gated = []
     for j in range(block_len):
         projected = lax.dot_general(
-            weight_ref[...], normed[j], (((1,), (1,)), ((), ())), preferred_element_type=jnp.float32
+            rows_ref[...], normed[j], (((1,), (1,)), ((), ())), preferred_element_type=jnp.float32
         )
-        col_in = col_start + block * block_len + j < length
-        inside = jnp.where(row_in & col_in, 1.0, 0.0)
-        gated.append(projected[:channels] * jax.nn.sigmoid(projected[channels:]) * inside)
+        sig = jax.nn.sigmoid(projected[2 * hidden_width :])
+        gated.append(projected[: 2 * hidden_width] * sig * inside[j])
     gated = jnp.swapaxes(jnp.stack(gated, 0), 0, 1).astype(jnp.bfloat16)
-    tile_ref[...] = gated.reshape(tile_ref.shape)
-
-
-def project(scalars, pair_rep, weight_rows, gain, block_len=16):
+    tile_ref[:, 0] = gated[:hidden_width]
+    tile_ref[:, 1] = gated[hidden_width:]
+
+
+def project(lengths, pair_rep, weight_in, gain, block_len=16):
     row_len, col_len, width = pair_rep.shape
-    hidden_width = weight_rows.shape[0] // 4
+    hidden_width = (weight_in.shape[1] - width) // 4
     return pl.pallas_call(
         project_kernel,
         grid=(col_len // block_len,),
         in_specs=[
             pl.BlockSpec(memory_space=pltpu.SMEM),
             pl.BlockSpec((row_len, block_len, width), lambda j: (0, j, 0)),
-            pl.BlockSpec(weight_rows.shape, lambda j: (0, 0)),
+            pl.BlockSpec(weight_in.shape, lambda j: (0, 0)),
             pl.BlockSpec((1, width), lambda j: (0, 0)),
         ],
         out_specs=[
@@ -152,8 +173,148 @@
             jax.ShapeDtypeStruct((hidden_width, 2, col_len, row_len), jnp.bfloat16),
             jax.ShapeDtypeStruct((col_len, row_len, width), jnp.bfloat16),
         ],
+        scratch_shapes=[pltpu.VMEM((4 * hidden_width, width), jnp.bfloat16)],
         name="project",
-    )(scalars, pair_rep, weight_rows, gain[None])
+    )(lengths, pair_rep, weight_in, gain[None])
+
+
+def factors_kernel(lengths_ref, norm_ref, weight_ref, factor_ref):
+    block_len, row_len, _ = norm_ref.shape
+    half = weight_ref.shape[0] // 2
+    inside = tile_inside(lengths_ref, row_len, block_len)
+    for j in range(block_len):
+        projected = lax.dot_general(
+            weight_ref[...], norm_ref[j], (((1,), (1,)), ((), ())), preferred_element_type=jnp.float32
+        )
+        sig = jax.nn.sigmoid(projected[half:])
+        kept = sig * inside[j]
+        factor_ref[j, :half] = kept.astype(jnp.bfloat16)
+        factor_ref[j, half:] = (projected[:half] * kept * (1.0 - sig)).astype(jnp.bfloat16)
+
+
+def gate_factors(lengths, z_norm, weight_rows, block_len=16):
+    col_len, row_len, width = z_norm.shape
+    return pl.pallas_call(
+        factors_kernel,
+        grid=(col_len // block_len,),
+        in_specs=[
+            pl.BlockSpec(memory_space=pltpu.SMEM),
+            pl.BlockSpec((block_len, row_len, width), lambda j: (j, 0, 0)),
+            pl.BlockSpec(weight_rows.shape, lambda j: (0, 0)),
+        ],
+        out_specs=pl.BlockSpec((block_len, weight_rows.shape[0], row_len), lambda j: (j, 0, 0)),
+        out_shape=jax.ShapeDtypeStruct((col_len, weight_rows.shape[0], row_len), jnp.bfloat16),
+        name="gate_factors",
+    )(lengths, z_norm, weight_rows)
+
+
+def projection_grads(grad_ref, factor_ref):
+    hidden_width, _, block_len, row_len = grad_ref.shape
+    grads = grad_ref[...].astype(jnp.float32).reshape(2 * hidden_width, block_len, row_len)
+    grads = jnp.swapaxes(grads, 0, 1)
+    return [
+        jnp.concatenate(
+            [
+                (grads[j] * factor_ref[j, : 2 * hidden_width].astype(jnp.float32)),
+                (grads[j] * factor_ref[j, 2 * hidden_width :].astype(jnp.float32)),
+            ],
+            0,
+        ).astype(jnp.bfloat16)
+        for j in range(block_len)
+    ]
+
+
+def weight_sums_kernel(grad_ref, factor_ref, norm_ref, gate_ref, out_ref, sum_ref, total_ref):
+    hidden_width, _, block_len, row_len = grad_ref.shape
+    width = norm_ref.shape[2]
+    step = pl.program_id(0)
+    grads = jnp.concatenate(projection_grads(grad_ref, factor_ref), 1)
+    partial = jnp.dot(
+        grads,
+        norm_ref[...].reshape(block_len * row_len, width),
+        preferred_element_type=jnp.float32,
+    )
+
+    @pl.when(step == 0)
+    def _():
+        total_ref[...] = partial
+
+    @pl.when(step > 0)
+    def _():
+        total_ref[...] += partial
+
+    @pl.when(step == pl.num_programs(0) - 1)
+    def _():
+        for side in range(2):
+            for kind in range(2):
+                rows = total_ref[
+                    pl.ds(kind * 2 * hidden_width + side, hidden_width, stride=2), :
+                ]
+                at = (2 * side + kind) * width
+                sum_ref[at : at + width] = rows.T
+        sum_ref[4 * width : 5 * width] = gate_ref[...]
+        sum_ref[5 * width : 6 * width] = out_ref[...]
+        sum_ref[6 * width :] = jnp.zeros((2 * width, width), jnp.float32)
+
+
+def weight_sums(grad_tiles, factors, z_norm, grad_w_gate, grad_w_out, block_len=16):
+    hidden_width, _, col_len, row_len = grad_tiles.shape
+    width = z_norm.shape[2]
+    square = pl.BlockSpec((width, width), lambda j: (0, 0))
+    return pl.pallas_call(
+        weight_sums_kernel,
+        grid=(col_len // block_len,),
+        in_specs=[
+            pl.BlockSpec((hidden_width, 2, block_len, row_len), lambda j: (0, 0, j, 0)),
+            pl.BlockSpec((block_len, 4 * hidden_width, row_len), lambda j: (j, 0, 0)),
+            pl.BlockSpec((block_len, row_len, width), lambda j: (j, 0, 0)),
+            square,
+            square,
+        ],
+        out_specs=pl.BlockSpec((8 * width, width), lambda j: (0, 0)),
+        out_shape=jax.ShapeDtypeStruct((8 * width, width), jnp.float32),
+        scratch_shapes=[pltpu.VMEM((4 * hidden_width, width), jnp.float32)],
+        name="weight_sums",
+    )(grad_tiles, factors, z_norm, grad_w_gate, grad_w_out)
+
+
+def pair_grad_kernel(
+    pair_ref, grad_ref, factor_ref, gate_ref, weight_ref, w_gate_ref, gain_ref, out_ref
+):
+    block_len = pair_ref.shape[1]
+    z_hat, z_inverse = layer_norm(jnp.swapaxes(pair_ref[...].astype(jnp.float32), 0, 1))
+    grads = projection_grads(grad_ref, factor_ref)
+    grad_norm = []
+    for j in range(block_len):
+        total = jnp.dot(weight_ref[...], grads[j], preferred_element_type=jnp.float32)
+        total += lax.dot_general(
+            w_gate_ref[...], gate_ref[j], (((1,), (1,)), ((), ())), preferred_element_type=jnp.float32
+        )
+        grad_norm.append(total.T)
+    grad_hat = jnp.stack(grad_norm, 0) * gain_ref[...]
+    grad_pair = normalize_back(grad_hat, z_hat, z_inverse, -1)
+    out_ref[...] = jnp.swapaxes(grad_pair, 0, 1).astype(jnp.bfloat16)
+
+
+def pair_grad(pair_rep, grad_tiles, factors, grad_gate, w_tri, w_gate, gain, block_len=16):
+    row_len, col_len, width = pair_rep.shape
+    hidden_width = grad_tiles.shape[0]
+    return pl.pallas_call(
+        pair_grad_kernel,
+        grid=(col_len // block_len,),
+        in_specs=[
+            pl.BlockSpec((row_len, block_len, width), lambda j: (0, j, 0)),
+            pl.BlockSpec((hidden_width, 2, block_len, row_len), lambda j: (0, 0, j, 0)),
+            pl.BlockSpec((block_len, 4 * hidden_width, row_len), lambda j: (j, 0, 0)),
+            pl.BlockSpec((block_len, row_len, width), lambda j: (j, 0, 0)),
+            pl.BlockSpec(w_tri.shape, lambda j: (0, 0)),
+            pl.BlockSpec(w_gate.shape, lambda j: (0, 0)),
+            pl.BlockSpec((1, width), lambda j: (0, 0)),
+        ],
+        out_specs=pl.BlockSpec((row_len, block_len, width), lambda j: (0, j, 0)),
+        out_shape=jax.ShapeDtypeStruct(pair_rep.shape, jnp.bfloat16),
+        name="pair_grad",
+    )(pair_rep, grad_tiles, factors, grad_gate, w_tri, w_gate, gain[None])
 
 
 def outer_grad_kernel(outer_ref, back_ref, mean_ref, grad_ref):
@@ -189,25 +350,17 @@
     share = hidden_width // devices
     lookup = jnp.arange(groups) == lax.axis_index("grp")
     own_length = jnp.sum(jnp.where(lookup, lengths, 0))
-    row_start = lax.axis_index("row") * row_len
-    col_start = lax.axis_index("col") * col_len
-    scalars = jnp.stack([own_length, row_start, col_start]).astype(jnp.int32)
-    row_in = row_start + jnp.arange(row_len) < own_length
-    col_in = col_start + jnp.arange(col_len) < own_length
-    flipped = (col_in[:, None] & row_in[None, :]).astype(jnp.float32)
-    flipped_c = flipped[:, :, None]
+    row_in = lax.axis_index("row") * row_len + jnp.arange(row_len) < own_length
+    col_in = lax.axis_index("col") * col_len + jnp.arange(col_len) < own_length
+    flipped_c = (col_in[:, None] & row_in[None, :]).astype(jnp.float32)[:, :, None]
     w_gate = weight_in[:, 4 * hidden_width :]
+
+    pair_tiles, z_norm = project(lengths, pair_rep[0], weight_in, gain_in)
+    pair_ch = exchange(pair_tiles).reshape(devices, share, 2, col_len, row_len)
+
     w_tri = weight_in[:, : 4 * hidden_width].reshape(width, 2, 2, hidden_width)
     w_tri = w_tri.transpose(0, 2, 3, 1).reshape(width, 4 * hidden_width)
-
-    pair_tiles, z_norm = project(scalars, pair_rep[0], w_tri.T, gain_in)
-    pair_ch = exchange(pair_tiles).reshape(devices, share, 2, col_len, row_len)
-
-    projected = jnp.einsum("jic,cq->qji", z_norm, w_tri, preferred_element_type=jnp.float32)
-    projected = projected.reshape(2, hidden_width, 2, col_len, row_len)
-    sig = jax.nn.sigmoid(projected[1])
-    factors = jnp.stack([sig * flipped, projected[0] * flipped * sig * (1.0 - sig)], 0)
-    factors = factors.astype(jnp.bfloat16)
+    factors = gate_factors(lengths, z_norm, w_tri.T)
     gate_pre = jnp.einsum("jic,cd->jid", z_norm, w_gate, preferred_element_type=jnp.float32)
     gate = jax.nn.sigmoid(gate_pre) * flipped_c
     grad_out = jnp.swapaxes(cotangent[0], 0, 1).astype(jnp.float32)
@@ -233,32 +386,19 @@
     grad_gate = (grad_out * proj_out * gate * (1.0 - gate)).astype(jnp.bfloat16)
     grad_w_out = jnp.einsum("hji,jic->hc", o_norm, grad_proj, preferred_element_type=jnp.float32)
     grad_w_gate = jnp.einsum("jic,jid->cd", z_norm, grad_gate, preferred_element_type=jnp.float32)
-    grad_z_gate = jnp.einsum("jid,cd->jic", grad_gate, w_gate, preferred_element_type=jnp.float32)
-
-    grad_ch, mixed, grad_z_gate, grad_w_gate, grad_w_out = lax.optimization_barrier(
-        (grad_ch, mixed, grad_z_gate, grad_w_gate, grad_w_out)
+
+    grad_ch, mixed, grad_gate, grad_w_gate, grad_w_out = lax.optimization_barrier(
+        (grad_ch, mixed, grad_gate, grad_w_gate, grad_w_out)
     )
     grad_parts = triangle_back(pair_ch, grad_ch, rows_n, cols_n)
     grad_tiles = exchange(grad_parts.reshape(hidden_width, 2, col_len, row_len))
-    grad_proj_in = (grad_tiles.astype(jnp.float32) * factors.astype(jnp.float32)).astype(jnp.bfloat16)
-    grad_proj_in = grad_proj_in.reshape(4 * hidden_width, col_len, row_len)
-    grad_w_tri = jnp.einsum("jic,qji->cq", z_norm, grad_proj_in, preferred_element_type=jnp.float32)
-    totals = total_over_all(jnp.concatenate([grad_w_tri, grad_w_gate, grad_w_out], 1)) / N
-    grad_w_tri = totals[:, : 4 * hidden_width].reshape(width, 2, hidden_width, 2)
-    grad_w_tri = grad_w_tri.transpose(0, 3, 1, 2).reshape(width, 4 * hidden_width)
-    grad_w_in = jnp.concatenate(
-        [grad_w_tri, totals[:, 4 * hidden_width : weight_in.shape[1]]], 1
-    )
-    grad_w_out = totals[:, weight_in.shape[1] :]
+    sums = weight_sums(grad_tiles, factors, z_norm, grad_w_gate, grad_w_out)
+    totals = total_over_all(sums).reshape(8, width, width) / N
+    grad_w_in = jnp.concatenate([totals[block] for block in range(5)], 1)
+    grad_w_out = totals[5]
     grad_g_in = jnp.sum(grad_w_in * weight_in.astype(jnp.float32), axis=1) / gain_in
     grad_g_out = jnp.sum(grad_w_out * weight_out.astype(jnp.float32), axis=1) / gain_out
-
-    z_hat, z_inverse = normalize(jnp.swapaxes(pair_rep[0], 0, 1).astype(jnp.float32), -1)
-    grad_z_norm = grad_z_gate + jnp.einsum(
-        "qji,cq->jic", grad_proj_in, w_tri, preferred_element_type=jnp.float32
-    )
-    grad_pair = normalize_back(grad_z_norm * gain_in, z_hat, z_inverse, -1)
-    grad_pair = jnp.swapaxes(grad_pair.astype(jnp.bfloat16), 0, 1)
+    grad_pair = pair_grad(pair_rep[0], grad_tiles, factors, grad_gate, w_tri, w_gate, gain_in)
     return (mixed[None], grad_pair[None], grad_w_in, grad_w_out, grad_g_in, grad_g_out)
 
 

time: 325 us -> 275 us (0.85)
  blocking collectives: 36.9 us -> 115 us
  other arithmetic: 53.5 us -> 10.9 us
  local copies, waits for them, and re-layouts: 45.5 us -> 9.81 us
  Pallas kernels: 27.7 us -> 57.5 us
  waiting for transfers between devices: 69.1 us -> 39.9 us
  matrix products: 48.8 us -> 19.9 us
  starting transfers between devices: 37.9 us -> 19.3 us
    all_to_all x1 -> x2, blocking collectives: 36.9 us -> 94 us  [exchange(): return lax.all_to_all(tiles, TILE, split_axis=0, concat_axis=0, tiled=True)]
    pallas_call x0 -> x3, Pallas kernels: none -> 29.5 us  [the longest x1 14.2 us: pair_grad(): pl.pallas_call(pair_grad_kernel, grid=(col_len // block_len,), in_specs=[...]
    dot_general x4 -> x0, matrix products: 28.9 us -> none  [the longest x1 12.9 us: on_device(): jnp.einsum('jic,qji->cq', z_norm, grad_proj_in, preferred_element_type=jn...]
    all_to_all x0 -> x1, blocking collectives: none -> 21.3 us  [total_over_all(): lax.all_to_all(pieces, ALL, split_axis=0, concat_axis=0, tiled=True)]
    convert_element_type x1 -> x0, local copies, waits for them, and re-layouts: 13.5 us -> none  [on_device(): (grad_tiles.astype(jnp.float32) * factors.astype(jnp.float32)).astype(jnp...]
    all_to_all x3 -> x2, waiting for transfers between devices: 52.9 us -> 39.9 us  [exchange(): return lax.all_to_all(tiles, TILE, split_axis=0, concat_axis=0, tiled=True)]
    all_to_all x1 -> x0, waiting for transfers between devices: 12.1 us -> none  [total_over_all(): lax.all_to_all(pieces, ALL, split_axis=0, concat_axis=0, tiled=True)]
    convert_element_type x3 -> x1, other arithmetic: 12 us -> 0.08 us  [on_device(): (col_in[:, None] & row_in[None, :]).astype(jnp.float32)[:, :, None]]
  transfers between devices with their start and end apart: 5 -> 3, of which waited for: 5 -> 2; matrix products, arithmetic and copies ran while one was open for 27% -> 12% of each run, Pallas kernels for 0% -> 8%
where the time goes in v3:
time: 275 us; the launch traced here: 274 us
  blocking collectives  115 us (42%)
  Pallas kernels  57.5 us (21%)
  waiting for transfers between devices  39.9 us (15%)
  matrix products  19.9 us (7%)
  starting transfers between devices  19.3 us (7%)
  other arithmetic  10.9 us (4%)
  local copies, waits for them, and re-layouts  9.81 us (4%)
    all_to_all x2, blocking collectives, exchange(): return lax.all_to_all(tiles, TILE, split_axis=0, concat_axis=0, tiled=True)  94 us
    all_to_all x2, waiting for transfers between devices, exchange(): return lax.all_to_all(tiles, TILE, split_axis=0, concat_axis=0, tiled=True)  39.9 us
    all_to_all x1, blocking collectives, total_over_all(): lax.all_to_all(pieces, ALL, split_axis=0, concat_axis=0, tiled=True)  21.3 us
    all_to_all x2, starting transfers between devices, exchange(): return lax.all_to_all(tiles, TILE, split_axis=0, concat_axis=0, tiled=True)  15.1 us
    pallas_call x1, Pallas kernels, pair_grad(): pl.pallas_call(pair_grad_kernel, grid=(col_len // block_len,), in_specs=[...  14.2 us
    dot_general x1, matrix products, on_device(): jnp.einsum('hji,hc->jic', o_norm, weight_out, preferred_element_type=jnp....  10.1 us
    pallas_call x1, Pallas kernels, project(): pl.pallas_call(project_kernel, grid=(col_len // block_len,), in_specs=[pl...  10.1 us
    pallas_call x1, Pallas kernels, weight_sums(): pl.pallas_call(weight_sums_kernel, grid=(col_len // block_len,), in_specs...  8.47 us
  transfers between devices with their start and end apart: 3, of which 2 were waited for; matrix products, arithmetic and copies ran while one was open for 12% of the time, Pallas kernels for 8%

profile of v3, /device:TPU:1, one launch (start us, length us, event | category | flops | bytes accessed | tf_op | source)
XLA Modules:
  0.0 273.6 jit_solution(12041421855435043637)
XLA Ops:
  0.6 10.1 %project.1 = (bf16[128,2,64,128]{3,2,1,0:T(8,128)(2,1)}, bf16[64,128,128]{2,1,0:T(8,128)(2,1)}) custom-call(s32[4]{0:T(128)} %lengths_ref.3, bf16[128,64,128]{2,1,0:T(8,128)(2,1)} %bitcast.84, bf16[128,640]{1,0:T(8,128)(2,1)} %weight_ref.1, f32[1,128]{1,0:T(1,128)} %bitcast.90), custom_call_target="tpu_custom_call" | custom-call | tf_op jit(solution)/shard_map/project/pallas_call | solution.py:159
  10.7 10.0 %all-to-all-start = ((bf16[128,2,64,128]{3,2,1,0:T(8,128)(2,1)}), bf16[128,2,64,128]{3,2,1,0:T(8,128)(2,1)}, u32[]{:S(2)}, u32[]{:S(2)}) async-start(bf16[128,2,64,128]{3,2,1,0:T(8,128)(2,1)} %get-tuple-element.19), calls=%async_computation | async-start | bytes 8388608 | tf_op jit(solution)/shard_map/all_to_all | solution.py:31
  21.5 6.9 %gate_factors.1.factor_ref = bf16[64,512,128]{2,1,0:T(8,128)(2,1)} custom-call(s32[4]{0:T(128)} %lengths_ref.3, bf16[64,128,128]{2,1,0:T(8,128)(2,1)} %get-tuple-element.20.norm_ref, bf16[512,128]{1,0:T(8,128)(2,1)} %bitcast.88), custom_call_target="tpu_custom_call" | custom-call | tf_op jit(solution)/shard_map/gate_factors/pallas_call | solution.py:197
  30.5 5.6 %fusion.7 = (bf16[64,128,128]{2,1,0:T(8,128)(2,1)S(1)}, f32[64,128,128]{2,1,0:T(8,128)}) fusion(bf16[1,128,64,128]{3,2,1,0:T(8,128)(2,1)} %param.8, f32[64,128]{1,0:T(8,128)S(1)} %and_convert_fusion, bf16[64,128,128]{2,1,0:T(8,128)(2,1)S(1)} %copy-done.1, bf16[128,640]{1,0:T(8,128)(2,1)S(1)} %copy-done.9), kind=kOutput, calls=%fused_computation.10 | convolution fusion | flops 275775488 | bytes 10551296 | tf_op jit(solution)/shard_map/jic,cd->jid/dot_general | solution.py:364
  36.1 1.4 copy-done.6
  38.2 4.6 %fusion.31 = (f32[64,128]{1,0:T(8,128)S(1)}, f32[128,64,128]{2,1,0:T(8,128)}) fusion(f32[128]{0:T(128)S(1)} %copy-done.13, f32[64,128,128]{1,2,0:T(8,128)S(1)} %fusion.26), kind=kLoop, calls=%fused_computation.52 | loop fusion | flops 2088960 | bytes 8421888 | tf_op jit(solution)/shard_map/reduce_sum | solution.py:372
  43.4 30.5 %all-to-all-done = bf16[128,2,64,128]{3,2,1,0:T(8,128)(2,1)} async-done(((bf16[128,2,64,128]{3,2,1,0:T(8,128)(2,1)}), bf16[128,2,64,128]{3,2,1,0:T(8,128)(2,1)}, u32[]{:S(2)}, u32[]{:S(2)}) %all-to-all-start) | async-done | bytes 4194336 | tf_op jit(solution)/shard_map/all_to_all | solution.py:31
  73.9 5.2 %triangle_forward.1 = bf16[32,4,64,128]{3,2,1,0:T(8,128)(2,1)} custom-call(bf16[32,4,2,64,128]{4,3,2,1,0:T(8,128)(2,1)} %bitcast.2.pair_ref), custom_call_target="tpu_custom_call" | custom-call | tf_op jit(solution)/shard_map/triangle_forward/pallas_call | solution.py:75
  79.1 36.7 %all_to_all.30.outer_ref = bf16[128,64,128]{2,1,0:T(8,128)(2,1)} all-to-all(bf16[128,64,128]{2,1,0:T(8,128)(2,1)} %bitcast.82), channel_id=1, replica_groups=mesh['grp'=4,'row'=4,'col'=8] {'row','col'}, dimensions={0} | all-to-all | bytes 4194304 | tf_op jit(solution)/shard_map/all_to_all | solution.py:31
  115.8 5.9 %outer_grad.1 = bf16[128,64,128]{2,1,0:T(8,128)(2,1)} custom-call(bf16[128,64,128]{2,1,0:T(8,128)(2,1)} %all_to_all.30.outer_ref, f32[128,64,128]{2,1,0:T(8,128)} %get-tuple-element.22.back_ref, f32[64,128]{1,0:T(8,128)} %broadcast_multiply_fusion.2.mean_ref), custom_call_target="tpu_custom_call" | custom-call | tf_op jit(solution)/shard_map/outer_grad/pallas_call | solution.py:331
  121.7 5.1 %all-to-all-start.2 = ((bf16[128,64,128]{2,1,0:T(8,128)(2,1)}), bf16[128,64,128]{2,1,0:T(8,128)(2,1)}, u32[]{:S(2)}, u32[]{:S(2)}) async-start(bf16[128,64,128]{2,1,0:T(8,128)(2,1)} %outer_grad.1), calls=%async_computation.2 | async-start | bytes 4194304 | tf_op jit(solution)/shard_map/all_to_all | solution.py:31
  128.8 1.4 copy-done.5
  130.2 10.1 %fusion.10 = (bf16[64,128,128]{2,1,0:T(8,128)(2,1)S(1)}, bf16[128,64,128]{2,0,1:T(8,128)(2,1)}) fusion(f32[64,128,128]{2,1,0:T(8,128)S(1)} %copy-done.5, bf16[1,128,64,128]{3,2,1,0:T(8,128)(2,1)S(1)} %copy-done.8, bf16[128,128]{1,0:T(8,128)(2,1)S(1)} %copy-done.12, bf16[128,64,128]{2,1,0:T(8,128)(2,1)S(1)} %fusion.4), kind=kOutput, calls=%fused_computation.13 | convolution fusion | flops 276824064 | bytes 12615680 | tf_op jit(solution)/shard_map/hji,hc->jic/dot_general | solution.py:384
  140.3 1.4 convolution_bitcast_fusion.gate_ref
  141.7 1.0 copy-done.7
  142.7 2.1 fusion.17.out_ref
  144.8 9.4 %all-to-all-done.2 = bf16[128,64,128]{2,1,0:T(8,128)(2,1)} async-done(((bf16[128,64,128]{2,1,0:T(8,128)(2,1)}), bf16[128,64,128]{2,1,0:T(8,128)(2,1)}, u32[]{:S(2)}, u32[]{:S(2)}) %all-to-all-start.2) | async-done | bytes 2097184 | tf_op jit(solution)/shard_map/all_to_all | solution.py:31
  154.3 6.7 %triangle_backward.1 = bf16[32,4,2,64,128]{4,3,2,1,0:T(8,128)(2,1)} custom-call(bf16[32,4,2,64,128]{4,3,2,1,0:T(8,128)(2,1)} %bitcast.2.pair_ref, bf16[32,4,64,128]{3,2,1,0:T(8,128)(2,1)} %bitcast.12.grad_ref), custom_call_target="tpu_custom_call" | custom-call | tf_op jit(solution)/shard_map/triangle_backward/pallas_call | solution.py:89
  161.0 57.3 %all_to_all.31.grad_ref = bf16[128,2,64,128]{3,2,1,0:T(8,128)(2,1)} all-to-all(bf16[128,2,64,128]{3,2,1,0:T(8,128)(2,1)} %bitcast.81), channel_id=1, replica_groups=mesh['grp'=4,'row'=4,'col'=8] {'row','col'}, dimensions={0} | all-to-all | bytes 8388608 | tf_op jit(solution)/shard_map/all_to_all | solution.py:31
  218.3 8.5 %weight_sums.1 = f32[1024,128]{1,0:T(8,128)} custom-call(bf16[128,2,64,128]{3,2,1,0:T(8,128)(2,1)} %all_to_all.31.grad_ref, bf16[64,512,128]{2,1,0:T(8,128)(2,1)} %gate_factors.1.factor_ref, bf16[64,128,128]{2,1,0:T(8,128)(2,1)} %get-tuple-element.20.norm_ref, f32[128,128]{1,0:T(8,128)} %convolution_bitcast_fusion.gate_ref, f32[128,128]{1,0:T(8,128)} %fusion.17.out_ref), custom_call_target="tpu_custom_call" | custom-call | tf_op jit(solution)/shard_map/weight_sums/pallas_call | solution.py:264
  226.8 21.3 %all_to_all.32 = f32[128,8,128]{2,1,0:T(8,128)S(1)} all-to-all(f32[128,8,128]{2,1,0:T(8,128)} %bitcast.87), channel_id=1, replica_groups=mesh['grp'=4,'row'=4,'col'=8] {'grp','row','col'}, dimensions={0} | all-to-all | bytes 1048576 | tf_op jit(solution)/shard_map/all_to_all | solution.py:106
  249.1 4.3 %all-to-all-start.5 = ((f32[128,8,128]{2,1,0:T(8,128)}), f32[128,8,128]{2,1,0:T(8,128)S(1)}, u32[]{:S(2)}, u32[]{:S(2)}) async-start(f32[128,8,128]{2,1,0:T(8,128)} %broadcast_in_dim.16), calls=%async_computation.5 | async-start | bytes 1048576 | tf_op jit(solution)/shard_map/all_to_all | solution.py:108
  254.8 2.7 copy.28
  257.5 14.2 %pair_grad.1 = bf16[128,64,128]{2,1,0:T(8,128)(2,1)} custom-call(bf16[128,64,128]{2,1,0:T(8,128)(2,1)} %bitcast.85, bf16[128,2,64,128]{3,2,1,0:T(8,128)(2,1)} %all_to_all.31.grad_ref, bf16[64,512,128]{2,1,0:T(8,128)(2,1)} %gate_factors.1.factor_ref, bf16[64,128,128]{2,1,0:T(8,128)(2,1)} %copy-done.3, bf16[128,512]{1,0:T(8,128)(2,1)} %copy.27.weight_ref, ...), custom_call_target="tpu_custom_call" | custom-call | tf_op jit(solution)/shard_map/pair_grad/pallas_call | solution.py:302
  (58 shorter events, 10.4 us)
Async XLA Ops:
  10.7 10.0 %slice-start = ((bf16[128,640]{1,0:T(8,128)(2,1)}), bf16[128,512]{1,0:T(8,128)(2,1)S(1)}, s32[]{:S(2)}) async-start(bf16[128,640]{1,0:T(8,128)(2,1)} %weight_ref.1), calls=%async_computation.6 | async-start | bytes 262144 | tf_op jit(solution)/shard_map/slice | solution.py:361
  10.7 63.1 %all-to-all-start = ((bf16[128,2,64,128]{3,2,1,0:T(8,128)(2,1)}), bf16[128,2,64,128]{3,2,1,0:T(8,128)(2,1)}, u32[]{:S(2)}, u32[]{:S(2)}) async-start(bf16[128,2,64,128]{3,2,1,0:T(8,128)(2,1)} %get-tuple-element.19), calls=%async_computation | async-start | bytes 8388608 | tf_op jit(solution)/shard_map/all_to_all | solution.py:31
  21.5 6.9 %copy-start.14 = (s32[4]{0:T(128)S(1)}, s32[4]{0:T(128)}, u32[]{:S(2)}) copy-start(s32[4]{0:T(128)} %lengths_ref.3) | copy-start | bytes 52
  21.5 8.9 %copy-start.1 = (bf16[64,128,128]{2,1,0:T(8,128)(2,1)S(1)}, bf16[64,128,128]{2,1,0:T(8,128)(2,1)}, u32[]{:S(2)}) copy-start(bf16[64,128,128]{2,1,0:T(8,128)(2,1)} %get-tuple-element.20.norm_ref) | copy-start | bytes 6291460
  21.5 8.9 %copy-start.9 = (bf16[128,640]{1,0:T(8,128)(2,1)S(1)}, bf16[128,640]{1,0:T(8,128)(2,1)}, u32[]{:S(2)}) copy-start(bf16[128,640]{1,0:T(8,128)(2,1)} %weight_ref.1) | copy-start | bytes 491524
  30.5 7.0 %copy-start.12 = (bf16[128,128]{1,0:T(8,128)(2,1)S(1)}, bf16[128,128]{1,0:T(8,128)(2,1)}, u32[]{:S(2)}) copy-start(bf16[128,128]{1,0:T(8,128)(2,1)} %param.11) | copy-start | bytes 98308
  36.1 1.4 copy-start.6
  37.4 0.7 copy-start.13
  121.7 5.1 %copy-start = (bf16[128,64,128]{2,1,0:T(8,128)(2,1)S(1)}, bf16[128,64,128]{2,1,0:T(8,128)(2,1)}, u32[]{:S(2)}) copy-start(bf16[128,64,128]{2,1,0:T(8,128)(2,1)} %all_to_all.30.outer_ref) | copy-start | bytes 6291460
  121.7 32.5 %all-to-all-start.2 = ((bf16[128,64,128]{2,1,0:T(8,128)(2,1)}), bf16[128,64,128]{2,1,0:T(8,128)(2,1)}, u32[]{:S(2)}, u32[]{:S(2)}) async-start(bf16[128,64,128]{2,1,0:T(8,128)(2,1)} %outer_grad.1), calls=%async_computation.2 | async-start | bytes 4194304 | tf_op jit(solution)/shard_map/all_to_all | solution.py:31
  127.2 1.6 copy-start.8
  127.8 2.4 copy-start.5
  130.2 10.2 %copy-start.2 = (bf16[64,128,128]{2,1,0:T(8,128)(2,1)S(1)}, bf16[64,128,128]{2,1,0:T(8,128)(2,1)}, u32[]{:S(2)}) copy-start(bf16[64,128,128]{2,1,0:T(8,128)(2,1)} %get-tuple-element.20.norm_ref) | copy-start | bytes 6291460
  140.3 1.4 copy-start.3
  140.3 2.4 copy-start.7
  226.8 27.2 %copy-start.10 = (bf16[128,2,2,128]{0,1,3,2:T(2,128)(2,1)S(1)}, bf16[128,2,2,128]{0,1,3,2:T(2,128)(2,1)}, u32[]{:S(2)}) copy-start(bf16[128,2,2,128]{0,1,3,2:T(2,128)(2,1)} %copy.21) | copy-start | bytes 393220
  226.8 28.0 %copy-start.4 = (bf16[128,64,128]{2,0,1:T(8,128)(2,1)S(1)}, bf16[128,64,128]{2,0,1:T(8,128)(2,1)}, u32[]{:S(2)}) copy-start(bf16[128,64,128]{2,0,1:T(8,128)(2,1)} %get-tuple-element.26) | copy-start | bytes 6291460
  249.1 22.6 %all-to-all-start.5 = ((f32[128,8,128]{2,1,0:T(8,128)}), f32[128,8,128]{2,1,0:T(8,128)S(1)}, u32[]{:S(2)}, u32[]{:S(2)}) async-start(f32[128,8,128]{2,1,0:T(8,128)} %broadcast_in_dim.16), calls=%async_computation.5 | async-start | bytes 1048576 | tf_op jit(solution)/shard_map/all_to_all | solution.py:108
  271.7 0.9 copy-start.15
  272.4 1.2 copy-start.11

commit v4 on v3

--- a/solution.py
+++ b/solution.py
@@ -10,6 +10,7 @@
 N = 512
 ALL = ("grp", "row", "col")
 TILE = ("row", "col")
+STAGGER_NS = 22000
 
 
 epsilon = 1e-05
@@ -100,14 +101,6 @@
     )(pair_ch, grad_ch)
 
 
-def total_over_all(values):
-    devices = lax.axis_size(ALL)
-    pieces = values.reshape(devices, -1, values.shape[1])
-    arrived = lax.all_to_all(pieces, ALL, split_axis=0, concat_axis=0, tiled=True)
-    spread = jnp.broadcast_to(jnp.sum(arrived, axis=0, keepdims=True), pieces.shape)
-    return lax.all_to_all(spread, ALL, split_axis=0, concat_axis=0, tiled=True).reshape(values.shape)
-
-
 def layer_norm(values):
     centred = values - jnp.mean(values, axis=-1, keepdims=True)
     inverse = lax.rsqrt(jnp.mean(centred * centred, axis=-1, keepdims=True) + epsilon)
@@ -128,8 +121,13 @@
 def project_kernel(lengths_ref, pair_ref, weight_ref, gain_ref, tile_ref, norm_ref, rows_ref):
     row_len, block_len, _ = pair_ref.shape
     hidden_width = tile_ref.shape[0]
-
-    @pl.when(pl.program_id(0) == 0)
+    first = pl.program_id(0) == 0
+
+    @pl.when(first & (lax.axis_index("grp") % 2 == 1))
+    def _():
+        pl.delay(STAGGER_NS)
+
+    @pl.when(first)
     def _():
         for at, source in enumerate((0, 2, 1, 3)):
             part = weight_ref[:, source * hidden_width : (source + 1) * hidden_width]
@@ -279,7 +277,7 @@
 
 
 def pair_grad_kernel(
-    pair_ref, grad_ref, factor_ref, gate_ref, weight_ref, w_gate_ref, gain_ref, out_ref
+    pair_ref, grad_ref, factor_ref, gate_ref, weight_ref, w_gate_ref, gain_ref, _, out_ref
 ):
     block_len = pair_ref.shape[1]
     z_hat, z_inverse = layer_norm(jnp.swapaxes(pair_ref[...].astype(jnp.float32), 0, 1))
@@ -296,25 +294,60 @@
     out_ref[...] = jnp.swapaxes(grad_pair, 0, 1).astype(jnp.bfloat16)
 
 
-def pair_grad(pair_rep, grad_tiles, factors, grad_gate, w_tri, w_gate, gain, block_len=16):
+def pair_grad(half, into, pair_rep, grad_tiles, factors, grad_gate, w_tri, w_gate, gain, block_len=16):
     row_len, col_len, width = pair_rep.shape
     hidden_width = grad_tiles.shape[0]
+    steps = col_len // block_len // 2
+    first = half * steps
     return pl.pallas_call(
         pair_grad_kernel,
-        grid=(col_len // block_len,),
+        grid=(steps,),
         in_specs=[
-            pl.BlockSpec((row_len, block_len, width), lambda j: (0, j, 0)),
-            pl.BlockSpec((hidden_width, 2, block_len, row_len), lambda j: (0, 0, j, 0)),
-            pl.BlockSpec((block_len, 4 * hidden_width, row_len), lambda j: (j, 0, 0)),
-            pl.BlockSpec((block_len, row_len, width), lambda j: (j, 0, 0)),
+            pl.BlockSpec((row_len, block_len, width), lambda j: (0, first + j, 0)),
+            pl.BlockSpec((hidden_width, 2, block_len, row_len), lambda j: (0, 0, first + j, 0)),
+            pl.BlockSpec((block_len, 4 * hidden_width, row_len), lambda j: (first + j, 0, 0)),
+            pl.BlockSpec((block_len, row_len, width), lambda j: (first + j, 0, 0)),
             pl.BlockSpec(w_tri.shape, lambda j: (0, 0)),
             pl.BlockSpec(w_gate.shape, lambda j: (0, 0)),
             pl.BlockSpec((1, width), lambda j: (0, 0)),
-        ],
-        out_specs=pl.BlockSpec((row_len, block_len, width), lambda j: (0, j, 0)),
+            pl.BlockSpec(memory_space=pl.ANY),
+        ],
+        out_specs=pl.BlockSpec((row_len, block_len, width), lambda j: (0, first + j, 0)),
         out_shape=jax.ShapeDtypeStruct(pair_rep.shape, jnp.bfloat16),
+        input_output_aliases={7: 0},
         name="pair_grad",
-    )(pair_rep, grad_tiles, factors, grad_gate, w_tri, w_gate, gain[None])
+    )(pair_rep, grad_tiles, factors, grad_gate, w_tri, w_gate, gain[None], into)
+
+
+def finish_kernel(total_ref, w_in_ref, w_out_ref, g_in_ref, g_out_ref, gw_in_ref, gw_out_ref, gg_in_ref, gg_out_ref):
+    width = gw_out_ref.shape[0]
+    blocks = gw_in_ref.shape[1] // width
+    along_in = jnp.zeros((width, 1), jnp.float32)
+    for block in range(blocks):
+        part = total_ref[block * width : (block + 1) * width] / N
+        at = slice(block * width, (block + 1) * width)
+        gw_in_ref[:, at] = part
+        along_in += jnp.sum(part * w_in_ref[:, at].astype(jnp.float32), axis=1, keepdims=True)
+    part = total_ref[blocks * width : (blocks + 1) * width] / N
+    gw_out_ref[...] = part
+    along_out = jnp.sum(part * w_out_ref[...].astype(jnp.float32), axis=1, keepdims=True)
+    gg_in_ref[...] = jnp.broadcast_to(along_in, (width, width)).T[:1] / g_in_ref[...]
+    gg_out_ref[...] = jnp.broadcast_to(along_out, (width, width)).T[:1] / g_out_ref[...]
+
+
+def finish(totals, weight_in, weight_out, gain_in, gain_out):
+    row = jax.ShapeDtypeStruct((1, gain_in.shape[0]), jnp.float32)
+    grads = pl.pallas_call(
+        finish_kernel,
+        out_shape=[
+            jax.ShapeDtypeStruct(weight_in.shape, jnp.float32),
+            jax.ShapeDtypeStruct(weight_out.shape, jnp.float32),
+            row,
+            row,
+        ],
+        name="finish",
+    )(totals, weight_in, weight_out, gain_in[None], gain_out[None])
+    return grads[0], grads[1], grads[2][0], grads[3][0]
 
 
 def outer_grad_kernel(outer_ref, back_ref, mean_ref, grad_ref):
@@ -393,12 +426,17 @@
     grad_parts = triangle_back(pair_ch, grad_ch, rows_n, cols_n)
     grad_tiles = exchange(grad_parts.reshape(hidden_width, 2, col_len, row_len))
     sums = weight_sums(grad_tiles, factors, z_norm, grad_w_gate, grad_w_out)
-    totals = total_over_all(sums).reshape(8, width, width) / N
-    grad_w_in = jnp.concatenate([totals[block] for block in range(5)], 1)
-    grad_w_out = totals[5]
-    grad_g_in = jnp.sum(grad_w_in * weight_in.astype(jnp.float32), axis=1) / gain_in
-    grad_g_out = jnp.sum(grad_w_out * weight_out.astype(jnp.float32), axis=1) / gain_out
-    grad_pair = pair_grad(pair_rep[0], grad_tiles, factors, grad_gate, w_tri, w_gate, gain_in)
+    pieces = sums.reshape(lax.axis_size(ALL), -1, width)
+    arrived = lax.all_to_all(pieces, ALL, split_axis=0, concat_axis=0, tiled=True)
+    pair_parts = (pair_rep[0], grad_tiles, factors, grad_gate, w_tri, w_gate, gain_in)
+    grad_pair = pair_grad(0, z_norm.reshape(pair_rep.shape[1:]), *pair_parts)
+    arrived, grad_pair = lax.optimization_barrier((arrived, grad_pair))
+    spread = jnp.broadcast_to(jnp.sum(arrived, axis=0, keepdims=True), pieces.shape)
+    totals = lax.all_to_all(spread, ALL, split_axis=0, concat_axis=0, tiled=True)
+    grad_pair = pair_grad(1, grad_pair, *pair_parts)
+    grad_w_in, grad_w_out, grad_g_in, grad_g_out = finish(
+        totals.reshape(sums.shape), weight_in, weight_out, gain_in, gain_out
+    )
     return (mixed[None], grad_pair[None], grad_w_in, grad_w_out, grad_g_in, grad_g_out)
 
 

time: 275 us -> 254 us (0.924)
  blocking collectives: 115 us -> 74.5 us
  Pallas kernels: 57.5 us -> 84.4 us
  waiting for transfers between devices: 39.9 us -> 27.2 us
  starting transfers between devices: 19.3 us -> 26.3 us
    pallas_call x1, Pallas kernels: 10.1 us -> 32.1 us  [project(): pl.pallas_call(project_kernel, grid=(col_len // block_len,), in_specs=[pl...]
    all_to_all x1 -> x0, blocking collectives: 21.3 us -> none  [total_over_all(): lax.all_to_all(pieces, ALL, split_axis=0, concat_axis=0, tiled=True)]
    all_to_all x2, blocking collectives: 94 us -> 74.5 us  [exchange(): return lax.all_to_all(tiles, TILE, split_axis=0, concat_axis=0, tiled=True)]
    all_to_all x2, waiting for transfers between devices: 39.9 us -> 20.8 us  [exchange(): return lax.all_to_all(tiles, TILE, split_axis=0, concat_axis=0, tiled=True)]
    all_to_all x1 -> x2, starting transfers between devices: 4.28 us -> 11.3 us  [the longest x1 5.9 us: on_device(): lax.all_to_all(spread, ALL, split_axis=0, concat_axis=0, tiled=True)]
    all_to_all x1 -> x2, waiting for transfers between devices: 0.01 us -> 6.48 us  [the longest x1 3.87 us: on_device(): lax.all_to_all(pieces, ALL, split_axis=0, concat_axis=0, tiled=True)]
    pallas_call x1 -> x3, Pallas kernels: 14.2 us -> 19 us  [the longest x2 17.1 us: pair_grad(): pl.pallas_call(pair_grad_kernel, grid=(steps,), in_specs=[pl.BlockSpec((r...]
    unnamed x37 -> x31, local copies, waits for them, and re-layouts: 6.74 us -> 7.5 us
  transfers between devices with their start and end apart: 3 -> 4, of which waited for: 2 -> 4; matrix products, arithmetic and copies ran while one was open for 12% -> 13% of each run, Pallas kernels for 8% -> 9%
where the time goes in v4:
time: 254 us; the launch traced here: 253 us
  Pallas kernels  84.4 us (33%)
  blocking collectives  74.5 us (29%)
  waiting for transfers between devices  27.2 us (11%)
  starting transfers between devices  26.3 us (10%)
  matrix products  19.9 us (8%)
  local copies, waits for them, and re-layouts  10.6 us (4%)
  other arithmetic  9.01 us (4%)
    all_to_all x2, blocking collectives, exchange(): return lax.all_to_all(tiles, TILE, split_axis=0, concat_axis=0, tiled=True)  74.5 us
    pallas_call x1, Pallas kernels, project(): pl.pallas_call(project_kernel, grid=(col_len // block_len,), in_specs=[pl...  32.1 us
    all_to_all x2, waiting for transfers between devices, exchange(): return lax.all_to_all(tiles, TILE, split_axis=0, concat_axis=0, tiled=True)  20.8 us
    pallas_call x2, Pallas kernels, pair_grad(): pl.pallas_call(pair_grad_kernel, grid=(steps,), in_specs=[pl.BlockSpec((r...  17.1 us
    all_to_all x2, starting transfers between devices, exchange(): return lax.all_to_all(tiles, TILE, split_axis=0, concat_axis=0, tiled=True)  15 us
    dot_general x1, matrix products, on_device(): jnp.einsum('hji,hc->jic', o_norm, weight_out, preferred_element_type=jnp....  10.1 us
    pallas_call x1, Pallas kernels, weight_sums(): pl.pallas_call(weight_sums_kernel, grid=(col_len // block_len,), in_specs...  8.51 us
    unnamed x31, local copies, waits for them, and re-layouts  7.5 us
  transfers between devices with their start and end apart: 4, of which 4 were waited for; matrix products, arithmetic and copies ran while one was open for 13% of the time, Pallas kernels for 9%

profile of v4, /device:TPU:1, one launch (start us, length us, event | category | flops | bytes accessed | tf_op | source)
XLA Modules:
  0.0 252.7 jit_solution(1479737224808692430)
XLA Ops:
  0.6 32.1 %project.1 = (bf16[128,2,64,128]{3,2,1,0:T(8,128)(2,1)}, bf16[64,128,128]{2,1,0:T(8,128)(2,1)}) custom-call(s32[4]{0:T(128)} %lengths_ref.3, bf16[128,64,128]{2,1,0:T(8,128)(2,1)} %bitcast.65, bf16[128,640]{1,0:T(8,128)(2,1)} %w_in_ref.1, f32[1,128]{1,0:T(1,128)} %bitcast.75), custom_call_target="tpu_custom_call" | custom-call | tf_op jit(solution)/shard_map/project/pallas_call | solution.py:157
  32.8 10.0 %all-to-all-start = ((bf16[128,2,64,128]{3,2,1,0:T(8,128)(2,1)}), bf16[128,2,64,128]{3,2,1,0:T(8,128)(2,1)}, u32[]{:S(2)}, u32[]{:S(2)}) async-start(bf16[128,2,64,128]{3,2,1,0:T(8,128)(2,1)} %get-tuple-element.25), calls=%async_computation | async-start | bytes 8388608 | tf_op jit(solution)/shard_map/all_to_all | solution.py:32
  43.6 6.9 %gate_factors.1.factor_ref = bf16[64,512,128]{2,1,0:T(8,128)(2,1)} custom-call(s32[4]{0:T(128)} %lengths_ref.3, bf16[64,128,128]{2,1,0:T(8,128)(2,1)} %get-tuple-element.26.norm_ref, bf16[512,128]{1,0:T(8,128)(2,1)} %bitcast.73), custom_call_target="tpu_custom_call" | custom-call | tf_op jit(solution)/shard_map/gate_factors/pallas_call | solution.py:195
  52.5 5.6 %fusion.7 = (bf16[64,128,128]{2,1,0:T(8,128)(2,1)S(1)}, f32[64,128,128]{2,1,0:T(8,128)}) fusion(bf16[1,128,64,128]{3,2,1,0:T(8,128)(2,1)} %param.8, f32[64,128]{1,0:T(8,128)S(1)} %and_convert_fusion, bf16[64,128,128]{2,1,0:T(8,128)(2,1)S(1)} %copy-done.1, bf16[128,640]{1,0:T(8,128)(2,1)S(1)} %copy-done.10), kind=kOutput, calls=%fused_computation.10 | convolution fusion | flops 275775488 | bytes 10551296 | tf_op jit(solution)/shard_map/jic,cd->jid/dot_general | solution.py:397
  60.2 4.6 %fusion.26 = (f32[64,128]{1,0:T(8,128)S(1)}, f32[128,64,128]{2,1,0:T(8,128)}) fusion(f32[128]{0:T(128)S(1)} %copy-done.13, f32[64,128,128]{1,2,0:T(8,128)S(1)} %fusion.21), kind=kLoop, calls=%fused_computation.38 | loop fusion | flops 2088960 | bytes 8421888 | tf_op jit(solution)/shard_map/reduce_sum | solution.py:405
  65.4 18.3 %all-to-all-done = bf16[128,2,64,128]{3,2,1,0:T(8,128)(2,1)} async-done(((bf16[128,2,64,128]{3,2,1,0:T(8,128)(2,1)}), bf16[128,2,64,128]{3,2,1,0:T(8,128)(2,1)}, u32[]{:S(2)}, u32[]{:S(2)}) %all-to-all-start) | async-done | bytes 4194336 | tf_op jit(solution)/shard_map/all_to_all | solution.py:32
  83.7 5.2 %triangle_forward.1 = bf16[32,4,64,128]{3,2,1,0:T(8,128)(2,1)} custom-call(bf16[32,4,2,64,128]{4,3,2,1,0:T(8,128)(2,1)} %bitcast.2.pair_ref), custom_call_target="tpu_custom_call" | custom-call | tf_op jit(solution)/shard_map/triangle_forward/pallas_call | solution.py:76
  88.9 26.7 %all_to_all.30.outer_ref = bf16[128,64,128]{2,1,0:T(8,128)(2,1)} all-to-all(bf16[128,64,128]{2,1,0:T(8,128)(2,1)} %bitcast.69), channel_id=1, replica_groups=mesh['grp'=4,'row'=4,'col'=8] {'row','col'}, dimensions={0} | all-to-all | bytes 4194304 | tf_op jit(solution)/shard_map/all_to_all | solution.py:32
  115.6 6.0 %outer_grad.1 = bf16[128,64,128]{2,1,0:T(8,128)(2,1)} custom-call(bf16[128,64,128]{2,1,0:T(8,128)(2,1)} %all_to_all.30.outer_ref, f32[128,64,128]{2,1,0:T(8,128)} %get-tuple-element.28.back_ref, f32[64,128]{1,0:T(8,128)} %broadcast_multiply_fusion.1.mean_ref), custom_call_target="tpu_custom_call" | custom-call | tf_op jit(solution)/shard_map/outer_grad/pallas_call | solution.py:364
  121.6 5.1 %all-to-all-start.2 = ((bf16[128,64,128]{2,1,0:T(8,128)(2,1)}), bf16[128,64,128]{2,1,0:T(8,128)(2,1)}, u32[]{:S(2)}, u32[]{:S(2)}) async-start(bf16[128,64,128]{2,1,0:T(8,128)(2,1)} %outer_grad.1), calls=%async_computation.2 | async-start | bytes 4194304 | tf_op jit(solution)/shard_map/all_to_all | solution.py:32
  130.0 10.1 %fusion.10 = (bf16[64,128,128]{2,1,0:T(8,128)(2,1)S(1)}, bf16[128,64,128]{2,0,1:T(8,128)(2,1)}) fusion(f32[64,128,128]{2,1,0:T(8,128)S(1)} %copy-done.5, bf16[1,128,64,128]{3,2,1,0:T(8,128)(2,1)S(1)} %copy-done.9, bf16[128,128]{1,0:T(8,128)(2,1)S(1)} %copy-done.12, bf16[128,64,128]{2,1,0:T(8,128)(2,1)S(1)} %fusion.4), kind=kOutput, calls=%fused_computation.13 | convolution fusion | flops 276824064 | bytes 12615680 | tf_op jit(solution)/shard_map/hji,hc->jic/dot_general | solution.py:417
  142.5 2.1 fusion.17.out_ref
  144.6 2.5 all-to-all-done.2
  147.1 6.7 %triangle_backward.1 = bf16[32,4,2,64,128]{4,3,2,1,0:T(8,128)(2,1)} custom-call(bf16[32,4,2,64,128]{4,3,2,1,0:T(8,128)(2,1)} %bitcast.2.pair_ref, bf16[32,4,64,128]{3,2,1,0:T(8,128)(2,1)} %bitcast.12.grad_ref), custom_call_target="tpu_custom_call" | custom-call | tf_op jit(solution)/shard_map/triangle_backward/pallas_call | solution.py:90
  153.7 47.8 %all_to_all.31.grad_ref = bf16[128,2,64,128]{3,2,1,0:T(8,128)(2,1)} all-to-all(bf16[128,2,64,128]{3,2,1,0:T(8,128)(2,1)} %bitcast.68), channel_id=1, replica_groups=mesh['grp'=4,'row'=4,'col'=8] {'row','col'}, dimensions={0} | all-to-all | bytes 8388608 | tf_op jit(solution)/shard_map/all_to_all | solution.py:32
  201.6 8.5 %weight_sums.1 = f32[1024,128]{1,0:T(8,128)} custom-call(bf16[128,2,64,128]{3,2,1,0:T(8,128)(2,1)} %all_to_all.31.grad_ref, bf16[64,512,128]{2,1,0:T(8,128)(2,1)} %gate_factors.1.factor_ref, bf16[64,128,128]{2,1,0:T(8,128)(2,1)} %get-tuple-element.26.norm_ref, f32[128,128]{1,0:T(8,128)} %convolution_bitcast_fusion.gate_ref, f32[128,128]{1,0:T(8,128)} %fusion.17.out_ref), custom_call_target="tpu_custom_call" | custom-call | tf_op jit(solution)/shard_map/weight_sums/pallas_call | solution.py:262
  210.1 5.4 %all-to-all-start.4 = ((f32[128,8,128]{2,1,0:T(8,128)}), f32[128,8,128]{2,1,0:T(8,128)S(1)}, u32[]{:S(2)}, u32[]{:S(2)}) async-start(f32[128,8,128]{2,1,0:T(8,128)} %bitcast.72), calls=%async_computation.4 | async-start | bytes 1048576 | tf_op jit(solution)/shard_map/all_to_all | solution.py:430
  216.8 8.6 %pair_grad.2._ = bf16[128,64,128]{2,1,0:T(8,128)(2,1)} custom-call(bf16[128,64,128]{2,1,0:T(8,128)(2,1)} %bitcast.66, bf16[128,2,64,128]{3,2,1,0:T(8,128)(2,1)} %all_to_all.31.grad_ref, bf16[64,512,128]{2,1,0:T(8,128)(2,1)} %gate_factors.1.factor_ref, bf16[64,128,128]{2,1,0:T(8,128)(2,1)} %copy-done.3, ...), custom_call_target="tpu_custom_call", output_to_operand_aliasing={{}: (7, {})} | custom-call | tf_op jit(solution)/shard_map/pair_grad/pallas_call | solution.py:302
  225.4 3.9 %all-to-all-done.4 = f32[128,8,128]{2,1,0:T(8,128)S(1)} async-done(((f32[128,8,128]{2,1,0:T(8,128)}), f32[128,8,128]{2,1,0:T(8,128)S(1)}, u32[]{:S(2)}, u32[]{:S(2)}) %all-to-all-start.4) | async-done | bytes 524320 | tf_op jit(solution)/shard_map/all_to_all | solution.py:430
  230.3 5.9 %all-to-all-start.5 = ((f32[128,8,128]{2,1,0:T(8,128)}), f32[128,8,128]{2,1,0:T(8,128)S(1)}, u32[]{:S(2)}, u32[]{:S(2)}) async-start(f32[128,8,128]{2,1,0:T(8,128)} %broadcast_in_dim.18), calls=%async_computation.5 | async-start | bytes 1048576 | tf_op jit(solution)/shard_map/all_to_all | solution.py:435
  236.2 2.7 %copy.31 = bf16[1,128,64,128]{3,2,1,0:T(8,128)(2,1)} copy(bf16[1,128,64,128]{3,1,2,0:T(8,128)(2,1)S(1)} %bitcast.70) | data formatting | bytes 4194304
  238.9 8.5 %pair_grad.3 = bf16[128,64,128]{2,1,0:T(8,128)(2,1)} custom-call(bf16[128,64,128]{2,1,0:T(8,128)(2,1)} %bitcast.67, bf16[128,2,64,128]{3,2,1,0:T(8,128)(2,1)} %all_to_all.31.grad_ref, bf16[64,512,128]{2,1,0:T(8,128)(2,1)} %gate_factors.1.factor_ref, bf16[64,128,128]{2,1,0:T(8,128)(2,1)} %copy-done.3, ...), custom_call_target="tpu_custom_call", output_to_operand_aliasing={{}: (7, {})} | custom-call | tf_op jit(solution)/shard_map/pair_grad/pallas_call | solution.py:302
  247.4 2.6 %all-to-all-done.5 = f32[128,8,128]{2,1,0:T(8,128)S(1)} async-done(((f32[128,8,128]{2,1,0:T(8,128)}), f32[128,8,128]{2,1,0:T(8,128)S(1)}, u32[]{:S(2)}, u32[]{:S(2)}) %all-to-all-start.5) | async-done | bytes 524320 | tf_op jit(solution)/shard_map/all_to_all | solution.py:435
  250.8 1.9 finish.1
  (50 shorter events, 14.4 us)
Async XLA Ops:
  32.8 10.0 %slice-start = ((bf16[128,640]{1,0:T(8,128)(2,1)}), bf16[128,512]{1,0:T(8,128)(2,1)S(1)}, s32[]{:S(2)}) async-start(bf16[128,640]{1,0:T(8,128)(2,1)} %w_in_ref.1), calls=%async_computation.6 | async-start | bytes 262144 | tf_op jit(solution)/shard_map/slice | solution.py:394
  32.8 50.9 %all-to-all-start = ((bf16[128,2,64,128]{3,2,1,0:T(8,128)(2,1)}), bf16[128,2,64,128]{3,2,1,0:T(8,128)(2,1)}, u32[]{:S(2)}, u32[]{:S(2)}) async-start(bf16[128,2,64,128]{3,2,1,0:T(8,128)(2,1)} %get-tuple-element.25), calls=%async_computation | async-start | bytes 8388608 | tf_op jit(solution)/shard_map/all_to_all | solution.py:32
  43.6 6.9 %copy-start.14 = (s32[4]{0:T(128)S(1)}, s32[4]{0:T(128)}, u32[]{:S(2)}) copy-start(s32[4]{0:T(128)} %lengths_ref.3) | copy-start | bytes 52
  43.6 8.9 %copy-start.1 = (bf16[64,128,128]{2,1,0:T(8,128)(2,1)S(1)}, bf16[64,128,128]{2,1,0:T(8,128)(2,1)}, u32[]{:S(2)}) copy-start(bf16[64,128,128]{2,1,0:T(8,128)(2,1)} %get-tuple-element.26.norm_ref) | copy-start | bytes 6291460
  43.6 8.9 %copy-start.10 = (bf16[128,640]{1,0:T(8,128)(2,1)S(1)}, bf16[128,640]{1,0:T(8,128)(2,1)}, u32[]{:S(2)}) copy-start(bf16[128,640]{1,0:T(8,128)(2,1)} %w_in_ref.1) | copy-start | bytes 491524
  52.5 7.0 %copy-start.12 = (bf16[128,128]{1,0:T(8,128)(2,1)S(1)}, bf16[128,128]{1,0:T(8,128)(2,1)}, u32[]{:S(2)}) copy-start(bf16[128,128]{1,0:T(8,128)(2,1)} %w_out_ref.1) | copy-start | bytes 98308
  58.1 1.4 copy-start.6
  59.5 0.7 copy-start.13
  121.6 5.1 %copy-start = (bf16[128,64,128]{2,1,0:T(8,128)(2,1)S(1)}, bf16[128,64,128]{2,1,0:T(8,128)(2,1)}, u32[]{:S(2)}) copy-start(bf16[128,64,128]{2,1,0:T(8,128)(2,1)} %all_to_all.30.outer_ref) | copy-start | bytes 6291460
  121.6 25.5 %all-to-all-start.2 = ((bf16[128,64,128]{2,1,0:T(8,128)(2,1)}), bf16[128,64,128]{2,1,0:T(8,128)(2,1)}, u32[]{:S(2)}, u32[]{:S(2)}) async-start(bf16[128,64,128]{2,1,0:T(8,128)(2,1)} %outer_grad.1), calls=%async_computation.2 | async-start | bytes 4194304 | tf_op jit(solution)/shard_map/all_to_all | solution.py:32
  127.0 1.6 copy-start.9
  127.7 2.4 copy-start.5
  130.0 10.2 %copy-start.2 = (bf16[64,128,128]{2,1,0:T(8,128)(2,1)S(1)}, bf16[64,128,128]{2,1,0:T(8,128)(2,1)}, u32[]{:S(2)}) copy-start(bf16[64,128,128]{2,1,0:T(8,128)(2,1)} %get-tuple-element.26.norm_ref) | copy-start | bytes 6291460
  140.2 1.4 copy-start.3
  140.2 2.4 copy-start.7
  201.6 14.5 %copy-start.11 = (bf16[128,2,2,128]{0,1,3,2:T(2,128)(2,1)S(1)}, bf16[128,2,2,128]{0,1,3,2:T(2,128)(2,1)}, u32[]{:S(2)}) copy-start(bf16[128,2,2,128]{0,1,3,2:T(2,128)(2,1)} %copy.23) | copy-start | bytes 393220
  210.1 19.2 %all-to-all-start.4 = ((f32[128,8,128]{2,1,0:T(8,128)}), f32[128,8,128]{2,1,0:T(8,128)S(1)}, u32[]{:S(2)}, u32[]{:S(2)}) async-start(f32[128,8,128]{2,1,0:T(8,128)} %bitcast.72), calls=%async_computation.4 | async-start | bytes 1048576 | tf_op jit(solution)/shard_map/all_to_all | solution.py:430
  225.4 10.8 %copy-start.4 = (bf16[128,64,128]{2,0,1:T(8,128)(2,1)S(1)}, bf16[128,64,128]{2,0,1:T(8,128)(2,1)}, u32[]{:S(2)}) copy-start(bf16[128,64,128]{2,0,1:T(8,128)(2,1)} %get-tuple-element.32) | copy-start | bytes 6291460
  230.3 19.7 %all-to-all-start.5 = ((f32[128,8,128]{2,1,0:T(8,128)}), f32[128,8,128]{2,1,0:T(8,128)S(1)}, u32[]{:S(2)}, u32[]{:S(2)}) async-start(f32[128,8,128]{2,1,0:T(8,128)} %broadcast_in_dim.18), calls=%async_computation.5 | async-start | bytes 1048576 | tf_op jit(solution)/shard_map/all_to_all | solution.py:435
  250.0 0.8 copy-start.8

commit v5 on v4

--- a/solution.py
+++ b/solution.py
@@ -10,7 +10,7 @@
 N = 512
 ALL = ("grp", "row", "col")
 TILE = ("row", "col")
-STAGGER_NS = 22000
+STAGGER_NS = 2000
 
 
 epsilon = 1e-05
@@ -123,10 +123,6 @@
     hidden_width = tile_ref.shape[0]
     first = pl.program_id(0) == 0
 
-    @pl.when(first & (lax.axis_index("grp") % 2 == 1))
-    def _():
-        pl.delay(STAGGER_NS)
-
     @pl.when(first)
     def _():
         for at, source in enumerate((0, 2, 1, 3)):
@@ -176,10 +172,28 @@
     )(lengths, pair_rep, weight_in, gain[None])
 
 
-def factors_kernel(lengths_ref, norm_ref, weight_ref, factor_ref):
-    block_len, row_len, _ = norm_ref.shape
+def side_kernel(
+    lengths_ref,
+    weight_ref,
+    w_gate_ref,
+    w_out_ref,
+    gain_ref,
+    norm_ref,
+    cotangent_ref,
+    factor_ref,
+    gate_ref,
+    grad_proj_ref,
+    back_ref,
+    mean_ref,
+):
+    block_len, row_len, width = norm_ref.shape
     half = weight_ref.shape[0] // 2
     inside = tile_inside(lengths_ref, row_len, block_len)
+    grad_out = jnp.swapaxes(cotangent_ref[...].astype(jnp.float32), 0, 1)
+    length = lengths_ref[lax.axis_index("grp")]
+    row_at = lax.axis_index("row") * row_len + lax.broadcasted_iota(jnp.int32, (row_len, 1), 0)
+    col_start = (lax.axis_index("col") * pl.num_programs(0) + pl.program_id(0)) * block_len
+    backs = []
     for j in range(block_len):
         projected = lax.dot_general(
             weight_ref[...], norm_ref[j], (((1,), (1,)), ((), ())), preferred_element_type=jnp.float32
@@ -188,22 +202,83 @@
         kept = sig * inside[j]
         factor_ref[j, :half] = kept.astype(jnp.bfloat16)
         factor_ref[j, half:] = (projected[:half] * kept * (1.0 - sig)).astype(jnp.bfloat16)
-
-
-def gate_factors(lengths, z_norm, weight_rows, block_len=16):
+        here = jnp.where((row_at < length) & (col_start + j < length), 1.0, 0.0)
+        gate_pre = jnp.dot(norm_ref[j], w_gate_ref[...], preferred_element_type=jnp.float32)
+        gate = jax.nn.sigmoid(gate_pre) * here
+        gate_ref[j] = gate
+        grad_proj = (grad_out[j] * gate).astype(jnp.bfloat16)
+        grad_proj_ref[j] = grad_proj
+        back = gain_ref[...] * lax.dot_general(
+            w_out_ref[...], grad_proj, (((1,), (1,)), ((), ())), preferred_element_type=jnp.float32
+        )
+        mean_ref[j : j + 1] = jnp.mean(back, axis=0, keepdims=True)
+        backs.append(back)
+    back_ref[...] = jnp.swapaxes(jnp.stack(backs, 0), 0, 1)
+
+
+def gain_rows(gain_ref):
+    width = gain_ref.shape[1]
+    return jnp.broadcast_to(gain_ref[...], (width, width)).T
+
+
+def side_pipeline(odd, specs_in, specs_out, steps, lengths_ref, weight_ref, w_out_ref, gain_ref, *refs):
+    *refs, wide_ref, rows_ref, spread_ref = refs
+    inputs, outputs = refs[: len(specs_in)], refs[-len(specs_out) :]
+    width = w_out_ref.shape[0]
+
+    @pl.when(lax.axis_index("grp") % 2 == odd)
+    def _():
+        if odd and STAGGER_NS:
+            pl.delay(STAGGER_NS)
+        for side in range(2):
+            for kind in range(2):
+                source = (2 * side + kind) * width
+                part = weight_ref[:, source : source + width].astype(jnp.float32).T
+                wide_ref[pl.ds(kind * 2 * width + side, width, stride=2), :] = part
+        rows_ref[...] = wide_ref[...].astype(jnp.bfloat16)
+        spread_ref[...] = gain_rows(gain_ref)
+        w_gate_ref = weight_ref.at[:, 4 * width :]
+        pltpu.emit_pipeline(
+            functools.partial(side_kernel, lengths_ref, rows_ref, w_gate_ref, w_out_ref, spread_ref),
+            grid=(steps,),
+            in_specs=specs_in,
+            out_specs=specs_out,
+        )(*inputs, *outputs)
+
+
+def side_work(odd, into, lengths, weight_in, w_out, gain_out, z_norm, cotangent, block_len=16):
     col_len, row_len, width = z_norm.shape
-    return pl.pallas_call(
-        factors_kernel,
-        grid=(col_len // block_len,),
-        in_specs=[
-            pl.BlockSpec(memory_space=pltpu.SMEM),
-            pl.BlockSpec((block_len, row_len, width), lambda j: (j, 0, 0)),
-            pl.BlockSpec(weight_rows.shape, lambda j: (0, 0)),
-        ],
-        out_specs=pl.BlockSpec((block_len, weight_rows.shape[0], row_len), lambda j: (j, 0, 0)),
-        out_shape=jax.ShapeDtypeStruct((col_len, weight_rows.shape[0], row_len), jnp.bfloat16),
-        name="gate_factors",
-    )(lengths, z_norm, weight_rows)
+    hidden_width = w_out.shape[0]
+    by_pair = pl.BlockSpec((block_len, row_len, width), lambda j: (j, 0, 0))
+    specs_in = [by_pair, pl.BlockSpec((row_len, block_len, width), lambda j: (0, j, 0))]
+    specs_out = [
+        pl.BlockSpec((block_len, 4 * hidden_width, row_len), lambda j: (j, 0, 0)),
+        by_pair,
+        by_pair,
+        pl.BlockSpec((hidden_width, block_len, row_len), lambda j: (0, j, 0)),
+        pl.BlockSpec((block_len, row_len), lambda j: (j, 0)),
+    ]
+    anywhere = pl.BlockSpec(memory_space=pl.ANY)
+    in_vmem = pl.BlockSpec(memory_space=pltpu.VMEM)
+    return pl.pallas_call(
+        functools.partial(side_pipeline, odd, specs_in, specs_out, col_len // block_len),
+        in_specs=[pl.BlockSpec(memory_space=pltpu.SMEM)] + [in_vmem] * 3 + [anywhere] * (2 + len(into)),
+        out_specs=[anywhere] * len(specs_out),
+        out_shape=[
+            pltpu.HBM((col_len, 4 * hidden_width, row_len), jnp.bfloat16),
+            pltpu.HBM(z_norm.shape, jnp.float32),
+            pltpu.HBM(z_norm.shape, jnp.bfloat16),
+            pltpu.HBM((hidden_width, col_len, row_len), jnp.float32),
+            pltpu.HBM((col_len, row_len), jnp.float32),
+        ],
+        scratch_shapes=[
+            pltpu.VMEM((4 * hidden_width, width), jnp.float32),
+            pltpu.VMEM((4 * hidden_width, width), jnp.bfloat16),
+            pltpu.VMEM((hidden_width, width), jnp.float32),
+        ],
+        input_output_aliases={6 + at: at for at in range(len(into))},
+        name="side_work",
+    )(lengths, weight_in, w_out, gain_out[None], z_norm, cotangent, *into)
 
 
 def projection_grads(grad_ref, factor_ref):
@@ -220,6 +295,78 @@
         ).astype(jnp.bfloat16)
         for j in range(block_len)
     ]
+
+
+def block_output_kernel(
+    outer_ref, gate_ref, grad_proj_ref, cotangent_ref, norm_ref, w_out_ref, gain_ref,
+    mixed_ref, grad_gate_ref, sum_out_ref, sum_gate_ref,
+):
+    hidden_width, block_len, row_len = outer_ref.shape
+    width = norm_ref.shape[2]
+    o_hat, _ = normalize(outer_ref[...].astype(jnp.float32), 0)
+    o_hat = jnp.swapaxes(o_hat, 0, 1)
+    grad_out = jnp.swapaxes(cotangent_ref[...].astype(jnp.float32), 0, 1)
+    spread = gain_rows(gain_ref)
+    normed, mixed = [], []
+    for j in range(block_len):
+        o_norm = (o_hat[j] * spread).astype(jnp.bfloat16)
+        normed.append(o_norm)
+        proj_out = lax.dot_general(
+            o_norm, w_out_ref[...], (((0,), (0,)), ((), ())), preferred_element_type=jnp.float32
+        )
+        gate = gate_ref[j]
+        mixed.append(gate * proj_out)
+        grad_gate_ref[j] = (grad_out[j] * proj_out * gate * (1.0 - gate)).astype(jnp.bfloat16)
+    mixed_ref[...] = jnp.swapaxes(jnp.stack(mixed, 0), 0, 1).astype(jnp.bfloat16)
+    flat = (block_len * row_len, width)
+    sum_out = jnp.dot(
+        jnp.concatenate(normed, 1), grad_proj_ref[...].reshape(flat), preferred_element_type=jnp.float32
+    )
+    sum_gate = lax.dot_general(
+        norm_ref[...].reshape(flat),
+        grad_gate_ref[...].reshape(flat),
+        (((0,), (0,)), ((), ())),
+        preferred_element_type=jnp.float32,
+    )
+
+    @pl.when(pl.program_id(0) == 0)
+    def _():
+        sum_out_ref[...] = sum_out
+        sum_gate_ref[...] = sum_gate
+
+    @pl.when(pl.program_id(0) > 0)
+    def _():
+        sum_out_ref[...] += sum_out
+        sum_gate_ref[...] += sum_gate
+
+
+def block_output(outer_tile, gate, grad_proj, cotangent, z_norm, w_out, gain_out, block_len=16):
+    hidden_width, col_len, row_len = outer_tile.shape
+    width = z_norm.shape[2]
+    by_pair = pl.BlockSpec((block_len, row_len, width), lambda j: (j, 0, 0))
+    natural = pl.BlockSpec((row_len, block_len, width), lambda j: (0, j, 0))
+    square = pl.BlockSpec((width, width), lambda j: (0, 0))
+    return pl.pallas_call(
+        block_output_kernel,
+        grid=(col_len // block_len,),
+        in_specs=[
+            pl.BlockSpec((hidden_width, block_len, row_len), lambda j: (0, j, 0)),
+            by_pair,
+            by_pair,
+            natural,
+            by_pair,
+            square,
+            pl.BlockSpec((1, width), lambda j: (0, 0)),
+        ],
+        out_specs=[natural, by_pair, square, square],
+        out_shape=[
+            pltpu.HBM(cotangent.shape, jnp.bfloat16),
+            jax.ShapeDtypeStruct(z_norm.shape, jnp.bfloat16),
+            jax.ShapeDtypeStruct((width, width), jnp.float32),
+            jax.ShapeDtypeStruct((width, width), jnp.float32),
+        ],
+        name="block_output",
+    )(outer_tile, gate, grad_proj, cotangent, z_norm, w_out, gain_out[None])
 
 
 def weight_sums_kernel(grad_ref, factor_ref, norm_ref, gate_ref, out_ref, sum_ref, total_ref):
@@ -351,11 +498,29 @@
 
 
 def outer_grad_kernel(outer_ref, back_ref, mean_ref, grad_ref):
-    o_hat, o_inverse = normalize(outer_ref[...].astype(jnp.float32), 0)
-    back = back_ref[...]
-    second_mean = jnp.mean(back * o_hat, axis=0, keepdims=True)
-    grad = o_inverse * (back - mean_ref[...][None] - o_hat * second_mean)
-    grad_ref[...] = grad.astype(jnp.bfloat16)
+    hidden_width = outer_ref.shape[0]
+    zero = jnp.zeros(mean_ref.shape, jnp.float32)
+
+    def over_channels(step, start):
+        return lax.fori_loop(0, hidden_width, step, start, unroll=16)
+
+    mean = over_channels(lambda h, run: run + outer_ref[h].astype(jnp.float32), zero) / hidden_width
+
+    def products(h, run):
+        centred = outer_ref[h].astype(jnp.float32) - mean
+        return run[0] + centred * centred, run[1] + centred * back_ref[h]
+
+    square, cross = over_channels(products, (zero, zero))
+    inverse = lax.rsqrt(square / hidden_width + epsilon)
+    slope = inverse * inverse * inverse * (cross / hidden_width)
+    offset = inverse * mean_ref[...]
+
+    def write(h, run):
+        centred = outer_ref[h].astype(jnp.float32) - mean
+        grad_ref[h] = (inverse * back_ref[h] - offset - centred * slope).astype(jnp.bfloat16)
+        return run
+
+    over_channels(write, 0)
 
 
 def outer_grad(outer_tile, back, back_mean, block_len=16):
@@ -372,7 +537,6 @@
 
 
 def on_device(pair_rep, cotangent, lengths, weight_in, weight_out, gain_in, gain_out):
-    groups = lax.axis_size("grp")
     rows_n = lax.axis_size("row")
     cols_n = lax.axis_size("col")
     devices = rows_n * cols_n
@@ -381,50 +545,33 @@
     width = pair_rep.shape[3]
     hidden_width = weight_out.shape[0]
     share = hidden_width // devices
-    lookup = jnp.arange(groups) == lax.axis_index("grp")
-    own_length = jnp.sum(jnp.where(lookup, lengths, 0))
-    row_in = lax.axis_index("row") * row_len + jnp.arange(row_len) < own_length
-    col_in = lax.axis_index("col") * col_len + jnp.arange(col_len) < own_length
-    flipped_c = (col_in[:, None] & row_in[None, :]).astype(jnp.float32)[:, :, None]
-    w_gate = weight_in[:, 4 * hidden_width :]
 
     pair_tiles, z_norm = project(lengths, pair_rep[0], weight_in, gain_in)
+    side_args = (lengths, weight_in, weight_out, gain_out, z_norm, cotangent[0])
+    side = side_work(1, (), *side_args)
+    pair_tiles, *side = lax.optimization_barrier((pair_tiles, *side))
     pair_ch = exchange(pair_tiles).reshape(devices, share, 2, col_len, row_len)
-
-    w_tri = weight_in[:, : 4 * hidden_width].reshape(width, 2, 2, hidden_width)
-    w_tri = w_tri.transpose(0, 2, 3, 1).reshape(width, 4 * hidden_width)
-    factors = gate_factors(lengths, z_norm, w_tri.T)
-    gate_pre = jnp.einsum("jic,cd->jid", z_norm, w_gate, preferred_element_type=jnp.float32)
-    gate = jax.nn.sigmoid(gate_pre) * flipped_c
-    grad_out = jnp.swapaxes(cotangent[0], 0, 1).astype(jnp.float32)
-    grad_proj = (grad_out * gate).astype(jnp.bfloat16)
-    grad_o_norm = jnp.einsum(
-        "jic,hc->hji", grad_proj, weight_out, preferred_element_type=jnp.float32
-    )
-    back = grad_o_norm * gain_out[:, None, None]
-    back_mean = jnp.mean(back, axis=0)
-    pair_ch, factors, gate, grad_proj, back, back_mean = lax.optimization_barrier(
-        (pair_ch, factors, gate, grad_proj, back, back_mean)
-    )
-
     outer_ch = triangle(pair_ch, rows_n, cols_n)
+    outer_ch, *side = lax.optimization_barrier((outer_ch, *side))
     outer_tile = exchange(outer_ch.reshape(hidden_width, col_len, row_len))
+    side = side_work(0, tuple(side), *side_args)
+    outer_tile, *side = lax.optimization_barrier((outer_tile, *side))
+    factors, gate, grad_proj, back, back_mean = side
     grad_outer = outer_grad(outer_tile, back, back_mean)
     grad_ch = exchange(grad_outer).reshape(devices, share, col_len, row_len)
 
-    o_hat, _ = normalize(outer_tile.astype(jnp.float32), 0)
-    o_norm = (o_hat * gain_out[:, None, None]).astype(jnp.bfloat16)
-    proj_out = jnp.einsum("hji,hc->jic", o_norm, weight_out, preferred_element_type=jnp.float32)
-    mixed = jnp.swapaxes((gate * proj_out).astype(jnp.bfloat16), 0, 1)
-    grad_gate = (grad_out * proj_out * gate * (1.0 - gate)).astype(jnp.bfloat16)
-    grad_w_out = jnp.einsum("hji,jic->hc", o_norm, grad_proj, preferred_element_type=jnp.float32)
-    grad_w_gate = jnp.einsum("jic,jid->cd", z_norm, grad_gate, preferred_element_type=jnp.float32)
-
+    mixed, grad_gate, grad_w_out, grad_w_gate = block_output(
+        outer_tile, gate, grad_proj, cotangent[0], z_norm, weight_out, gain_out
+    )
     grad_ch, mixed, grad_gate, grad_w_gate, grad_w_out = lax.optimization_barrier(
         (grad_ch, mixed, grad_gate, grad_w_gate, grad_w_out)
     )
     grad_parts = triangle_back(pair_ch, grad_ch, rows_n, cols_n)
     grad_tiles = exchange(grad_parts.reshape(hidden_width, 2, col_len, row_len))
+    grad_tiles, late_weight = lax.optimization_barrier((grad_tiles, weight_in))
+    w_tri = late_weight[:, : 4 * hidden_width].reshape(width, 2, 2, hidden_width)
+    w_tri = w_tri.transpose(0, 2, 3, 1).reshape(width, 4 * hidden_width)
+    w_gate = late_weight[:, 4 * hidden_width :]
     sums = weight_sums(grad_tiles, factors, z_norm, grad_w_gate, grad_w_out)
     pieces = sums.reshape(lax.axis_size(ALL), -1, width)
     arrived = lax.all_to_all(pieces, ALL, split_axis=0, concat_axis=0, tiled=True)

time: 254 us -> 253 us (level)
  blocking collectives: 74.5 us -> 103 us
  matrix products: 19.9 us -> 0 us
  waiting for transfers between devices: 27.2 us -> 39 us
  other arithmetic: 9.01 us -> 0.14 us
  starting transfers between devices: 26.3 us -> 19.5 us
  local copies, waits for them, and re-layouts: 10.6 us -> 5.91 us
    all_to_all x2, blocking collectives: 74.5 us -> 103 us  [exchange(): return lax.all_to_all(tiles, TILE, split_axis=0, concat_axis=0, tiled=True)]
    pallas_call x1, Pallas kernels: 32.1 us -> 10.1 us  [project(): pl.pallas_call(project_kernel, grid=(col_len // block_len,), in_specs=[pl...]
    pallas_call x1 -> x3, Pallas kernels: 6.86 us -> 27.9 us  [the longest x2 17.5 us: side_work(): pl.pallas_call(functools.partial(side_pipeline, odd, specs_in, specs_out,...]
    dot_general x5 -> x0, matrix products: 19.9 us -> none  [the longest x1 10.1 us: on_device(): jnp.einsum('hji,hc->jic', o_norm, weight_out, preferred_element_type=jnp....]
    all_to_all x2, waiting for transfers between devices: 20.8 us -> 30.1 us  [exchange(): return lax.all_to_all(tiles, TILE, split_axis=0, concat_axis=0, tiled=True)]
    all_to_all x2, starting transfers between devices: 15 us -> 8.02 us  [exchange(): return lax.all_to_all(tiles, TILE, split_axis=0, concat_axis=0, tiled=True)]
    reduce_sum x4 -> x0, other arithmetic: 6.15 us -> none  [the longest x1 4.57 us: on_device(): back_mean = jnp.mean(back, axis=0)]
    unnamed x31 -> x8, local copies, waits for them, and re-layouts: 7.5 us -> 3.48 us
  transfers between devices with their start and end apart: 4 -> 4, of which waited for: 4 -> 4; matrix products, arithmetic and copies ran while one was open for 13% -> 1% of each run, Pallas kernels for 9% -> 11%
where the time goes in v5:
time: 253 us; the launch traced here: 252 us
  blocking collectives  103 us (41%)
  Pallas kernels  83.6 us (33%)
  waiting for transfers between devices  39 us (15%)
  starting transfers between devices  19.5 us (8%)
  local copies, waits for them, and re-layouts  5.91 us (2%)
    all_to_all x2, blocking collectives, exchange(): return lax.all_to_all(tiles, TILE, split_axis=0, concat_axis=0, tiled=True)  103 us
    all_to_all x2, waiting for transfers between devices, exchange(): return lax.all_to_all(tiles, TILE, split_axis=0, concat_axis=0, tiled=True)  30.1 us
    pallas_call x2, Pallas kernels, side_work(): pl.pallas_call(functools.partial(side_pipeline, odd, specs_in, specs_out,...  17.5 us
    pallas_call x2, Pallas kernels, pair_grad(): pl.pallas_call(pair_grad_kernel, grid=(steps,), in_specs=[pl.BlockSpec((r...  17.1 us
    pallas_call x1, Pallas kernels, block_output(): pl.pallas_call(block_output_kernel, grid=(col_len // block_len,), in_spec...  10.5 us
    pallas_call x1, Pallas kernels, project(): pl.pallas_call(project_kernel, grid=(col_len // block_len,), in_specs=[pl...  10.1 us
    pallas_call x1, Pallas kernels, weight_sums(): pl.pallas_call(weight_sums_kernel, grid=(col_len // block_len,), in_specs...  8.54 us
    all_to_all x2, starting transfers between devices, exchange(): return lax.all_to_all(tiles, TILE, split_axis=0, concat_axis=0, tiled=True)  8.02 us
  transfers between devices with their start and end apart: 4, of which 4 were waited for; matrix products, arithmetic and copies ran while one was open for 1% of the time, Pallas kernels for 11%

profile of v5, /device:TPU:1, one launch (start us, length us, event | category | flops | bytes accessed | tf_op | source)
XLA Modules:
  0.0 252.1 jit_solution(11712570989498544425)
XLA Ops:
  0.6 10.1 %project.1 = (bf16[128,2,64,128]{3,2,1,0:T(8,128)(2,1)}, bf16[64,128,128]{2,1,0:T(8,128)(2,1)}) custom-call(s32[4]{0:T(128)} %lengths_ref.5, bf16[128,64,128]{2,1,0:T(8,128)(2,1)} %bitcast.25, bf16[128,640]{1,0:T(8,128)(2,1)} %w_in_ref.1, f32[1,128]{1,0:T(1,128)} %bitcast.38), custom_call_target="tpu_custom_call" | custom-call | tf_op jit(solution)/shard_map/project/pallas_call | solution.py:153
  10.7 16.5 %side_work.2 = (bf16[64,512,128]{2,1,0:T(8,128)(2,1)}, f32[64,128,128]{2,1,0:T(8,128)}, bf16[64,128,128]{2,1,0:T(8,128)(2,1)}, f32[128,64,128]{2,1,0:T(8,128)}, f32[64,128]{1,0:T(8,128)}) custom-call(s32[4]{0:T(128)} %lengths_ref.5, bf16[128,640]{1,0:T(8,128)(2,1)} %w_in_ref.1, bf16[128,128]{1,0:T(8,128)(2,1)} %w_out_ref.7, f32[1,128]{1,0:T(1,128)} %bitcast.34, ...), custom_call_target="tpu_custom_call" | custom-call | tf_op jit(solution)/shard_map/side_work/pallas_call | solution.py:263
  27.2 47.7 %all_to_all.30 = bf16[128,2,64,128]{3,2,1,0:T(8,128)(2,1)} all-to-all(bf16[128,2,64,128]{3,2,1,0:T(8,128)(2,1)} %get-tuple-element.60), channel_id=1, replica_groups=mesh['grp'=4,'row'=4,'col'=8] {'row','col'}, dimensions={0} | all-to-all | bytes 8388608 | tf_op jit(solution)/shard_map/all_to_all | solution.py:32
  74.9 5.2 %triangle_forward.1 = bf16[32,4,64,128]{3,2,1,0:T(8,128)(2,1)} custom-call(bf16[32,4,2,64,128]{4,3,2,1,0:T(8,128)(2,1)} %bitcast.20), custom_call_target="tpu_custom_call" | custom-call | tf_op jit(solution)/shard_map/triangle_forward/pallas_call | solution.py:76
  80.2 4.0 %all-to-all-start.1 = ((bf16[128,64,128]{2,1,0:T(8,128)(2,1)}), bf16[128,64,128]{2,1,0:T(8,128)(2,1)S(1)}, u32[]{:S(2)}, u32[]{:S(2)}) async-start(bf16[128,64,128]{2,1,0:T(8,128)(2,1)} %bitcast.30), calls=%async_computation.1 | async-start | bytes 4194304 | tf_op jit(solution)/shard_map/all_to_all | solution.py:32
  84.2 1.0 side_work.3
  85.2 18.4 %all-to-all-done.1.outer_ref = bf16[128,64,128]{2,1,0:T(8,128)(2,1)S(1)} async-done(((bf16[128,64,128]{2,1,0:T(8,128)(2,1)}), bf16[128,64,128]{2,1,0:T(8,128)(2,1)S(1)}, u32[]{:S(2)}, u32[]{:S(2)}) %all-to-all-start.1) | async-done | bytes 2097184 | tf_op jit(solution)/shard_map/all_to_all | solution.py:32
  103.6 1.4 copy-done
  104.9 6.0 %outer_grad.1 = bf16[128,64,128]{2,1,0:T(8,128)(2,1)} custom-call(bf16[128,64,128]{2,1,0:T(8,128)(2,1)} %copy-done, f32[128,64,128]{2,1,0:T(8,128)} %get-tuple-element.78.back_ref, f32[64,128]{1,0:T(8,128)} %get-tuple-element.79.mean_ref), custom_call_target="tpu_custom_call" | custom-call | tf_op jit(solution)/shard_map/outer_grad/pallas_call | solution.py:529
  110.9 4.0 %all-to-all-start.2 = ((bf16[128,64,128]{2,1,0:T(8,128)(2,1)}), bf16[128,64,128]{2,1,0:T(8,128)(2,1)S(1)}, u32[]{:S(2)}, u32[]{:S(2)}) async-start(bf16[128,64,128]{2,1,0:T(8,128)(2,1)} %outer_grad.1), calls=%async_computation.2 | async-start | bytes 4194304 | tf_op jit(solution)/shard_map/all_to_all | solution.py:32
  114.9 10.5 %block_output.1 = (bf16[128,64,128]{2,1,0:T(8,128)(2,1)}, bf16[64,128,128]{2,1,0:T(8,128)(2,1)}, f32[128,128]{1,0:T(8,128)}, f32[128,128]{1,0:T(8,128)}) custom-call(bf16[128,64,128]{2,1,0:T(8,128)(2,1)} %copy-done, f32[64,128,128]{2,1,0:T(8,128)} %get-tuple-element.80.gate_ref, bf16[64,128,128]{2,1,0:T(8,128)(2,1)} %get-tuple-element.81.grad_proj_ref, ...), custom_call_target="tpu_custom_call" | custom-call | tf_op jit(solution)/shard_map/block_output/pallas_call | solution.py:349
  125.4 11.7 %all-to-all-done.2 = bf16[128,64,128]{2,1,0:T(8,128)(2,1)S(1)} async-done(((bf16[128,64,128]{2,1,0:T(8,128)(2,1)}), bf16[128,64,128]{2,1,0:T(8,128)(2,1)S(1)}, u32[]{:S(2)}, u32[]{:S(2)}) %all-to-all-start.2) | async-done | bytes 2097184 | tf_op jit(solution)/shard_map/all_to_all | solution.py:32
  137.0 1.3 copy-done.1
  138.4 6.7 %triangle_backward.1 = bf16[32,4,2,64,128]{4,3,2,1,0:T(8,128)(2,1)} custom-call(bf16[32,4,2,64,128]{4,3,2,1,0:T(8,128)(2,1)} %bitcast.21, bf16[32,4,64,128]{3,2,1,0:T(8,128)(2,1)} %bitcast.29), custom_call_target="tpu_custom_call" | custom-call | tf_op jit(solution)/shard_map/triangle_backward/pallas_call | solution.py:90
  145.1 55.5 %all_to_all.31.grad_ref = bf16[128,2,64,128]{3,2,1,0:T(8,128)(2,1)} all-to-all(bf16[128,2,64,128]{3,2,1,0:T(8,128)(2,1)} %bitcast.28), channel_id=1, replica_groups=mesh['grp'=4,'row'=4,'col'=8] {'row','col'}, dimensions={0} | all-to-all | bytes 8388608 | tf_op jit(solution)/shard_map/all_to_all | solution.py:32
  200.6 8.5 %weight_sums.1 = f32[1024,128]{1,0:T(8,128)} custom-call(bf16[128,2,64,128]{3,2,1,0:T(8,128)(2,1)} %all_to_all.31.grad_ref, bf16[64,512,128]{2,1,0:T(8,128)(2,1)} %get-tuple-element.89.factor_ref, bf16[64,128,128]{2,1,0:T(8,128)(2,1)} %get-tuple-element.54.refs_0_.norm_ref, f32[128,128]{1,0:T(8,128)} %get-tuple-element.92.gate_ref, ...), custom_call_target="tpu_custom_call" | custom-call | tf_op jit(solution)/shard_map/weight_sums/pallas_call | solution.py:409
  209.2 5.4 %all-to-all-start.4 = ((f32[128,8,128]{2,1,0:T(8,128)}), f32[128,8,128]{2,1,0:T(8,128)S(1)}, u32[]{:S(2)}, u32[]{:S(2)}) async-start(f32[128,8,128]{2,1,0:T(8,128)} %bitcast.32), calls=%async_computation.4 | async-start | bytes 1048576 | tf_op jit(solution)/shard_map/all_to_all | solution.py:577
  216.2 8.6 %pair_grad.2._ = bf16[128,64,128]{2,1,0:T(8,128)(2,1)} custom-call(bf16[128,64,128]{2,1,0:T(8,128)(2,1)} %bitcast.26, bf16[128,2,64,128]{3,2,1,0:T(8,128)(2,1)} %all_to_all.31.grad_ref, bf16[64,512,128]{2,1,0:T(8,128)(2,1)} %get-tuple-element.89.factor_ref, bf16[64,128,128]{2,1,0:T(8,128)(2,1)} %get-tuple-element.90.gate_ref, ...), custom_call_target="tpu_custom_call", output_to_operand_aliasing={{}: (7, {})} | custom-call | tf_op jit(solution)/shard_map/pair_grad/pallas_call | solution.py:449
  224.7 3.7 %all-to-all-done.4 = f32[128,8,128]{2,1,0:T(8,128)S(1)} async-done(((f32[128,8,128]{2,1,0:T(8,128)}), f32[128,8,128]{2,1,0:T(8,128)S(1)}, u32[]{:S(2)}, u32[]{:S(2)}) %all-to-all-start.4) | async-done | bytes 524320 | tf_op jit(solution)/shard_map/all_to_all | solution.py:577
  228.6 0.9 broadcast_in_dim.28
  229.5 6.1 %all-to-all-start.5 = ((f32[128,8,128]{2,1,0:T(8,128)}), f32[128,8,128]{2,1,0:T(8,128)S(1)}, u32[]{:S(2)}, u32[]{:S(2)}) async-start(f32[128,8,128]{2,1,0:T(8,128)} %broadcast_in_dim.28), calls=%async_computation.5 | async-start | bytes 1048576 | tf_op jit(solution)/shard_map/all_to_all | solution.py:582
  235.5 8.6 %pair_grad.3 = bf16[128,64,128]{2,1,0:T(8,128)(2,1)} custom-call(bf16[128,64,128]{2,1,0:T(8,128)(2,1)} %bitcast.27, bf16[128,2,64,128]{3,2,1,0:T(8,128)(2,1)} %all_to_all.31.grad_ref, bf16[64,512,128]{2,1,0:T(8,128)(2,1)} %get-tuple-element.89.factor_ref, bf16[64,128,128]{2,1,0:T(8,128)(2,1)} %get-tuple-element.90.gate_ref, ...), custom_call_target="tpu_custom_call", output_to_operand_aliasing={{}: (7, {})} | custom-call | tf_op jit(solution)/shard_map/pair_grad/pallas_call | solution.py:449
  244.1 5.3 %all-to-all-done.5 = f32[128,8,128]{2,1,0:T(8,128)S(1)} async-done(((f32[128,8,128]{2,1,0:T(8,128)}), f32[128,8,128]{2,1,0:T(8,128)S(1)}, u32[]{:S(2)}, u32[]{:S(2)}) %all-to-all-start.5) | async-done | bytes 524320 | tf_op jit(solution)/shard_map/all_to_all | solution.py:582
  250.2 1.9 finish.1
  (13 shorter events, 2.5 us)
Async XLA Ops:
  80.2 23.4 %all-to-all-start.1 = ((bf16[128,64,128]{2,1,0:T(8,128)(2,1)}), bf16[128,64,128]{2,1,0:T(8,128)(2,1)S(1)}, u32[]{:S(2)}, u32[]{:S(2)}) async-start(bf16[128,64,128]{2,1,0:T(8,128)(2,1)} %bitcast.30), calls=%async_computation.1 | async-start | bytes 4194304 | tf_op jit(solution)/shard_map/all_to_all | solution.py:32
  103.6 1.4 copy-start
  110.9 26.1 %all-to-all-start.2 = ((bf16[128,64,128]{2,1,0:T(8,128)(2,1)}), bf16[128,64,128]{2,1,0:T(8,128)(2,1)S(1)}, u32[]{:S(2)}, u32[]{:S(2)}) async-start(bf16[128,64,128]{2,1,0:T(8,128)(2,1)} %outer_grad.1), calls=%async_computation.2 | async-start | bytes 4194304 | tf_op jit(solution)/shard_map/all_to_all | solution.py:32
  137.0 1.3 copy-start.1
  200.6 14.0 %copy-start.2 = (bf16[128,640]{1,0:T(8,128)(2,1)S(1)}, bf16[128,640]{1,0:T(8,128)(2,1)}, u32[]{:S(2)}) copy-start(bf16[128,640]{1,0:T(8,128)(2,1)} %w_in_ref.1) | copy-start | bytes 491524
  200.6 14.6 %slice-start = ((bf16[128,640]{1,0:T(8,128)(2,1)}), bf16[128,512]{1,0:T(8,128)(2,1)S(1)}, s32[]{:S(2)}) async-start(bf16[128,640]{1,0:T(8,128)(2,1)} %w_in_ref.1), calls=%async_computation.6 | async-start | bytes 262144 | tf_op jit(solution)/shard_map/slice | solution.py:572
  209.2 19.3 %all-to-all-start.4 = ((f32[128,8,128]{2,1,0:T(8,128)}), f32[128,8,128]{2,1,0:T(8,128)S(1)}, u32[]{:S(2)}, u32[]{:S(2)}) async-start(f32[128,8,128]{2,1,0:T(8,128)} %bitcast.32), calls=%async_computation.4 | async-start | bytes 1048576 | tf_op jit(solution)/shard_map/all_to_all | solution.py:577
  229.5 19.9 %all-to-all-start.5 = ((f32[128,8,128]{2,1,0:T(8,128)}), f32[128,8,128]{2,1,0:T(8,128)S(1)}, u32[]{:S(2)}, u32[]{:S(2)}) async-start(f32[128,8,128]{2,1,0:T(8,128)} %broadcast_in_dim.28), calls=%async_computation.5 | async-start | bytes 1048576 | tf_op jit(solution)/shard_map/all_to_all | solution.py:582
  249.4 0.8 copy-start.3

commit v6 on v5

--- a/solution.py
+++ b/solution.py
@@ -10,7 +10,7 @@
 N = 512
 ALL = ("grp", "row", "col")
 TILE = ("row", "col")
-STAGGER_NS = 2000
+STAGGER_NS = 7000
 
 
 epsilon = 1e-05
@@ -95,8 +95,9 @@
             pl.BlockSpec((devices, 1, col_len, row_len), lambda h: (0, h, 0, 0)),
         ],
         out_specs=pl.BlockSpec((devices, 1, 2, col_len, row_len), lambda h: (0, h, 0, 0, 0)),
-        out_shape=jax.ShapeDtypeStruct(pair_ch.shape, jnp.bfloat16),
+        out_shape=pltpu.HBM(pair_ch.shape, jnp.bfloat16),
         scratch_shapes=[pltpu.VMEM((side, side), jnp.bfloat16)] * 3,
+        compiler_params=pltpu.CompilerParams(vmem_limit_bytes=48 << 20),
         name="triangle_backward",
     )(pair_ch, grad_ch)
 
@@ -361,10 +362,11 @@
         out_specs=[natural, by_pair, square, square],
         out_shape=[
             pltpu.HBM(cotangent.shape, jnp.bfloat16),
-            jax.ShapeDtypeStruct(z_norm.shape, jnp.bfloat16),
-            jax.ShapeDtypeStruct((width, width), jnp.float32),
-            jax.ShapeDtypeStruct((width, width), jnp.float32),
-        ],
+            pltpu.HBM(z_norm.shape, jnp.bfloat16),
+            pltpu.HBM((width, width), jnp.float32),
+            pltpu.HBM((width, width), jnp.float32),
+        ],
+        compiler_params=pltpu.CompilerParams(vmem_limit_bytes=48 << 20),
         name="block_output",
     )(outer_tile, gate, grad_proj, cotangent, z_norm, w_out, gain_out[None])
 
@@ -492,6 +494,7 @@
             row,
             row,
         ],
+        compiler_params=pltpu.CompilerParams(vmem_limit_bytes=16 << 20),
         name="finish",
     )(totals, weight_in, weight_out, gain_in[None], gain_out[None])
     return grads[0], grads[1], grads[2][0], grads[3][0]
@@ -531,7 +534,8 @@
         grid=(col_len // block_len,),
         in_specs=[whole, whole, pl.BlockSpec((block_len, row_len), lambda j: (j, 0))],
         out_specs=whole,
-        out_shape=jax.ShapeDtypeStruct(outer_tile.shape, jnp.bfloat16),
+        out_shape=pltpu.HBM(outer_tile.shape, jnp.bfloat16),
+        compiler_params=pltpu.CompilerParams(vmem_limit_bytes=48 << 20),
         name="outer_grad",
     )(outer_tile, back, back_mean)
 

time: 253 us -> 233 us (0.921)
  blocking collectives: 103 us -> 84.5 us
  waiting for transfers between devices: 39 us -> 34 us
  Pallas kernels: 83.6 us -> 87.4 us
    all_to_all x2, blocking collectives: 103 us -> 84.5 us  [exchange(): return lax.all_to_all(tiles, TILE, split_axis=0, concat_axis=0, tiled=True)]
    pallas_call x2, Pallas kernels: 17.5 us -> 22.5 us  [side_work(): pl.pallas_call(functools.partial(side_pipeline, odd, specs_in, specs_out,...]
    all_to_all x2, waiting for transfers between devices: 30.1 us -> 25.8 us  [exchange(): return lax.all_to_all(tiles, TILE, split_axis=0, concat_axis=0, tiled=True)]
  transfers between devices with their start and end apart: 4 -> 4, of which waited for: 4 -> 4; matrix products, arithmetic and copies ran while one was open for 1% -> 1% of each run, Pallas kernels for 11% -> 12%
where the time goes in v6:
time: 233 us; the launch traced here: 232 us
  Pallas kernels  87.4 us (38%)
  blocking collectives  84.5 us (36%)
  waiting for transfers between devices  34 us (15%)
  starting transfers between devices  20.9 us (9%)
  local copies, waits for them, and re-layouts  4.78 us (2%)
    all_to_all x2, blocking collectives, exchange(): return lax.all_to_all(tiles, TILE, split_axis=0, concat_axis=0, tiled=True)  84.5 us
    all_to_all x2, waiting for transfers between devices, exchange(): return lax.all_to_all(tiles, TILE, split_axis=0, concat_axis=0, tiled=True)  25.8 us
    pallas_call x2, Pallas kernels, side_work(): pl.pallas_call(functools.partial(side_pipeline, odd, specs_in, specs_out,...  22.5 us
    pallas_call x2, Pallas kernels, pair_grad(): pl.pallas_call(pair_grad_kernel, grid=(steps,), in_specs=[pl.BlockSpec((r...  17.9 us
    all_to_all x2, starting transfers between devices, exchange(): return lax.all_to_all(tiles, TILE, split_axis=0, concat_axis=0, tiled=True)  10.1 us
    pallas_call x1, Pallas kernels, project(): pl.pallas_call(project_kernel, grid=(col_len // block_len,), in_specs=[pl...  10.1 us
    pallas_call x1, Pallas kernels, block_output(): pl.pallas_call(block_output_kernel, grid=(col_len // block_len,), in_spec...  9.83 us
    pallas_call x1, Pallas kernels, weight_sums(): pl.pallas_call(weight_sums_kernel, grid=(col_len // block_len,), in_specs...  8.53 us
  transfers between devices with their start and end apart: 4, of which 4 were waited for; matrix products, arithmetic and copies ran while one was open for 1% of the time, Pallas kernels for 12%

profile of v6, /device:TPU:1, one launch (start us, length us, event | category | flops | bytes accessed | tf_op | source)
XLA Modules:
  0.0 232.4 jit_solution(15036211731070371681)
XLA Ops:
  0.6 10.1 %project.1 = (bf16[128,2,64,128]{3,2,1,0:T(8,128)(2,1)}, bf16[64,128,128]{2,1,0:T(8,128)(2,1)}) custom-call(s32[4]{0:T(128)} %lengths_ref.5, bf16[128,64,128]{2,1,0:T(8,128)(2,1)} %bitcast.34, bf16[128,640]{1,0:T(8,128)(2,1)} %w_in_ref.1, f32[1,128]{1,0:T(1,128)} %bitcast.23), custom_call_target="tpu_custom_call" | custom-call | tf_op jit(solution)/shard_map/project/pallas_call | solution.py:154
  10.7 21.5 %side_work.2 = (bf16[64,512,128]{2,1,0:T(8,128)(2,1)}, f32[64,128,128]{2,1,0:T(8,128)}, bf16[64,128,128]{2,1,0:T(8,128)(2,1)}, f32[128,64,128]{2,1,0:T(8,128)}, f32[64,128]{1,0:T(8,128)}) custom-call(s32[4]{0:T(128)} %lengths_ref.5, bf16[128,640]{1,0:T(8,128)(2,1)} %w_in_ref.1, bf16[128,128]{1,0:T(8,128)(2,1)} %w_out_ref.7, f32[1,128]{1,0:T(1,128)} %bitcast.19, ...), custom_call_target="tpu_custom_call" | custom-call | tf_op jit(solution)/shard_map/side_work/pallas_call | solution.py:264
  32.2 44.2 %all_to_all.30 = bf16[128,2,64,128]{3,2,1,0:T(8,128)(2,1)} all-to-all(bf16[128,2,64,128]{3,2,1,0:T(8,128)(2,1)} %get-tuple-element.60), channel_id=1, replica_groups=mesh['grp'=4,'row'=4,'col'=8] {'row','col'}, dimensions={0} | all-to-all | bytes 8388608 | tf_op jit(solution)/shard_map/all_to_all | solution.py:32
  76.4 5.2 %triangle_forward.1 = bf16[32,4,64,128]{3,2,1,0:T(8,128)(2,1)} custom-call(bf16[32,4,2,64,128]{4,3,2,1,0:T(8,128)(2,1)} %bitcast.29), custom_call_target="tpu_custom_call" | custom-call | tf_op jit(solution)/shard_map/triangle_forward/pallas_call | solution.py:76
  81.7 5.2 %all-to-all-start.1 = ((bf16[128,64,128]{2,1,0:T(8,128)(2,1)}), bf16[128,64,128]{2,1,0:T(8,128)(2,1)S(1)}, u32[]{:S(2)}, u32[]{:S(2)}) async-start(bf16[128,64,128]{2,1,0:T(8,128)(2,1)} %bitcast.38), calls=%async_computation.1 | async-start | bytes 4194304 | tf_op jit(solution)/shard_map/all_to_all | solution.py:32
  86.9 1.0 side_work.3
  87.9 18.3 %all-to-all-done.1.outer_ref = bf16[128,64,128]{2,1,0:T(8,128)(2,1)S(1)} async-done(((bf16[128,64,128]{2,1,0:T(8,128)(2,1)}), bf16[128,64,128]{2,1,0:T(8,128)(2,1)S(1)}, u32[]{:S(2)}, u32[]{:S(2)}) %all-to-all-start.1) | async-done | bytes 2097184 | tf_op jit(solution)/shard_map/all_to_all | solution.py:32
  106.9 5.7 %outer_grad.1 = bf16[128,64,128]{2,1,0:T(8,128)(2,1)} custom-call(bf16[128,64,128]{2,1,0:T(8,128)(2,1)S(1)} %all-to-all-done.1.outer_ref, f32[128,64,128]{2,1,0:T(8,128)} %get-tuple-element.78.back_ref, f32[64,128]{1,0:T(8,128)S(1)} %copy-done.3), custom_call_target="tpu_custom_call" | custom-call | tf_op jit(solution)/shard_map/outer_grad/pallas_call | solution.py:532
  112.7 4.9 %all-to-all-start.2 = ((bf16[128,64,128]{2,1,0:T(8,128)(2,1)}), bf16[128,64,128]{2,1,0:T(8,128)(2,1)}, u32[]{:S(2)}, u32[]{:S(2)}) async-start(bf16[128,64,128]{2,1,0:T(8,128)(2,1)} %outer_grad.1), calls=%async_computation.2 | async-start | bytes 4194304 | tf_op jit(solution)/shard_map/all_to_all | solution.py:32
  117.6 1.6 copy-done
  119.2 9.8 %block_output.1 = (bf16[128,64,128]{2,1,0:T(8,128)(2,1)}, bf16[64,128,128]{2,1,0:T(8,128)(2,1)}, f32[128,128]{1,0:T(8,128)}, f32[128,128]{1,0:T(8,128)}) custom-call(bf16[128,64,128]{2,1,0:T(8,128)(2,1)S(1)} %all-to-all-done.1.outer_ref, f32[64,128,128]{2,1,0:T(8,128)} %get-tuple-element.80.gate_ref, bf16[64,128,128]{2,1,0:T(8,128)(2,1)S(1)} %copy-done, ...), custom_call_target="tpu_custom_call" | custom-call | tf_op jit(solution)/shard_map/block_output/pallas_call | solution.py:350
  129.0 7.5 %all-to-all-done.2 = bf16[128,64,128]{2,1,0:T(8,128)(2,1)} async-done(((bf16[128,64,128]{2,1,0:T(8,128)(2,1)}), bf16[128,64,128]{2,1,0:T(8,128)(2,1)}, u32[]{:S(2)}, u32[]{:S(2)}) %all-to-all-start.2) | async-done | bytes 2097184 | tf_op jit(solution)/shard_map/all_to_all | solution.py:32
  136.5 6.7 %triangle_backward.1 = bf16[32,4,2,64,128]{4,3,2,1,0:T(8,128)(2,1)} custom-call(bf16[32,4,2,64,128]{4,3,2,1,0:T(8,128)(2,1)} %bitcast.30, bf16[32,4,64,128]{3,2,1,0:T(8,128)(2,1)} %bitcast.6.grad_ref), custom_call_target="tpu_custom_call" | custom-call | tf_op jit(solution)/shard_map/triangle_backward/pallas_call | solution.py:90
  143.3 40.3 %all_to_all.31.grad_ref = bf16[128,2,64,128]{3,2,1,0:T(8,128)(2,1)} all-to-all(bf16[128,2,64,128]{3,2,1,0:T(8,128)(2,1)} %bitcast.37), channel_id=1, replica_groups=mesh['grp'=4,'row'=4,'col'=8] {'row','col'}, dimensions={0} | all-to-all | bytes 8388608 | tf_op jit(solution)/shard_map/all_to_all | solution.py:32
  183.6 8.5 %weight_sums.1 = f32[1024,128]{1,0:T(8,128)} custom-call(bf16[128,2,64,128]{3,2,1,0:T(8,128)(2,1)} %all_to_all.31.grad_ref, bf16[64,512,128]{2,1,0:T(8,128)(2,1)} %get-tuple-element.89.factor_ref, bf16[64,128,128]{2,1,0:T(8,128)(2,1)} %get-tuple-element.54.refs_0_.norm_ref, f32[128,128]{1,0:T(8,128)} %get-tuple-element.92.gate_ref, ...), custom_call_target="tpu_custom_call" | custom-call | tf_op jit(solution)/shard_map/weight_sums/pallas_call | solution.py:411
  192.1 4.7 %all-to-all-start.4 = ((f32[128,8,128]{2,1,0:T(8,128)}), f32[128,8,128]{2,1,0:T(8,128)S(1)}, u32[]{:S(2)}, u32[]{:S(2)}) async-start(f32[128,8,128]{2,1,0:T(8,128)} %bitcast.39), calls=%async_computation.4 | async-start | bytes 1048576 | tf_op jit(solution)/shard_map/all_to_all | solution.py:581
  197.7 0.8 copy.23.weight_ref
  198.4 8.6 %pair_grad.2._ = bf16[128,64,128]{2,1,0:T(8,128)(2,1)} custom-call(bf16[128,64,128]{2,1,0:T(8,128)(2,1)} %bitcast.35, bf16[128,2,64,128]{3,2,1,0:T(8,128)(2,1)} %all_to_all.31.grad_ref, bf16[64,512,128]{2,1,0:T(8,128)(2,1)} %get-tuple-element.89.factor_ref, bf16[64,128,128]{2,1,0:T(8,128)(2,1)} %get-tuple-element.90.gate_ref, ...), custom_call_target="tpu_custom_call", output_to_operand_aliasing={{}: (7, {})} | custom-call | tf_op jit(solution)/shard_map/pair_grad/pallas_call | solution.py:451
  207.0 3.7 %all-to-all-done.4 = f32[128,8,128]{2,1,0:T(8,128)S(1)} async-done(((f32[128,8,128]{2,1,0:T(8,128)}), f32[128,8,128]{2,1,0:T(8,128)S(1)}, u32[]{:S(2)}, u32[]{:S(2)}) %all-to-all-start.4) | async-done | bytes 524320 | tf_op jit(solution)/shard_map/all_to_all | solution.py:581
  210.8 0.9 broadcast_in_dim.28
  211.7 6.1 %all-to-all-start.5 = ((f32[128,8,128]{2,1,0:T(8,128)}), f32[128,8,128]{2,1,0:T(8,128)S(1)}, u32[]{:S(2)}, u32[]{:S(2)}) async-start(f32[128,8,128]{2,1,0:T(8,128)} %broadcast_in_dim.28), calls=%async_computation.5 | async-start | bytes 1048576 | tf_op jit(solution)/shard_map/all_to_all | solution.py:586
  217.8 9.4 %pair_grad.3 = bf16[128,64,128]{2,1,0:T(8,128)(2,1)} custom-call(bf16[128,64,128]{2,1,0:T(8,128)(2,1)} %bitcast.36, bf16[128,2,64,128]{3,2,1,0:T(8,128)(2,1)} %all_to_all.31.grad_ref, bf16[64,512,128]{2,1,0:T(8,128)(2,1)} %get-tuple-element.89.factor_ref, bf16[64,128,128]{2,1,0:T(8,128)(2,1)} %get-tuple-element.90.gate_ref, ...), custom_call_target="tpu_custom_call", output_to_operand_aliasing={{}: (7, {})} | custom-call | tf_op jit(solution)/shard_map/pair_grad/pallas_call | solution.py:451
  227.2 4.5 %all-to-all-done.5 = f32[128,8,128]{2,1,0:T(8,128)S(1)} async-done(((f32[128,8,128]{2,1,0:T(8,128)}), f32[128,8,128]{2,1,0:T(8,128)S(1)}, u32[]{:S(2)}, u32[]{:S(2)}) %all-to-all-start.5) | async-done | bytes 524320 | tf_op jit(solution)/shard_map/all_to_all | solution.py:586
  231.6 0.8 finish.1
  (17 shorter events, 1.7 us)
Async XLA Ops:
  81.7 24.5 %all-to-all-start.1 = ((bf16[128,64,128]{2,1,0:T(8,128)(2,1)}), bf16[128,64,128]{2,1,0:T(8,128)(2,1)S(1)}, u32[]{:S(2)}, u32[]{:S(2)}) async-start(bf16[128,64,128]{2,1,0:T(8,128)(2,1)} %bitcast.38), calls=%async_computation.1 | async-start | bytes 4194304 | tf_op jit(solution)/shard_map/all_to_all | solution.py:32
  106.2 0.8 copy-start.3
  112.7 4.9 %copy-start.2 = (bf16[128,128]{1,0:T(8,128)(2,1)S(1)}, bf16[128,128]{1,0:T(8,128)(2,1)}, u32[]{:S(2)}) copy-start(bf16[128,128]{1,0:T(8,128)(2,1)} %w_out_ref.7) | copy-start | bytes 98308
  112.7 4.9 %copy-start.4 = (f32[128]{0:T(128)S(1)}, f32[128]{0:T(128)}, u32[]{:S(2)}) copy-start(f32[128]{0:T(128)} %param.13) | copy-start | bytes 1540
  112.7 23.9 %all-to-all-start.2 = ((bf16[128,64,128]{2,1,0:T(8,128)(2,1)}), bf16[128,64,128]{2,1,0:T(8,128)(2,1)}, u32[]{:S(2)}, u32[]{:S(2)}) async-start(bf16[128,64,128]{2,1,0:T(8,128)(2,1)} %outer_grad.1), calls=%async_computation.2 | async-start | bytes 4194304 | tf_op jit(solution)/shard_map/all_to_all | solution.py:32
  117.6 1.6 copy-start
  183.6 13.3 %copy-start.1 = (bf16[128,640]{1,0:T(8,128)(2,1)S(1)}, bf16[128,640]{1,0:T(8,128)(2,1)}, u32[]{:S(2)}) copy-start(bf16[128,640]{1,0:T(8,128)(2,1)} %w_in_ref.1) | copy-start | bytes 491524
  183.6 13.9 %slice-start = ((bf16[128,640]{1,0:T(8,128)(2,1)}), bf16[128,512]{1,0:T(8,128)(2,1)S(1)}, s32[]{:S(2)}) async-start(bf16[128,640]{1,0:T(8,128)(2,1)} %w_in_ref.1), calls=%async_computation.6 | async-start | bytes 262144 | tf_op jit(solution)/shard_map/slice | solution.py:576
  192.1 18.6 %all-to-all-start.4 = ((f32[128,8,128]{2,1,0:T(8,128)}), f32[128,8,128]{2,1,0:T(8,128)S(1)}, u32[]{:S(2)}, u32[]{:S(2)}) async-start(f32[128,8,128]{2,1,0:T(8,128)} %bitcast.39), calls=%async_computation.4 | async-start | bytes 1048576 | tf_op jit(solution)/shard_map/all_to_all | solution.py:581
  211.7 19.9 %all-to-all-start.5 = ((f32[128,8,128]{2,1,0:T(8,128)}), f32[128,8,128]{2,1,0:T(8,128)S(1)}, u32[]{:S(2)}, u32[]{:S(2)}) async-start(f32[128,8,128]{2,1,0:T(8,128)} %broadcast_in_dim.28), calls=%async_computation.5 | async-start | bytes 1048576 | tf_op jit(solution)/shard_map/all_to_all | solution.py:586
  217.8 13.8 %copy-start.5 = (f32[128]{0:T(128)S(1)}, f32[128]{0:T(128)}, u32[]{:S(2)}) copy-start(f32[128]{0:T(128)} %param.12) | copy-start | bytes 1540

commit v7 on v6

--- a/solution.py
+++ b/solution.py
@@ -419,8 +419,9 @@
             square,
         ],
         out_specs=pl.BlockSpec((8 * width, width), lambda j: (0, 0)),
-        out_shape=jax.ShapeDtypeStruct((8 * width, width), jnp.float32),
+        out_shape=pltpu.HBM((8 * width, width), jnp.float32),
         scratch_shapes=[pltpu.VMEM((4 * hidden_width, width), jnp.float32)],
+        compiler_params=pltpu.CompilerParams(vmem_limit_bytes=46 << 20),
         name="weight_sums",
     )(grad_tiles, factors, z_norm, grad_w_gate, grad_w_out)
 

time: 233 us -> 234 us (level)
  no operation moved by 1% of the time
where the time goes in v7:
time: 234 us; the launch traced here: 232 us
  Pallas kernels  88.1 us (38%)
  blocking collectives  83.8 us (36%)
  waiting for transfers between devices  34.1 us (15%)
  starting transfers between devices  20.7 us (9%)
  local copies, waits for them, and re-layouts  4.82 us (2%)
    all_to_all x2, blocking collectives, exchange(): return lax.all_to_all(tiles, TILE, split_axis=0, concat_axis=0, tiled=True)  83.8 us
    all_to_all x2, waiting for transfers between devices, exchange(): return lax.all_to_all(tiles, TILE, split_axis=0, concat_axis=0, tiled=True)  25.9 us
    pallas_call x2, Pallas kernels, side_work(): pl.pallas_call(functools.partial(side_pipeline, odd, specs_in, specs_out,...  22.5 us
    pallas_call x2, Pallas kernels, pair_grad(): pl.pallas_call(pair_grad_kernel, grid=(steps,), in_specs=[pl.BlockSpec((r...  17.9 us
    pallas_call x1, Pallas kernels, project(): pl.pallas_call(project_kernel, grid=(col_len // block_len,), in_specs=[pl...  10.1 us
    all_to_all x2, starting transfers between devices, exchange(): return lax.all_to_all(tiles, TILE, split_axis=0, concat_axis=0, tiled=True)  9.98 us
    pallas_call x1, Pallas kernels, block_output(): pl.pallas_call(block_output_kernel, grid=(col_len // block_len,), in_spec...  9.83 us
    pallas_call x1, Pallas kernels, weight_sums(): pl.pallas_call(weight_sums_kernel, grid=(col_len // block_len,), in_specs...  9.42 us
  transfers between devices with their start and end apart: 4, of which 4 were waited for; matrix products, arithmetic and copies ran while one was open for 1% of the time, Pallas kernels for 12%

profile of v7, /device:TPU:1, one launch (start us, length us, event | category | flops | bytes accessed | tf_op | source)
XLA Modules:
  0.0 232.5 jit_solution(12734636355862609759)
XLA Ops:
  0.6 10.1 %project.1 = (bf16[128,2,64,128]{3,2,1,0:T(8,128)(2,1)}, bf16[64,128,128]{2,1,0:T(8,128)(2,1)}) custom-call(s32[4]{0:T(128)} %lengths_ref.5, bf16[128,64,128]{2,1,0:T(8,128)(2,1)} %bitcast.34, bf16[128,640]{1,0:T(8,128)(2,1)} %w_in_ref.1, f32[1,128]{1,0:T(1,128)} %bitcast.25), custom_call_target="tpu_custom_call" | custom-call | tf_op jit(solution)/shard_map/project/pallas_call | solution.py:154
  10.7 21.5 %side_work.2 = (bf16[64,512,128]{2,1,0:T(8,128)(2,1)}, f32[64,128,128]{2,1,0:T(8,128)}, bf16[64,128,128]{2,1,0:T(8,128)(2,1)}, f32[128,64,128]{2,1,0:T(8,128)}, f32[64,128]{1,0:T(8,128)}) custom-call(s32[4]{0:T(128)} %lengths_ref.5, bf16[128,640]{1,0:T(8,128)(2,1)} %w_in_ref.1, bf16[128,128]{1,0:T(8,128)(2,1)} %w_out_ref.7, f32[1,128]{1,0:T(1,128)} %bitcast.21, ...), custom_call_target="tpu_custom_call" | custom-call | tf_op jit(solution)/shard_map/side_work/pallas_call | solution.py:264
  32.2 44.2 %all_to_all.30 = bf16[128,2,64,128]{3,2,1,0:T(8,128)(2,1)} all-to-all(bf16[128,2,64,128]{3,2,1,0:T(8,128)(2,1)} %get-tuple-element.60), channel_id=1, replica_groups=mesh['grp'=4,'row'=4,'col'=8] {'row','col'}, dimensions={0} | all-to-all | bytes 8388608 | tf_op jit(solution)/shard_map/all_to_all | solution.py:32
  76.5 5.2 %triangle_forward.1 = bf16[32,4,64,128]{3,2,1,0:T(8,128)(2,1)} custom-call(bf16[32,4,2,64,128]{4,3,2,1,0:T(8,128)(2,1)} %bitcast.29), custom_call_target="tpu_custom_call" | custom-call | tf_op jit(solution)/shard_map/triangle_forward/pallas_call | solution.py:76
  81.7 5.1 %all-to-all-start.1 = ((bf16[128,64,128]{2,1,0:T(8,128)(2,1)}), bf16[128,64,128]{2,1,0:T(8,128)(2,1)S(1)}, u32[]{:S(2)}, u32[]{:S(2)}) async-start(bf16[128,64,128]{2,1,0:T(8,128)(2,1)} %bitcast.38), calls=%async_computation.1 | async-start | bytes 4194304 | tf_op jit(solution)/shard_map/all_to_all | solution.py:32
  86.8 1.0 side_work.3
  87.8 18.3 %all-to-all-done.1.outer_ref = bf16[128,64,128]{2,1,0:T(8,128)(2,1)S(1)} async-done(((bf16[128,64,128]{2,1,0:T(8,128)(2,1)}), bf16[128,64,128]{2,1,0:T(8,128)(2,1)S(1)}, u32[]{:S(2)}, u32[]{:S(2)}) %all-to-all-start.1) | async-done | bytes 2097184 | tf_op jit(solution)/shard_map/all_to_all | solution.py:32
  106.8 5.7 %outer_grad.1 = bf16[128,64,128]{2,1,0:T(8,128)(2,1)} custom-call(bf16[128,64,128]{2,1,0:T(8,128)(2,1)S(1)} %all-to-all-done.1.outer_ref, f32[128,64,128]{2,1,0:T(8,128)} %get-tuple-element.78.back_ref, f32[64,128]{1,0:T(8,128)S(1)} %copy-done.5), custom_call_target="tpu_custom_call" | custom-call | tf_op jit(solution)/shard_map/outer_grad/pallas_call | solution.py:533
  112.6 4.9 %all-to-all-start.2 = ((bf16[128,64,128]{2,1,0:T(8,128)(2,1)}), bf16[128,64,128]{2,1,0:T(8,128)(2,1)}, u32[]{:S(2)}, u32[]{:S(2)}) async-start(bf16[128,64,128]{2,1,0:T(8,128)(2,1)} %outer_grad.1), calls=%async_computation.2 | async-start | bytes 4194304 | tf_op jit(solution)/shard_map/all_to_all | solution.py:32
  117.5 1.6 copy-done.2
  119.1 9.8 %block_output.1 = (bf16[128,64,128]{2,1,0:T(8,128)(2,1)}, bf16[64,128,128]{2,1,0:T(8,128)(2,1)}, f32[128,128]{1,0:T(8,128)}, f32[128,128]{1,0:T(8,128)}) custom-call(bf16[128,64,128]{2,1,0:T(8,128)(2,1)S(1)} %all-to-all-done.1.outer_ref, f32[64,128,128]{2,1,0:T(8,128)} %get-tuple-element.80.gate_ref, bf16[64,128,128]{2,1,0:T(8,128)(2,1)S(1)} %copy-done.2, ...), custom_call_target="tpu_custom_call" | custom-call | tf_op jit(solution)/shard_map/block_output/pallas_call | solution.py:350
  129.0 7.6 %all-to-all-done.2 = bf16[128,64,128]{2,1,0:T(8,128)(2,1)} async-done(((bf16[128,64,128]{2,1,0:T(8,128)(2,1)}), bf16[128,64,128]{2,1,0:T(8,128)(2,1)}, u32[]{:S(2)}, u32[]{:S(2)}) %all-to-all-start.2) | async-done | bytes 2097184 | tf_op jit(solution)/shard_map/all_to_all | solution.py:32
  136.5 6.7 %triangle_backward.1 = bf16[32,4,2,64,128]{4,3,2,1,0:T(8,128)(2,1)} custom-call(bf16[32,4,2,64,128]{4,3,2,1,0:T(8,128)(2,1)} %bitcast.30, bf16[32,4,64,128]{3,2,1,0:T(8,128)(2,1)} %bitcast.6.grad_ref), custom_call_target="tpu_custom_call" | custom-call | tf_op jit(solution)/shard_map/triangle_backward/pallas_call | solution.py:90
  143.2 39.5 %all_to_all.31.grad_ref = bf16[128,2,64,128]{3,2,1,0:T(8,128)(2,1)S(1)} all-to-all(bf16[128,2,64,128]{3,2,1,0:T(8,128)(2,1)} %bitcast.37), channel_id=1, replica_groups=mesh['grp'=4,'row'=4,'col'=8] {'row','col'}, dimensions={0} | all-to-all | bytes 8388608 | tf_op jit(solution)/shard_map/all_to_all | solution.py:32
  182.8 9.4 %weight_sums.1 = f32[1024,128]{1,0:T(8,128)} custom-call(bf16[128,2,64,128]{3,2,1,0:T(8,128)(2,1)S(1)} %all_to_all.31.grad_ref, bf16[64,512,128]{2,1,0:T(8,128)(2,1)} %get-tuple-element.89.factor_ref, bf16[64,128,128]{2,1,0:T(8,128)(2,1)S(1)} %copy-done, f32[128,128]{1,0:T(8,128)S(1)} %copy-done.7, f32[128,128]{1,0:T(8,128)S(1)} %copy-done.6), custom_call_target="tpu_custom_call" | custom-call | tf_op jit(solution)/shard_map/weight_sums/pallas_call | solution.py:411
  192.3 4.6 %all-to-all-start.4 = ((f32[128,8,128]{2,1,0:T(8,128)}), f32[128,8,128]{2,1,0:T(8,128)S(1)}, u32[]{:S(2)}, u32[]{:S(2)}) async-start(f32[128,8,128]{2,1,0:T(8,128)} %bitcast.39), calls=%async_computation.4 | async-start | bytes 1048576 | tf_op jit(solution)/shard_map/all_to_all | solution.py:582
  197.7 0.8 copy.23.weight_ref
  198.5 8.6 %pair_grad.2._ = bf16[128,64,128]{2,1,0:T(8,128)(2,1)} custom-call(bf16[128,64,128]{2,1,0:T(8,128)(2,1)} %bitcast.35, bf16[128,2,64,128]{3,2,1,0:T(8,128)(2,1)} %copy-done.1, bf16[64,512,128]{2,1,0:T(8,128)(2,1)} %get-tuple-element.89.factor_ref, bf16[64,128,128]{2,1,0:T(8,128)(2,1)} %get-tuple-element.90.gate_ref, ...), custom_call_target="tpu_custom_call", output_to_operand_aliasing={{}: (7, {})} | custom-call | tf_op jit(solution)/shard_map/pair_grad/pallas_call | solution.py:452
  207.0 3.7 %all-to-all-done.4 = f32[128,8,128]{2,1,0:T(8,128)S(1)} async-done(((f32[128,8,128]{2,1,0:T(8,128)}), f32[128,8,128]{2,1,0:T(8,128)S(1)}, u32[]{:S(2)}, u32[]{:S(2)}) %all-to-all-start.4) | async-done | bytes 524320 | tf_op jit(solution)/shard_map/all_to_all | solution.py:582
  210.9 0.9 broadcast_in_dim.28
  211.8 6.1 %all-to-all-start.5 = ((f32[128,8,128]{2,1,0:T(8,128)}), f32[128,8,128]{2,1,0:T(8,128)S(1)}, u32[]{:S(2)}, u32[]{:S(2)}) async-start(f32[128,8,128]{2,1,0:T(8,128)} %broadcast_in_dim.28), calls=%async_computation.5 | async-start | bytes 1048576 | tf_op jit(solution)/shard_map/all_to_all | solution.py:587
  217.8 9.3 %pair_grad.3 = bf16[128,64,128]{2,1,0:T(8,128)(2,1)} custom-call(bf16[128,64,128]{2,1,0:T(8,128)(2,1)} %bitcast.36, bf16[128,2,64,128]{3,2,1,0:T(8,128)(2,1)} %copy-done.1, bf16[64,512,128]{2,1,0:T(8,128)(2,1)} %get-tuple-element.89.factor_ref, bf16[64,128,128]{2,1,0:T(8,128)(2,1)} %get-tuple-element.90.gate_ref, ...), custom_call_target="tpu_custom_call", output_to_operand_aliasing={{}: (7, {})} | custom-call | tf_op jit(solution)/shard_map/pair_grad/pallas_call | solution.py:452
  227.1 4.5 %all-to-all-done.5 = f32[128,8,128]{2,1,0:T(8,128)S(1)} async-done(((f32[128,8,128]{2,1,0:T(8,128)}), f32[128,8,128]{2,1,0:T(8,128)S(1)}, u32[]{:S(2)}, u32[]{:S(2)}) %all-to-all-start.5) | async-done | bytes 524320 | tf_op jit(solution)/shard_map/all_to_all | solution.py:587
  231.7 0.8 finish.1
  (25 shorter events, 1.7 us)
Async XLA Ops:
  81.7 24.4 %all-to-all-start.1 = ((bf16[128,64,128]{2,1,0:T(8,128)(2,1)}), bf16[128,64,128]{2,1,0:T(8,128)(2,1)S(1)}, u32[]{:S(2)}, u32[]{:S(2)}) async-start(bf16[128,64,128]{2,1,0:T(8,128)(2,1)} %bitcast.38), calls=%async_computation.1 | async-start | bytes 4194304 | tf_op jit(solution)/shard_map/all_to_all | solution.py:32
  106.1 0.8 copy-start.5
  112.6 4.9 %copy-start.4 = (bf16[128,128]{1,0:T(8,128)(2,1)S(1)}, bf16[128,128]{1,0:T(8,128)(2,1)}, u32[]{:S(2)}) copy-start(bf16[128,128]{1,0:T(8,128)(2,1)} %w_out_ref.7) | copy-start | bytes 98308
  112.6 4.9 %copy-start.8 = (f32[128]{0:T(128)S(1)}, f32[128]{0:T(128)}, u32[]{:S(2)}) copy-start(f32[128]{0:T(128)} %param.13) | copy-start | bytes 1540
  112.6 23.9 %all-to-all-start.2 = ((bf16[128,64,128]{2,1,0:T(8,128)(2,1)}), bf16[128,64,128]{2,1,0:T(8,128)(2,1)}, u32[]{:S(2)}, u32[]{:S(2)}) async-start(bf16[128,64,128]{2,1,0:T(8,128)(2,1)} %outer_grad.1), calls=%async_computation.2 | async-start | bytes 4194304 | tf_op jit(solution)/shard_map/all_to_all | solution.py:32
  117.5 1.6 copy-start.2
  143.2 39.6 %copy-start = (bf16[64,128,128]{2,1,0:T(8,128)(2,1)S(1)}, bf16[64,128,128]{2,1,0:T(8,128)(2,1)}, u32[]{:S(2)}) copy-start(bf16[64,128,128]{2,1,0:T(8,128)(2,1)} %get-tuple-element.54.refs_0_.norm_ref) | copy-start | bytes 6291460
  143.2 39.6 %copy-start.6 = (f32[128,128]{1,0:T(8,128)S(1)}, f32[128,128]{1,0:T(8,128)}, u32[]{:S(2)}) copy-start(f32[128,128]{1,0:T(8,128)} %get-tuple-element.93.out_ref) | copy-start | bytes 196612
  143.2 39.6 %copy-start.7 = (f32[128,128]{1,0:T(8,128)S(1)}, f32[128,128]{1,0:T(8,128)}, u32[]{:S(2)}) copy-start(f32[128,128]{1,0:T(8,128)} %get-tuple-element.92.gate_ref) | copy-start | bytes 196612
  182.8 9.5 %copy-start.1 = (bf16[128,2,64,128]{3,2,1,0:T(8,128)(2,1)}, bf16[128,2,64,128]{3,2,1,0:T(8,128)(2,1)S(1)}, u32[]{:S(2)}) copy-start(bf16[128,2,64,128]{3,2,1,0:T(8,128)(2,1)S(1)} %all_to_all.31.grad_ref) | copy-start | bytes 12582916
  182.8 14.1 %copy-start.3 = (bf16[128,640]{1,0:T(8,128)(2,1)S(1)}, bf16[128,640]{1,0:T(8,128)(2,1)}, u32[]{:S(2)}) copy-start(bf16[128,640]{1,0:T(8,128)(2,1)} %w_in_ref.1) | copy-start | bytes 491524
  182.8 14.7 %slice-start = ((bf16[128,640]{1,0:T(8,128)(2,1)}), bf16[128,512]{1,0:T(8,128)(2,1)S(1)}, s32[]{:S(2)}) async-start(bf16[128,640]{1,0:T(8,128)(2,1)} %w_in_ref.1), calls=%async_computation.6 | async-start | bytes 262144 | tf_op jit(solution)/shard_map/slice | solution.py:577
  192.3 18.5 %all-to-all-start.4 = ((f32[128,8,128]{2,1,0:T(8,128)}), f32[128,8,128]{2,1,0:T(8,128)S(1)}, u32[]{:S(2)}, u32[]{:S(2)}) async-start(f32[128,8,128]{2,1,0:T(8,128)} %bitcast.39), calls=%async_computation.4 | async-start | bytes 1048576 | tf_op jit(solution)/shard_map/all_to_all | solution.py:582
  211.8 19.9 %all-to-all-start.5 = ((f32[128,8,128]{2,1,0:T(8,128)}), f32[128,8,128]{2,1,0:T(8,128)S(1)}, u32[]{:S(2)}, u32[]{:S(2)}) async-start(f32[128,8,128]{2,1,0:T(8,128)} %broadcast_in_dim.28), calls=%async_computation.5 | async-start | bytes 1048576 | tf_op jit(solution)/shard_map/all_to_all | solution.py:587
  217.8 13.8 %copy-start.9 = (f32[128]{0:T(128)S(1)}, f32[128]{0:T(128)}, u32[]{:S(2)}) copy-start(f32[128]{0:T(128)} %param.12) | copy-start | bytes 1540
